TPU v7x, 512 devices: a whole 4x4x16 slice. The times are simulated.
512 devices in a mesh: dp: 32 (over x, z_hi, core), tensor: 16 (over z_lo, y).
Axes of the slice: x: 4, y: 4, z: 16 (z_hi: 4, z_lo: 4; z = z_hi * 4 + z_lo), core: 2. Of those that a mesh axis runs over, the one named last changes fastest.
Arguments:
- activations: bfloat16 [640, 26624], P('dp', 'tensor'), may hold values from -6 to 6
- weight_codes: int32 [26624, 8192], P(('tensor', 'dp')), may hold values from 0 to 15
- scale_index: int32 [26624, 64], P(('tensor', 'dp')), may hold values from 0 to 15, as said below
- scale_table: float32 [16], replicated
- bit_widths: int32 [1, 26624, 64], P(None, ('tensor', 'dp')), may hold values from 2 to 4
Outputs:
- base_output: bfloat16 [640, 8192], P('tensor', 'dp')
- scores: float32 [1, 640], P(None, 'tensor')
Inputs may be any that keep to these rules, and one draw needn't show every extreme that they name: `scale_index`: an entry of scale_table for each row and each group of 128 columns.
All inputs are finite; a program needn't handle non-finite values.
Results may differ from a plain program's by a relative error of at most 0.0058.
Values may be sent and summed in bfloat16 or wider, within the bound.
No kernel may reach another device: no remote copies, remote signals or barrier semaphores. Data moves between devices by JAX's collectives and lax.ppermute only.
A program may use at most 64 MiB of HBM per device.

v0:
```python
import math

import jax
import jax.numpy as jnp
from jax import lax
from jax.sharding import PartitionSpec as P

HB = 128
NCAND = 1


score_divisor = 512.0


def side_by_side(arrays, axis, split_dim, concat_dim, along):
    columns = [a.reshape(*a.shape[:along], -1) for a in arrays]
    both = jnp.concatenate(columns, axis=along)
    whole, at, done = (
        lax.all_to_all(both, axis, split_axis=split_dim, concat_axis=concat_dim, tiled=True),
        0,
        [],
    )
    for a, column in zip(arrays, columns):
        piece = whole[..., at : at + column.shape[along]]
        done.append(piece.reshape(*piece.shape[:along], *a.shape[along:]))
        at += column.shape[along]
    return tuple(done)


def split_up(value, dim, size):
    before, after = (value.shape[:dim], value.shape[dim + 1 :])
    return jnp.moveaxis(value.reshape(*before, size, -1, *after), dim, 0)


def sum_at_owner(value, axis, dim):
    size = lax.axis_size(axis)
    tiles = lax.all_to_all(split_up(value, dim, size), axis, 0, 0, tiled=True)
    return jnp.sum(tiles, axis=0)


def from_everyone(value, axis):
    size = lax.axis_size(axis)
    return lax.all_to_all(
        jnp.broadcast_to(value[None], (size, *value.shape)), axis, 0, 0, tiled=True
    )


def over_copies(value, axis):
    return from_everyone(value, axis).sum(axis=0)


def sylvester(order_size):
    positions = jnp.arange(order_size, dtype=jnp.int32)
    intersection = positions[:, None] & positions[None, :]
    parity = jnp.zeros((order_size, order_size), jnp.int32)
    for shift_bit in range(max(order_size.bit_length() - 1, 0)):
        parity = parity + (intersection >> shift_bit & 1)
    parity = parity % 2
    return (1 - 2 * parity).astype(jnp.float32)


def dequantize(grouped, index_rows, scale_table, bits_rows):
    one_hot = (index_rows[..., None] == jnp.arange(scale_table.shape[0], dtype=jnp.int32)).astype(
        jnp.float32
    )
    scales = jnp.sum(one_hot * scale_table, axis=-1)
    base_w = ((grouped - 8).astype(jnp.float32) * scales[..., None]).astype(jnp.bfloat16)
    step_size = jnp.where(bits_rows == 2, 4, jnp.where(bits_rows == 3, 2, 1)).astype(jnp.int32)[
        ..., None
    ]
    cand_codes = grouped[None] // step_size * step_size + step_size // 2
    cand_w = ((cand_codes - 8).astype(jnp.float32) * scales[None, :, :, None]).astype(jnp.bfloat16)
    row_count = grouped.shape[0]
    col_count = grouped.shape[1] * grouped.shape[2]
    return jnp.concatenate([base_w[None], cand_w], axis=0).reshape(NCAND + 1, row_count, col_count)


def local(activations, weight_codes, scale_index, scale_table, bit_widths):
    tensor_size = lax.axis_size("tensor")
    tok_rows, feat_width = activations.shape
    block_signs = sylvester(HB).astype(jnp.bfloat16)
    blocked = jnp.einsum(
        "rnb,bc->rnc",
        activations.reshape(tok_rows, feat_width // HB, HB),
        block_signs,
        preferred_element_type=jnp.float32,
    ).reshape(tok_rows, feat_width)
    sign_matrix = sylvester(tensor_size)
    shaped = blocked.reshape(tok_rows, tensor_size, feat_width // tensor_size)
    spread = jnp.einsum(
        "js,rsc->rjc",
        sign_matrix,
        lax.all_to_all(shaped, "tensor", split_axis=1, concat_axis=1, tiled=True),
        precision=lax.Precision.HIGHEST,
    )
    mixed_rows = lax.all_to_all(spread, "tensor", split_axis=1, concat_axis=1, tiled=True).reshape(
        tok_rows, feat_width
    )
    rotated = (mixed_rows * (1.0 / math.sqrt(HB * tensor_size))).astype(jnp.bfloat16)
    all_tokens = lax.all_gather(rotated, "dp", axis=0, tiled=True)
    store_rows, model_width = weight_codes.shape
    group_count = scale_index.shape[1]
    group_width = model_width // group_count
    code_wire = weight_codes.reshape(store_rows, group_count, group_width).astype(jnp.bfloat16)
    index_wire = scale_index.astype(jnp.bfloat16)
    bits_wire = jnp.transpose(bit_widths, (1, 2, 0)).astype(jnp.bfloat16)
    code_home, index_home, bits_home = side_by_side(
        (code_wire, index_wire, bits_wire), "dp", 1, 0, 2
    )
    local_grouped = code_home.astype(jnp.int32)
    local_index = index_home.astype(jnp.int32)
    local_bits = jnp.transpose(bits_home.astype(jnp.int32), (2, 0, 1))
    local_weights = dequantize(local_grouped, local_index, scale_table, local_bits)
    token_sums = sum_at_owner(
        jnp.einsum("tf,kfd->tkd", all_tokens, local_weights, preferred_element_type=jnp.float32),
        "tensor",
        0,
    )
    token_sums = jnp.transpose(token_sums, (1, 0, 2))
    base_rows = token_sums[0]
    cand_diffs = token_sums[1:] - base_rows[None]
    block_scores = jnp.sum(cand_diffs * cand_diffs, axis=2) / score_divisor
    scores = over_copies(block_scores, "dp")
    return (base_rows.astype(jnp.bfloat16), scores)


def solution(mesh):
    in_specs = (
        P("dp", "tensor"),
        P(("tensor", "dp"), None),
        P(("tensor", "dp"), None),
        P(),
        P(None, ("tensor", "dp"), None),
    )
    out_specs = (P("tensor", "dp"), P(None, "tensor"))
    return jax.shard_map(local, mesh=mesh, in_specs=in_specs, out_specs=out_specs, check_vma=False)
```

profile of v0, /device:TPU:1, one launch (start us, length us, event | category | flops | bytes accessed | tf_op | source)
XLA Modules:
  0.0 236.9 jit_solution(8731852525822146054)
XLA Ops:
  7.2 1.0 reshape.173
  8.7 17.6 %all_to_all.38 = f32[20,16,104]{2,0,1:T(8,128)S(1)} all-to-all(f32[20,16,104]{2,0,1:T(8,128)S(1)} %copy.92), channel_id=1, replica_groups=mesh['dp'=32,'tensor'=16] {'tensor'}, dimensions={1} | all-to-all | bytes 266240 | tf_op jit(solution)/shard_map/all_to_all | solution.py:93
  26.6 0.7 copy.94
  27.3 4.4 %all-to-all-start.1 = ((f32[20,16,104]{2,0,1:T(8,128)}), f32[20,16,104]{2,0,1:T(8,128)}, u32[]{:S(2)}, u32[]{:S(2)}) async-start(f32[20,16,104]{2,0,1:T(8,128)} %copy.94), calls=%async_computation.1 | async-start | bytes 393216 | tf_op jit(solution)/shard_map/all_to_all | solution.py:96
  33.8 1.0 copy.133
  34.8 3.5 %reshape.185 = bf16[32,2,6760]{2,1,0:T(2,128)(2,1)} reshape(bf16[64,52,130]{2,1,0:T(8,128)(2,1)S(1)} %bitcast.52) | data formatting | bytes 1730560
  38.3 1.8 all-to-all-done.1
  40.1 18.0 %all-to-all-start.2 = ((bf16[32,2,6760]{2,1,0:T(2,128)(2,1)}), bf16[32,2,6760]{2,1,0:T(2,128)(2,1)S(1)}, u32[]{:S(2)}, u32[]{:S(2)}) async-start(bf16[32,2,6760]{2,1,0:T(2,128)(2,1)} %reshape.185), calls=%async_computation.2 | async-start | bytes 1736704 | tf_op jit(solution)/shard_map/all_to_all | solution.py:19
  58.2 1.0 fusion.16
  59.1 0.8 reshape.176
  59.9 44.8 %all-to-all-done.2 = bf16[32,2,6760]{2,1,0:T(2,128)(2,1)S(1)} async-done(((bf16[32,2,6760]{2,1,0:T(2,128)(2,1)}), bf16[32,2,6760]{2,1,0:T(2,128)(2,1)S(1)}, u32[]{:S(2)}, u32[]{:S(2)}) %all-to-all-start.2) | async-done | bytes 865312 | tf_op jit(solution)/shard_map/all_to_all | solution.py:19
  104.8 3.2 %reshape.186 = bf16[64,52,130]{2,1,0:T(8,128)(2,1)S(1)} reshape(bf16[32,2,6760]{2,1,0:T(2,128)(2,1)S(1)} %all-to-all-done.2) | data formatting | bytes 1730560
  108.0 3.1 %copy.130 = bf16[52,32,2,130]{3,2,1,0:T(2,128)(2,1)} copy(bf16[52,32,2,130]{3,0,2,1:T(8,128)(2,1)S(1)} %bitcast.53) | data formatting | bytes 1730560 | tf_op jit(solution)/shard_map/all_to_all | solution.py:19
  111.1 6.1 %copy.101 = bf16[32,52,2,130]{1,0,3,2:T(8,128)(2,1)S(1)} copy(bf16[32,52,2,130]{3,2,0,1:T(2,128)(2,1)} %bitcast.54) | data formatting | bytes 1730560 | tf_op jit(solution)/shard_map/all_to_all | solution.py:19
  117.2 4.2 %all_to_all.30 = bf16[1664,2,130]{0,2,1:T(8,128)(2,1)S(1)} reshape(bf16[32,52,2,130]{1,0,3,2:T(8,128)(2,1)S(1)} %copy.101) | data formatting | bytes 1730560 | tf_op jit(solution)/shard_map/all_to_all | solution.py:19
  121.6 17.6 %fusion.10 = (bf16[1664,2,128]{0,2,1:T(8,128)(2,1)S(1)}, bf16[1664,2,128]{0,2,1:T(8,128)(2,1)S(1)}) fusion(f32[1664,2]{0,1:T(2,128)S(1)} %select_reduce_fusion, bf16[1664,2,130]{0,2,1:T(8,128)(2,1)S(1)} %all_to_all.30, s32[1664,2]{0,1:T(2,128)S(1)} %get-tuple-element.5, s32[1664,2]{0,1:T(2,128)S(1)} %bitcast.62, s32[1664,2]{0,1:T(2,128)S(1)} %get-tuple-element.4), kind=kLoop, calls=%fused_computation.15 | loop fusion | flops 8093696 | bytes 2609152 | tf_op jit(solution)/shard_map/convert_element_type | solution.py:67
  139.8 1.3 copy.108
  141.1 20.7 %all-gather.3.cloned.1.call-done = bf16[32,20,1664]{2,1,0:T(8,128)(2,1)} async-done(((bf16[1,20,1664]{2,1,0:T(8,128)(2,1)}), bf16[32,20,1664]{2,1,0:T(8,128)(2,1)}) %all-gather.3.cloned.1.call-update) | async-done | bytes 2129936 | tf_op jit(solution)/shard_map/all_gather | solution.py:100
  161.8 2.6 %reshape.182 = bf16[16,40,1664,1]{2,1,0,3:T(8,128)(2,1)S(1)} reshape(bf16[32,20,1664]{2,1,0:T(8,128)(2,1)} %all-gather.3.cloned.1.call-done) | data formatting | bytes 4259840 | tf_op jit(solution)/shard_map/tf,kfd->tkd/dot_general | solution.py:115
  164.4 2.5 %fusion = f32[16,40,2,256]{3,1,2,0:T(8,128)S(1)} fusion(bf16[16,40,1664,1]{2,1,0,3:T(8,128)(2,1)S(1)} %reshape.182, bf16[1,1664,256]{2,1,0:T(8,128)(2,1)} %copy.108, bf16[1,1664,256]{2,1,0:T(8,128)(2,1)S(1)} %copy.107), kind=kOutput, calls=%fused_computation.5 | convolution fusion | flops 1093926912 | bytes 5144576 | tf_op jit(solution)/shard_map/tf,kfd->tkd/dot_general | solution.py:115
  167.0 36.0 %all_to_all.39 = f32[16,40,2,256]{3,1,2,0:T(8,128)S(1)} all-to-all(f32[16,40,2,256]{3,1,2,0:T(8,128)S(1)} %fusion), channel_id=1, replica_groups=mesh['dp'=32,'tensor'=16] {'tensor'}, dimensions={0} | all-to-all | bytes 2621440 | tf_op jit(solution)/shard_map/all_to_all | solution.py:37
  203.2 0.6 broadcast_in_dim.17
  203.8 11.5 %all-to-all-start.4 = ((f32[32,1,40]{2,1,0:T(1,128)}), f32[32,1,40]{2,1,0:T(1,128)S(1)}, u32[]{:S(2)}, u32[]{:S(2)}) async-start(f32[32,1,40]{2,1,0:T(1,128)} %broadcast_in_dim.17), calls=%async_computation.4 | async-start | bytes 32768 | tf_op jit(solution)/shard_map/all_to_all | solution.py:43
  216.0 13.6 %all-to-all-done.4 = f32[32,1,40]{2,1,0:T(1,128)S(1)} async-done(((f32[32,1,40]{2,1,0:T(1,128)}), f32[32,1,40]{2,1,0:T(1,128)S(1)}, u32[]{:S(2)}, u32[]{:S(2)}) %all-to-all-start.4) | async-done | bytes 5152 | tf_op jit(solution)/shard_map/all_to_all | solution.py:43
  (35 shorter events, 5.0 us)
Async XLA Ops:
  7.2 24.6 %copy-start.2 = (s32[1,52,64]{2,0,1:T(1,128)S(1)}, s32[1,52,64]{2,0,1:T(1,128)}, u32[]{:S(2)}) copy-start(s32[1,52,64]{2,0,1:T(1,128)} %param.9) | copy-start | bytes 39940
  8.4 23.9 %copy-start.1 = (s32[52,64]{1,0:T(8,128)S(1)}, s32[52,64]{1,0:T(8,128)}, u32[]{:S(2)}) copy-start(s32[52,64]{1,0:T(8,128)} %param.7) | copy-start | bytes 39940
  8.7 24.1 %copy-start = (s32[52,8192]{1,0:T(8,128)S(1)}, s32[52,8192]{1,0:T(8,128)}, u32[]{:S(2)}) copy-start(s32[52,8192]{1,0:T(8,128)} %param.6) | copy-start | bytes 5111812
  27.3 12.8 %all-to-all-start.1 = ((f32[20,16,104]{2,0,1:T(8,128)}), f32[20,16,104]{2,0,1:T(8,128)}, u32[]{:S(2)}, u32[]{:S(2)}) async-start(f32[20,16,104]{2,0,1:T(8,128)} %copy.94), calls=%async_computation.1 | async-start | bytes 393216 | tf_op jit(solution)/shard_map/all_to_all | solution.py:96
  40.1 64.7 %all-to-all-start.2 = ((bf16[32,2,6760]{2,1,0:T(2,128)(2,1)}), bf16[32,2,6760]{2,1,0:T(2,128)(2,1)S(1)}, u32[]{:S(2)}, u32[]{:S(2)}) async-start(bf16[32,2,6760]{2,1,0:T(2,128)(2,1)} %reshape.185), calls=%async_computation.2 | async-start | bytes 1736704 | tf_op jit(solution)/shard_map/all_to_all | solution.py:19
  58.1 103.7 %all-gather.3.cloned.1.call-start = ((), (), s32[]{:S(2)}) async-start(), calls=%async_computation.5 | async-start | bytes 2635776 | tf_op jit(solution)/shard_map/all_gather | solution.py:100
  117.2 4.3 %copy-start.3 = (f32[16]{0:T(128)S(1)}, f32[16]{0:T(128)}, u32[]{:S(2)}) copy-start(f32[16]{0:T(128)} %param.8) | copy-start | bytes 196
  203.8 25.7 %all-to-all-start.4 = ((f32[32,1,40]{2,1,0:T(1,128)}), f32[32,1,40]{2,1,0:T(1,128)S(1)}, u32[]{:S(2)}, u32[]{:S(2)}) async-start(f32[32,1,40]{2,1,0:T(1,128)} %broadcast_in_dim.17), calls=%async_computation.4 | async-start | bytes 32768 | tf_op jit(solution)/shard_map/all_to_all | solution.py:43
Sparse Core Ops, SparseCore 0:
  62.0 99.7 all-gather.2
where the time goes:
time: 238 us; the launch traced here: 237 us
  waiting for transfers between devices  81 us (34%)
  blocking collectives  53.6 us (23%)
  starting transfers between devices  33.9 us (14%)
  local copies, waits for them, and re-layouts  30.9 us (13%)
  other arithmetic  20.1 us (8%)
  between operations  14.3 us (6%)
  matrix products  3.08 us (1%)
    all_to_all x1, waiting for transfers between devices, side_by_side(): lax.all_to_all(both, axis, split_axis=split_dim, concat_axis=concat_dim,...  44.8 us
    all_to_all x1, blocking collectives, sum_at_owner(): tiles = lax.all_to_all(split_up(value, dim, size), axis, 0, 0, tiled=True)  36 us
    all_gather x1, waiting for transfers between devices, local(): all_tokens = lax.all_gather(rotated, 'dp', axis=0, tiled=True)  20.7 us
    all_to_all x1, starting transfers between devices, side_by_side(): lax.all_to_all(both, axis, split_axis=split_dim, concat_axis=concat_dim,...  18 us
    all_to_all x1, blocking collectives, local(): lax.all_to_all(shaped, 'tensor', split_axis=1, concat_axis=1, tiled=True)  17.6 us
    convert_element_type x1, other arithmetic, dequantize(): ((grouped - 8).astype(jnp.float32) * scales[..., None]).astype(jnp.bfloat16)  17.6 us
    all_to_all x1, waiting for transfers between devices, from_everyone(): lax.all_to_all(jnp.broadcast_to(value[None], (size, *value.shape)), axis,...  13.6 us
    all_to_all x3, local copies, waits for them, and re-layouts, side_by_side(): lax.all_to_all(both, axis, split_axis=split_dim, concat_axis=concat_dim,...  13.3 us
  transfers between devices with their start and end apart: 4, of which 4 were waited for; matrix products, arithmetic and copies ran while one was open for 17% of the time, Pallas kernels for 0%

commit v1 on v0

v1 whole, which is shorter than its diff:
```python
import math

import jax
import jax.numpy as jnp
from jax import lax
from jax.experimental import pallas as pl
from jax.experimental.pallas import tpu as pltpu
from jax.sharding import Mesh, PartitionSpec as P


HB = 128
GROUP = 128
AXES = ("x", "zh", "c", "zl", "y")
SIZES = (4, 4, 2, 4, 4)
SCORE_DIVISOR = 512.0
F32 = jnp.float32
BF16 = jnp.bfloat16
VMEM = pl.BlockSpec(memory_space=pltpu.VMEM)
SMEM = pl.BlockSpec(memory_space=pltpu.SMEM)


def sylvester(order):
    at = jnp.arange(order, dtype=jnp.int32)
    both = at[:, None] & at[None, :]
    parity = jnp.zeros((order, order), jnp.int32)
    for bit in range(order.bit_length() - 1):
        parity = parity + (both >> bit & 1)
    return (1 - 2 * (parity % 2)).astype(F32)


def call(kernel, out_shape, in_specs, scratch=(), flops=0, moved=0):
    multi = isinstance(out_shape, (list, tuple))
    return pl.pallas_call(
        kernel,
        out_shape=out_shape,
        in_specs=in_specs,
        out_specs=[VMEM] * len(out_shape) if multi else VMEM,
        scratch_shapes=list(scratch),
        cost_estimate=pl.CostEstimate(flops=flops, bytes_accessed=moved, transcendentals=0),
    )


def block_kernel(act, signs, out):
    for n in range(act.shape[1] // HB):
        cols = slice(n * HB, (n + 1) * HB)
        out[:, cols] = jnp.dot(act[:, cols], signs[...], preferred_element_type=F32)


def pack_kernel(codes, index, bits, out, meta, turned, block):
    rows = codes.shape[0]
    parts, _, width = out.shape
    groups = index.shape[1]
    per = groups // parts
    meta[...] = jnp.zeros_like(meta)
    meta[0:rows, 0:groups] = index[...].astype(F32)
    meta[0:rows, groups : 2 * groups] = bits[...].astype(F32)
    turned[...] = meta[...].T
    block[...] = jnp.zeros_like(block)
    for p in range(parts):
        block[0:rows, :] = codes[:, p * width : (p + 1) * width].astype(F32)
        block[rows : rows + per, 0:GROUP] = turned[p * per : (p + 1) * per, :]
        block[rows : rows + per, GROUP : 2 * GROUP] = turned[groups + p * per : groups + (p + 1) * per, :]
        out[p] = block[...].astype(BF16)


def weight_kernel(rows, own, other, table, place, base, diff, meta, base_acc, diff_acc):
    parts, padded, width = own.shape
    per = width // GROUP
    groups = parts * per
    first = place[2] == 0
    turned = []
    for core in range(2):
        mine, theirs = (own, other) if core == 0 else (other, own)
        for p in range(parts):
            tail = jnp.where(first, mine[p, padded - 8 : padded, :].astype(F32), theirs[p, padded - 8 : padded, :].astype(F32))
            meta[p * per : (p + 1) * per, :] = tail[8 - per :, 0:GROUP]
            meta[groups + p * per : groups + (p + 1) * per, :] = tail[8 - per :, GROUP : 2 * GROUP]
        index = meta[0:groups, :]
        scale = jnp.zeros_like(index)
        for entry in range(table.shape[0]):
            scale = jnp.where(index == float(entry), table[entry], scale)
        meta[0:groups, :] = scale
        turned.append(meta[...].T)
    for p in range(parts):
        for core in range(2):
            mine, theirs = (own, other) if core == 0 else (other, own)
            start = (2 * p + core) * rows
            for k in range(per):
                cols = slice(k * GROUP, (k + 1) * GROUP)
                code = jnp.where(first, mine[p, :, cols], theirs[p, :, cols]).astype(F32)
                at = p * per + k
                scale = turned[core][0:padded, at : at + 1]
                width_bits = turned[core][0:padded, groups + at : groups + at + 1]
                two = jnp.floor(code * 0.25) * 4.0 + 2.0
                three = jnp.floor(code * 0.5) * 2.0 + 1.0
                cand = jnp.where(width_bits == 2.0, two, jnp.where(width_bits == 3.0, three, code))
                base_w = ((code - 8.0) * scale).astype(BF16).astype(F32)
                cand_w = ((cand - 8.0) * scale).astype(BF16).astype(F32)
                base_acc[start : start + padded, cols] = base_w
                diff_acc[start : start + padded, cols] = cand_w - base_w
    total = base.shape[0]
    base[...] = base_acc[0:total, :].astype(BF16)
    diff[...] = diff_acc[0:total, :].astype(BF16)


def matmul_kernel(t0, t1, t2, t3, base_w, diff_w, place, out, left, base_acc, diff_acc, both):
    rows = t0.shape[0]
    for k, piece in enumerate((t0, t1, t2, t3)):
        left[k * rows : (k + 1) * rows, :] = piece[...]
    base_acc[...] = jnp.dot(left[...], base_w[...], preferred_element_type=F32)
    diff_acc[...] = jnp.dot(left[...], diff_w[...], preferred_element_type=F32)
    toks = rows // 4
    for kx in range(4):
        for kz in range(4):
            start = kx * rows + kz * toks
            both[0:toks, :] = base_acc[start : start + toks, :]
            both[toks : 2 * toks, :] = diff_acc[start : start + toks, :]
            owner = lax.rem(place[0] - kx + 4, 4) * 4 + lax.rem(place[1] - kz + 4, 4)
            out[owner] = both[...].astype(BF16)


def sum_kernel(parts, base, score, total):
    acc = parts[0].astype(F32)
    for k in range(1, parts.shape[0]):
        acc = acc + parts[k].astype(F32)
    total[...] = acc
    toks = acc.shape[0] // 2
    half = acc.shape[1] // 2
    base[0] = total[0:toks, 0:half].astype(BF16)
    base[1] = total[0:toks, half:].astype(BF16)
    gap = total[toks : 2 * toks, :]
    score[...] = jnp.broadcast_to(jnp.sum(gap * gap, axis=1, keepdims=True), score.shape)


def shift(value, axis, by, size=4):
    return lax.ppermute(value, axis, [(i, (i + by) % size) for i in range(size)])


def trade(value, axis, bit, size=4):
    return lax.ppermute(value, axis, [(i, i ^ bit) for i in range(size)])


def local(activations, weight_codes, scale_index, scale_table, bit_widths):
  place = jnp.stack([lax.axis_index(a) for a in ("x", "zh", "c")]).astype(jnp.int32)
  toks, feat = activations.shape
  store, width = weight_codes.shape
  part = width // 16
  padded = store + 4
  wire = call(
      pack_kernel, jax.ShapeDtypeStruct((16, padded, part), BF16), [VMEM] * 3,
      [pltpu.VMEM((128, 128), F32), pltpu.VMEM((128, 128), F32), pltpu.VMEM((padded, part), F32)],
      0, store * width * 6,
  )(weight_codes, scale_index, bit_widths.reshape(store, -1))
  home = lax.all_to_all(wire, ("x", "zh"), 0, 0, tiled=True)
  other = trade(home, "c", 1, 2)

  value = call(
      block_kernel, jax.ShapeDtypeStruct((toks, feat), F32), [VMEM] * 2,
      (), 2 * toks * feat * HB, toks * feat * 6,
  )(activations, sylvester(HB).astype(BF16))
  for axis, bit in (("y", 1), ("y", 2), ("zl", 1), ("zl", 2)):
      sign = jnp.where(lax.axis_index(axis) & bit, -1.0, 1.0).astype(F32)
      value = trade(value, axis, bit) + sign * value
  rotated = (value * (1.0 / math.sqrt(HB * 16))).astype(BF16)
  near = [rotated] + [shift(rotated, "zh", k) for k in (1, 2, 3)]
  mid = jnp.concatenate(near, axis=0)
  far = [mid] + [shift(mid, "x", k) for k in (1, 2, 3)]

  rows = store
  base_w, diff_w = call(
      lambda *refs: weight_kernel(rows, *refs),
      [jax.ShapeDtypeStruct((feat, part), BF16)] * 2, [VMEM, VMEM, SMEM, SMEM],
      [pltpu.VMEM((128, 128), F32)] + [pltpu.VMEM((feat + 8, part), F32)] * 2,
      feat * part * 20, feat * part * 6,
  )(home, other, scale_table, place)
  sums = call(
      matmul_kernel, jax.ShapeDtypeStruct((16, 2 * toks, part), BF16),
      [VMEM] * 6 + [SMEM],
      [pltpu.VMEM((16 * toks, feat), BF16)] + [pltpu.VMEM((16 * toks, part), F32)] * 2
      + [pltpu.VMEM((2 * toks, part), F32)],
      4 * 16 * toks * feat * part, feat * part * 4 + 16 * toks * feat * 2,
  )(*far, base_w, diff_w, place)
  gathered = lax.all_to_all(sums, ("zl", "y"), 0, 0, tiled=True)
  halves, score = call(
      sum_kernel,
      [jax.ShapeDtypeStruct((2, toks, part // 2), BF16), jax.ShapeDtypeStruct((toks, 128), F32)],
      [VMEM], [pltpu.VMEM((2 * toks, part), F32)], 16 * 40 * part, 16 * 80 * part,
  )(gathered)
  spread = jnp.broadcast_to(score[:, 0][None, None, :], (32, 1, toks))
  everyone = lax.all_to_all(spread, ("x", "zh", "c"), 0, 0, tiled=True)
  scores = jnp.sum(everyone.reshape(16, 2 * toks), axis=0)[None] / SCORE_DIVISOR
  core = lax.axis_index("c")
  keep = lax.dynamic_index_in_dim(halves, core, 0, False)
  send = lax.dynamic_index_in_dim(halves, 1 - core, 0, False)
  got = trade(send, "c", 1, 2)
  base = jnp.where(core == 0, jnp.concatenate([keep, got], 0), jnp.concatenate([got, keep], 0))
  return base, scores


def solution(mesh):
    fine = Mesh(mesh.devices.reshape(SIZES), AXES)
    dp, tensor = ("x", "zh", "c"), ("zl", "y")
    return jax.shard_map(
        local, mesh=fine,
        in_specs=(P(dp, tensor), P(tensor + dp, None), P(tensor + dp, None), P(), P(None, tensor + dp, None)),
        out_specs=(P(tensor, dp), P(None, tensor)),
        check_vma=False,
    )
```

time: 238 us -> 190 us (0.80)
  starting transfers between devices: 33.9 us -> 97.8 us
  blocking collectives: 53.6 us -> 0 us
  local copies, waits for them, and re-layouts: 30.9 us -> 6.74 us
  waiting for transfers between devices: 81 us -> 62 us
  Pallas kernels: 0 us -> 17.7 us
  other arithmetic: 20.1 us -> 4.22 us
  between operations: 14.3 us -> 0.89 us
  matrix products: 3.08 us -> 0 us
    ppermute x0 -> x12, starting transfers between devices: none -> 59.4 us  [the longest x6 38.7 us: shift(): lax.ppermute(value, axis, [(i, (i + by) % size) for i in range(size)])]
    all_to_all x2 -> x0, blocking collectives: 53.6 us -> none  [the longest x1 36 us: sum_at_owner(): tiles = lax.all_to_all(split_up(value, dim, size), axis, 0, 0, tiled=True)]
    ppermute x0 -> x12, waiting for transfers between devices: none -> 34.6 us  [the longest x6 27.6 us: trade(): return lax.ppermute(value, axis, [(i, i ^ bit) for i in range(size)])]
    all_to_all x3, waiting for transfers between devices: 60.3 us -> 27.4 us  [the longest x1 15.4 us: local(): gathered = lax.all_to_all(sums, ('zl', 'y'), 0, 0, tiled=True)]
    all_gather x1 -> x0, waiting for transfers between devices: 20.7 us -> none  [local(): all_tokens = lax.all_gather(rotated, 'dp', axis=0, tiled=True)]
    convert_element_type x4 -> x2, other arithmetic: 18.6 us -> 0.72 us  [the longest x1 0.69 us: local(): sylvester(HB).astype(BF16)]
    pallas_call x0 -> x5, Pallas kernels: none -> 17.7 us  [the longest x1 6.74 us: local(): call(lambda *refs: weight_kernel(rows, *refs), [jax.ShapeDtypeStruct((fea...]
    all_to_all x3 -> x1, local copies, waits for them, and re-layouts: 13.3 us -> 0.51 us  [local(): everyone = lax.all_to_all(spread, ('x', 'zh', 'c'), 0, 0, tiled=True)]
  transfers between devices with their start and end apart: 4 -> 15, of which waited for: 4 -> 8; matrix products, arithmetic and copies ran while one was open for 17% -> 3% of each run, Pallas kernels for 0% -> 4%
where the time goes in v1:
time: 190 us; the launch traced here: 189 us
  starting transfers between devices  97.8 us (51%)
  waiting for transfers between devices  62 us (33%)
  Pallas kernels  17.7 us (9%)
  local copies, waits for them, and re-layouts  6.74 us (4%)
  other arithmetic  4.22 us (2%)
    ppermute x6, starting transfers between devices, shift(): lax.ppermute(value, axis, [(i, (i + by) % size) for i in range(size)])  38.7 us
    ppermute x6, waiting for transfers between devices, trade(): return lax.ppermute(value, axis, [(i, i ^ bit) for i in range(size)])  27.6 us
    ppermute x6, starting transfers between devices, trade(): return lax.ppermute(value, axis, [(i, i ^ bit) for i in range(size)])  20.7 us
    all_to_all x1, starting transfers between devices, local(): home = lax.all_to_all(wire, ('x', 'zh'), 0, 0, tiled=True)  18.2 us
    all_to_all x1, starting transfers between devices, local(): everyone = lax.all_to_all(spread, ('x', 'zh', 'c'), 0, 0, tiled=True)  15.9 us
    all_to_all x1, waiting for transfers between devices, local(): gathered = lax.all_to_all(sums, ('zl', 'y'), 0, 0, tiled=True)  15.4 us
    all_to_all x1, waiting for transfers between devices, local(): everyone = lax.all_to_all(spread, ('x', 'zh', 'c'), 0, 0, tiled=True)  11.3 us
    ppermute x6, waiting for transfers between devices, shift(): lax.ppermute(value, axis, [(i, (i + by) % size) for i in range(size)])  6.96 us
  transfers between devices with their start and end apart: 15, of which 8 were waited for; matrix products, arithmetic and copies ran while one was open for 3% of the time, Pallas kernels for 4%

profile of v1, /device:TPU:1, one launch (start us, length us, event | category | flops | bytes accessed | tf_op | source)
XLA Modules:
  0.0 189.3 jit_solution(4927121448495112636)
XLA Ops:
  2.0 2.8 %shard_map.69 = bf16[16,56,512]{2,1,0:T(8,128)(2,1)} custom-call(s32[52,8192]{1,0:T(8,128)} %codes.1, s32[52,64]{1,0:T(8,128)} %index.1, s32[52,64]{1,0:T(8,128)} %bitcast.12), custom_call_target="tpu_custom_call" | custom-call | bytes 2555904 | tf_op jit(solution)/shard_map/pallas_call | solution.py:149
  4.7 18.2 %all-to-all-start = ((bf16[16,56,512]{2,1,0:T(8,128)(2,1)}), bf16[16,56,512]{2,1,0:T(8,128)(2,1)S(1)}, u32[]{:S(2)}, u32[]{:S(2)}) async-start(bf16[16,56,512]{2,1,0:T(8,128)(2,1)} %shard_map.69), calls=%async_computation | async-start | bytes 1835008 | tf_op jit(solution)/shard_map/all_to_all | solution.py:154
  25.4 3.2 %collective-permute-start = (f32[20,1664]{1,0:T(8,128)}, f32[20,1664]{1,0:T(8,128)S(1)}, u32[]{:S(2)}, u32[]{:S(2)}) collective-permute-start(f32[20,1664]{1,0:T(8,128)} %shard_map.68), channel_id=1, source_target_pairs={{0,1},{1,0},{2,3},{3,2},{4,5},{5,4},{6,7},{7,6},{8,9},{9,8},{10,11... | collective-permute-start | bytes 399368 | tf_op jit(solution)/shard_map/ppermute | solution.py:140
  28.6 3.6 %collective-permute-done = f32[20,1664]{1,0:T(8,128)S(1)} collective-permute-done((f32[20,1664]{1,0:T(8,128)}, f32[20,1664]{1,0:T(8,128)S(1)}, u32[]{:S(2)}, u32[]{:S(2)}) %collective-permute-start) | collective-permute-done | bytes 133152 | tf_op jit(solution)/shard_map/ppermute | solution.py:140
  33.2 4.8 %collective-permute-start.1 = (f32[20,1664]{1,0:T(8,128)S(1)}, f32[20,1664]{1,0:T(8,128)S(1)}, u32[]{:S(2)}, u32[]{:S(2)}) collective-permute-start(f32[20,1664]{1,0:T(8,128)S(1)} %multiply_add_fusion.2), channel_id=1, source_target_pairs={{0,2},{1,3},{2,0},{3,1},{4,6},{5,7},{6,4},{7,5},{8,10},{9,11},{10,... | collective-permute-start | bytes 399368 | tf_op jit(solution)/shard_map/ppermute | solution.py:140
  38.0 3.0 %collective-permute-done.1 = f32[20,1664]{1,0:T(8,128)S(1)} collective-permute-done((f32[20,1664]{1,0:T(8,128)S(1)}, f32[20,1664]{1,0:T(8,128)S(1)}, u32[]{:S(2)}, u32[]{:S(2)}) %collective-permute-start.1) | collective-permute-done | bytes 133152 | tf_op jit(solution)/shard_map/ppermute | solution.py:140
  41.0 2.6 %collective-permute-start.2 = (f32[20,1664]{1,0:T(8,128)S(1)}, f32[20,1664]{1,0:T(8,128)S(1)}, u32[]{:S(2)}, u32[]{:S(2)}) collective-permute-start(f32[20,1664]{1,0:T(8,128)S(1)} %multiply_add_fusion.1), channel_id=1, source_target_pairs={{0,4},{4,0},{8,12},{12,8},{1,5},{5,1},{9,13},{13,9},{2,6},{6,2},{1... | collective-permute-start | bytes 399368 | tf_op jit(solution)/shard_map/ppermute | solution.py:140
  43.7 20.8 %collective-permute-done.2 = f32[20,1664]{1,0:T(8,128)S(1)} collective-permute-done((f32[20,1664]{1,0:T(8,128)S(1)}, f32[20,1664]{1,0:T(8,128)S(1)}, u32[]{:S(2)}, u32[]{:S(2)}) %collective-permute-start.2) | collective-permute-done | bytes 133152 | tf_op jit(solution)/shard_map/ppermute | solution.py:140
  64.5 1.9 %collective-permute-start.3 = (f32[20,1664]{1,0:T(8,128)S(1)}, f32[20,1664]{1,0:T(8,128)S(1)}, u32[]{:S(2)}, u32[]{:S(2)}) collective-permute-start(f32[20,1664]{1,0:T(8,128)S(1)} %multiply_add_fusion), channel_id=1, source_target_pairs={{0,8},{4,12},{8,0},{12,4},{1,9},{5,13},{9,1},{13,5},{2,10},{6,14},... | collective-permute-start | bytes 399368 | tf_op jit(solution)/shard_map/ppermute | solution.py:140
  67.1 6.0 %collective-permute-start.10 = (bf16[16,56,512]{2,1,0:T(8,128)(2,1)S(1)}, bf16[16,56,512]{2,1,0:T(8,128)(2,1)S(1)}, u32[]{:S(2)}, u32[]{:S(2)}) collective-permute-start(bf16[16,56,512]{2,1,0:T(8,128)(2,1)S(1)} %all-to-all-done.refs_0_), channel_id=1, source_target_pairs={{0,16},{16,0},{1,17},{17,1},{2,18},{18,2},{3,19},{19,3},{4,20},{20... | collective-permute-start | bytes 2752520 | tf_op jit(solution)/shard_map/ppermute | solution.py:140
  73.4 7.9 %collective-permute-start.4 = (bf16[20,1664]{1,0:T(8,128)(2,1)S(1)}, bf16[20,1664]{1,0:T(8,128)(2,1)S(1)}, u32[]{:S(2)}, u32[]{:S(2)}) collective-permute-start(bf16[20,1664]{1,0:T(8,128)(2,1)S(1)} %multiply_convert_fusion), channel_id=1, source_target_pairs={{0,32},{32,64},{64,96},{96,0},{1,33},{33,65},{65,97},{97,1},{2,34}... | collective-permute-start | bytes 199688 | tf_op jit(solution)/shard_map/ppermute | solution.py:136
  81.3 11.9 %collective-permute-start.5 = (bf16[20,1664]{1,0:T(8,128)(2,1)S(1)}, bf16[20,1664]{1,0:T(8,128)(2,1)S(1)}, u32[]{:S(2)}, u32[]{:S(2)}) collective-permute-start(bf16[20,1664]{1,0:T(8,128)(2,1)S(1)} %multiply_convert_fusion), channel_id=1, source_target_pairs={{0,64},{32,96},{64,0},{96,32},{1,65},{33,97},{65,1},{97,33},{2,66}... | collective-permute-start | bytes 199688 | tf_op jit(solution)/shard_map/ppermute | solution.py:136
  93.3 7.3 %collective-permute-start.6 = (bf16[20,1664]{1,0:T(8,128)(2,1)S(1)}, bf16[20,1664]{1,0:T(8,128)(2,1)S(1)}, u32[]{:S(2)}, u32[]{:S(2)}) collective-permute-start(bf16[20,1664]{1,0:T(8,128)(2,1)S(1)} %multiply_convert_fusion), channel_id=1, source_target_pairs={{0,96},{32,0},{64,32},{96,64},{1,97},{33,1},{65,33},{97,65},{2,98}... | collective-permute-start | bytes 199688 | tf_op jit(solution)/shard_map/ppermute | solution.py:136
  100.6 6.9 %collective-permute-done.6 = bf16[20,1664]{1,0:T(8,128)(2,1)S(1)} collective-permute-done((bf16[20,1664]{1,0:T(8,128)(2,1)S(1)}, bf16[20,1664]{1,0:T(8,128)(2,1)S(1)}, u32[]{:S(2)}, u32[]{:S(2)}) %collective-permute-start.6) | collective-permute-done | bytes 66592 | tf_op jit(solution)/shard_map/ppermute | solution.py:136
  107.6 4.2 %collective-permute-start.7 = (bf16[80,1664]{1,0:T(8,128)(2,1)S(1)}, bf16[80,1664]{1,0:T(8,128)(2,1)S(1)}, u32[]{:S(2)}, u32[]{:S(2)}) collective-permute-start(bf16[80,1664]{1,0:T(8,128)(2,1)S(1)} %pad_maximum_fusion.t0), channel_id=1, source_target_pairs={{0,128},{128,256},{256,384},{384,0},{1,129},{129,257},{257,385},{3... | collective-permute-start | bytes 798728 | tf_op jit(solution)/shard_map/ppermute | solution.py:136
  111.8 4.3 %collective-permute-start.8 = (bf16[80,1664]{1,0:T(8,128)(2,1)S(1)}, bf16[80,1664]{1,0:T(8,128)(2,1)S(1)}, u32[]{:S(2)}, u32[]{:S(2)}) collective-permute-start(bf16[80,1664]{1,0:T(8,128)(2,1)S(1)} %pad_maximum_fusion.t0), channel_id=1, source_target_pairs={{0,256},{128,384},{256,0},{384,128},{1,257},{129,385},{257,1},{385... | collective-permute-start | bytes 798728 | tf_op jit(solution)/shard_map/ppermute | solution.py:136
  116.1 3.1 %collective-permute-start.9 = (bf16[80,1664]{1,0:T(8,128)(2,1)S(1)}, bf16[80,1664]{1,0:T(8,128)(2,1)S(1)}, u32[]{:S(2)}, u32[]{:S(2)}) collective-permute-start(bf16[80,1664]{1,0:T(8,128)(2,1)S(1)} %pad_maximum_fusion.t0), channel_id=1, source_target_pairs={{0,384},{128,0},{256,128},{384,256},{1,385},{129,1},{257,129},{385... | collective-permute-start | bytes 798728 | tf_op jit(solution)/shard_map/ppermute | solution.py:136
  120.8 6.7 %shard_map.70 = (bf16[1664,512]{1,0:T(8,128)(2,1)}, bf16[1664,512]{1,0:T(8,128)(2,1)}) custom-call(bf16[16,56,512]{2,1,0:T(8,128)(2,1)} %copy-done, bf16[16,56,512]{2,1,0:T(8,128)(2,1)} %copy-done.3, f32[16]{0:T(128)} %refs_2_.1, s32[3]{0:T(128)} %pad_add_fusion.refs_3_.place), custom_call_target="tpu_custom_call" | custom-call | flops 17039360 | bytes 5111808 | tf_op jit(solution)/shard_map/pallas_call | solution.py:170
  128.4 4.6 %shard_map.71 = bf16[16,40,512]{2,1,0:T(8,128)(2,1)} custom-call(bf16[80,1664]{1,0:T(8,128)(2,1)} %copy-done.2, bf16[80,1664]{1,0:T(8,128)(2,1)} %copy-done.4, bf16[80,1664]{1,0:T(8,128)(2,1)} %copy-done.5, bf16[80,1664]{1,0:T(8,128)(2,1)} %copy-done.6, bf16[1664,512]{1,0:T(8,128)(2,1)} %get-tuple-element.6.base_w, ...), custom_call_target="tpu_custom_call" | custom-call | flops 1090519040 | bytes 4472832 | tf_op jit(solution)/shard_map/pallas_call | solution.py:176
  133.0 4.3 %all-to-all-start.1 = ((bf16[16,40,512]{2,1,0:T(8,128)(2,1)}), bf16[16,40,512]{2,1,0:T(8,128)(2,1)S(1)}, u32[]{:S(2)}, u32[]{:S(2)}) async-start(bf16[16,40,512]{2,1,0:T(8,128)(2,1)} %shard_map.71), calls=%async_computation.1 | async-start | bytes 1310720 | tf_op jit(solution)/shard_map/all_to_all | solution.py:183
  137.3 15.4 %all-to-all-done.1.parts = bf16[16,40,512]{2,1,0:T(8,128)(2,1)S(1)} async-done(((bf16[16,40,512]{2,1,0:T(8,128)(2,1)}), bf16[16,40,512]{2,1,0:T(8,128)(2,1)S(1)}, u32[]{:S(2)}, u32[]{:S(2)}) %all-to-all-start.1) | async-done | bytes 655392 | tf_op jit(solution)/shard_map/all_to_all | solution.py:183
  156.8 15.9 %all-to-all-start.2 = ((f32[32,1,20]{2,1,0:T(1,128)}), f32[32,1,20]{2,1,0:T(1,128)S(1)}, u32[]{:S(2)}, u32[]{:S(2)}) async-start(f32[32,1,20]{2,1,0:T(1,128)} %broadcast_in_dim.5), calls=%async_computation.2 | async-start | bytes 32768 | tf_op jit(solution)/shard_map/all_to_all | solution.py:190
  173.5 2.1 %collective-permute-start.11 = (bf16[20,256]{1,0:T(8,128)(2,1)S(1)}, bf16[20,256]{1,0:T(8,128)(2,1)S(1)}, u32[]{:S(2)}, u32[]{:S(2)}) collective-permute-start(bf16[20,256]{1,0:T(8,128)(2,1)S(1)} %get-tuple-element.11), channel_id=1, source_target_pairs={{0,16},{16,0},{1,17},{17,1},{2,18},{18,2},{3,19},{19,3},{4,20},{20... | collective-permute-start | bytes 30728 | tf_op jit(solution)/shard_map/ppermute | solution.py:140
  175.6 11.3 %all-to-all-done.2 = f32[32,1,20]{2,1,0:T(1,128)S(1)} async-done(((f32[32,1,20]{2,1,0:T(1,128)}), f32[32,1,20]{2,1,0:T(1,128)S(1)}, u32[]{:S(2)}, u32[]{:S(2)}) %all-to-all-start.2) | async-done | bytes 2592 | tf_op jit(solution)/shard_map/all_to_all | solution.py:190
  (42 shorter events, 15.5 us)
Async XLA Ops:
  4.7 62.4 %all-to-all-start = ((bf16[16,56,512]{2,1,0:T(8,128)(2,1)}), bf16[16,56,512]{2,1,0:T(8,128)(2,1)S(1)}, u32[]{:S(2)}, u32[]{:S(2)}) async-start(bf16[16,56,512]{2,1,0:T(8,128)(2,1)} %shard_map.69), calls=%async_computation | async-start | bytes 1835008 | tf_op jit(solution)/shard_map/all_to_all | solution.py:154
  25.4 6.8 %collective-permute-start = (f32[20,1664]{1,0:T(8,128)}, f32[20,1664]{1,0:T(8,128)S(1)}, u32[]{:S(2)}, u32[]{:S(2)}) collective-permute-start(f32[20,1664]{1,0:T(8,128)} %shard_map.68), channel_id=1, source_target_pairs={{0,1},{1,0},{2,3},{3,2},{4,5},{5,4},{6,7},{7,6},{8,9},{9,8},{10,11... | collective-permute-start | bytes 399368 | tf_op jit(solution)/shard_map/ppermute | solution.py:140
  33.2 7.8 %collective-permute-start.1 = (f32[20,1664]{1,0:T(8,128)S(1)}, f32[20,1664]{1,0:T(8,128)S(1)}, u32[]{:S(2)}, u32[]{:S(2)}) collective-permute-start(f32[20,1664]{1,0:T(8,128)S(1)} %multiply_add_fusion.2), channel_id=1, source_target_pairs={{0,2},{1,3},{2,0},{3,1},{4,6},{5,7},{6,4},{7,5},{8,10},{9,11},{10,... | collective-permute-start | bytes 399368 | tf_op jit(solution)/shard_map/ppermute | solution.py:140
  41.0 23.5 %collective-permute-start.2 = (f32[20,1664]{1,0:T(8,128)S(1)}, f32[20,1664]{1,0:T(8,128)S(1)}, u32[]{:S(2)}, u32[]{:S(2)}) collective-permute-start(f32[20,1664]{1,0:T(8,128)S(1)} %multiply_add_fusion.1), channel_id=1, source_target_pairs={{0,4},{4,0},{8,12},{12,8},{1,5},{5,1},{9,13},{13,9},{2,6},{6,2},{1... | collective-permute-start | bytes 399368 | tf_op jit(solution)/shard_map/ppermute | solution.py:140
  64.5 8.9 %collective-permute-start.3 = (f32[20,1664]{1,0:T(8,128)S(1)}, f32[20,1664]{1,0:T(8,128)S(1)}, u32[]{:S(2)}, u32[]{:S(2)}) collective-permute-start(f32[20,1664]{1,0:T(8,128)S(1)} %multiply_add_fusion), channel_id=1, source_target_pairs={{0,8},{4,12},{8,0},{12,4},{1,9},{5,13},{9,1},{13,5},{2,10},{6,14},... | collective-permute-start | bytes 399368 | tf_op jit(solution)/shard_map/ppermute | solution.py:140
  67.1 52.7 %copy-start = (bf16[16,56,512]{2,1,0:T(8,128)(2,1)}, bf16[16,56,512]{2,1,0:T(8,128)(2,1)S(1)}, u32[]{:S(2)}) copy-start(bf16[16,56,512]{2,1,0:T(8,128)(2,1)S(1)} %all-to-all-done.refs_0_) | copy-start | bytes 2752516
  67.1 52.7 %collective-permute-start.10 = (bf16[16,56,512]{2,1,0:T(8,128)(2,1)S(1)}, bf16[16,56,512]{2,1,0:T(8,128)(2,1)S(1)}, u32[]{:S(2)}, u32[]{:S(2)}) collective-permute-start(bf16[16,56,512]{2,1,0:T(8,128)(2,1)S(1)} %all-to-all-done.refs_0_), channel_id=1, source_target_pairs={{0,16},{16,0},{1,17},{17,1},{2,18},{18,2},{3,19},{19,3},{4,20},{20... | collective-permute-start | bytes 2752520 | tf_op jit(solution)/shard_map/ppermute | solution.py:140
  73.4 27.1 %collective-permute-start.4 = (bf16[20,1664]{1,0:T(8,128)(2,1)S(1)}, bf16[20,1664]{1,0:T(8,128)(2,1)S(1)}, u32[]{:S(2)}, u32[]{:S(2)}) collective-permute-start(bf16[20,1664]{1,0:T(8,128)(2,1)S(1)} %multiply_convert_fusion), channel_id=1, source_target_pairs={{0,32},{32,64},{64,96},{96,0},{1,33},{33,65},{65,97},{97,1},{2,34}... | collective-permute-start | bytes 199688 | tf_op jit(solution)/shard_map/ppermute | solution.py:136
  81.3 19.2 %collective-permute-start.5 = (bf16[20,1664]{1,0:T(8,128)(2,1)S(1)}, bf16[20,1664]{1,0:T(8,128)(2,1)S(1)}, u32[]{:S(2)}, u32[]{:S(2)}) collective-permute-start(bf16[20,1664]{1,0:T(8,128)(2,1)S(1)} %multiply_convert_fusion), channel_id=1, source_target_pairs={{0,64},{32,96},{64,0},{96,32},{1,65},{33,97},{65,1},{97,33},{2,66}... | collective-permute-start | bytes 199688 | tf_op jit(solution)/shard_map/ppermute | solution.py:136
  93.3 14.2 %collective-permute-start.6 = (bf16[20,1664]{1,0:T(8,128)(2,1)S(1)}, bf16[20,1664]{1,0:T(8,128)(2,1)S(1)}, u32[]{:S(2)}, u32[]{:S(2)}) collective-permute-start(bf16[20,1664]{1,0:T(8,128)(2,1)S(1)} %multiply_convert_fusion), channel_id=1, source_target_pairs={{0,96},{32,0},{64,32},{96,64},{1,97},{33,1},{65,33},{97,65},{2,98}... | collective-permute-start | bytes 199688 | tf_op jit(solution)/shard_map/ppermute | solution.py:136
  107.6 19.9 %copy-start.2 = (bf16[80,1664]{1,0:T(8,128)(2,1)}, bf16[80,1664]{1,0:T(8,128)(2,1)S(1)}, u32[]{:S(2)}) copy-start(bf16[80,1664]{1,0:T(8,128)(2,1)S(1)} %pad_maximum_fusion.t0) | copy-start | bytes 798724
  107.6 19.9 %collective-permute-start.7 = (bf16[80,1664]{1,0:T(8,128)(2,1)S(1)}, bf16[80,1664]{1,0:T(8,128)(2,1)S(1)}, u32[]{:S(2)}, u32[]{:S(2)}) collective-permute-start(bf16[80,1664]{1,0:T(8,128)(2,1)S(1)} %pad_maximum_fusion.t0), channel_id=1, source_target_pairs={{0,128},{128,256},{256,384},{384,0},{1,129},{129,257},{257,385},{3... | collective-permute-start | bytes 798728 | tf_op jit(solution)/shard_map/ppermute | solution.py:136
  111.8 15.7 %collective-permute-start.8 = (bf16[80,1664]{1,0:T(8,128)(2,1)S(1)}, bf16[80,1664]{1,0:T(8,128)(2,1)S(1)}, u32[]{:S(2)}, u32[]{:S(2)}) collective-permute-start(bf16[80,1664]{1,0:T(8,128)(2,1)S(1)} %pad_maximum_fusion.t0), channel_id=1, source_target_pairs={{0,256},{128,384},{256,0},{384,128},{1,257},{129,385},{257,1},{385... | collective-permute-start | bytes 798728 | tf_op jit(solution)/shard_map/ppermute | solution.py:136
  116.1 11.4 %collective-permute-start.9 = (bf16[80,1664]{1,0:T(8,128)(2,1)S(1)}, bf16[80,1664]{1,0:T(8,128)(2,1)S(1)}, u32[]{:S(2)}, u32[]{:S(2)}) collective-permute-start(bf16[80,1664]{1,0:T(8,128)(2,1)S(1)} %pad_maximum_fusion.t0), channel_id=1, source_target_pairs={{0,384},{128,0},{256,128},{384,256},{1,385},{129,1},{257,129},{385... | collective-permute-start | bytes 798728 | tf_op jit(solution)/shard_map/ppermute | solution.py:136
  119.8 0.9 copy-start.3
  127.5 0.7 copy-start.4
  127.5 0.8 copy-start.5
  127.5 0.9 copy-start.6
  133.0 19.7 %all-to-all-start.1 = ((bf16[16,40,512]{2,1,0:T(8,128)(2,1)}), bf16[16,40,512]{2,1,0:T(8,128)(2,1)S(1)}, u32[]{:S(2)}, u32[]{:S(2)}) async-start(bf16[16,40,512]{2,1,0:T(8,128)(2,1)} %shard_map.71), calls=%async_computation.1 | async-start | bytes 1310720 | tf_op jit(solution)/shard_map/all_to_all | solution.py:183
  152.7 0.9 copy-start.1
  156.8 30.1 %all-to-all-start.2 = ((f32[32,1,20]{2,1,0:T(1,128)}), f32[32,1,20]{2,1,0:T(1,128)S(1)}, u32[]{:S(2)}, u32[]{:S(2)}) async-start(f32[32,1,20]{2,1,0:T(1,128)} %broadcast_in_dim.5), calls=%async_computation.2 | async-start | bytes 32768 | tf_op jit(solution)/shard_map/all_to_all | solution.py:190
  173.5 15.2 %collective-permute-start.11 = (bf16[20,256]{1,0:T(8,128)(2,1)S(1)}, bf16[20,256]{1,0:T(8,128)(2,1)S(1)}, u32[]{:S(2)}, u32[]{:S(2)}) collective-permute-start(bf16[20,256]{1,0:T(8,128)(2,1)S(1)} %get-tuple-element.11), channel_id=1, source_target_pairs={{0,16},{16,0},{1,17},{17,1},{2,18},{18,2},{3,19},{19,3},{4,20},{20... | collective-permute-start | bytes 30728 | tf_op jit(solution)/shard_map/ppermute | solution.py:140

commit v2 on v1

v2 whole, which is shorter than its diff:
```python
import math

import jax
import jax.numpy as jnp
import numpy as np
from jax import lax
from jax.experimental import pallas as pl
from jax.experimental.pallas import tpu as pltpu
from jax.sharding import Mesh, PartitionSpec as P


HB = 128
LANES = 128
AXES = ("x", "zh", "c", "zl", "y")
SIZES = (4, 4, 2, 4, 4)
CHUNK = 104
SCORE_DIVISOR = 512.0
F32 = jnp.float32
BF16 = jnp.bfloat16
VMEM = pl.BlockSpec(memory_space=pltpu.VMEM)
SMEM = pl.BlockSpec(memory_space=pltpu.SMEM)


def chunk_signs():
    at = np.arange(HB)
    both = at[:, None] & at[None, :]
    parity = np.zeros((HB, HB), np.int64)
    for bit in range(7):
        parity ^= both >> bit & 1
    block = 1 - 2 * parity
    signs = np.zeros((16, 2 * HB, LANES), np.float32)
    first = []
    for m in range(16):
        n0 = min(CHUNK * m // HB, 11)
        first.append(n0 * HB)
        for w in range(CHUNK):
            h = CHUNK * m + w
            row = (h // HB - n0) * HB
            signs[m, row : row + HB, w] = block[:, h % HB]
    return signs, first


SIGNS, FIRST = chunk_signs()


def call(kernel, out_shape, in_specs, scratch=(), flops=0, moved=0, limit=16):
    multi = isinstance(out_shape, (list, tuple))
    return pl.pallas_call(
        kernel,
        out_shape=out_shape,
        in_specs=in_specs,
        out_specs=[VMEM] * len(out_shape) if multi else VMEM,
        scratch_shapes=list(scratch),
        compiler_params=pltpu.CompilerParams(vmem_limit_bytes=limit << 20),
        cost_estimate=pl.CostEstimate(flops=flops, bytes_accessed=moved, transcendentals=0),
    )


def block_kernel(act, signs, out):
    for m in range(16):
        xd, zd = divmod(m, 4)
        piece = jnp.dot(act[:, FIRST[m] : FIRST[m] + 2 * HB], signs[m], preferred_element_type=F32)
        out[zd, :, xd * LANES : (xd + 1) * LANES] = piece


def pack_kernel(codes, index, bits, out, meta, turned, block):
    rows = codes.shape[0]
    groups = index.shape[1]
    meta[...] = jnp.zeros_like(meta)
    meta[0:rows, 0:groups] = index[...].astype(F32)
    meta[0:rows, groups : 2 * groups] = bits[...].astype(F32)
    turned[...] = meta[...].T
    block[...] = jnp.zeros_like(block)
    for p in range(16):
        xd, yd = divmod(p, 4)
        for k in range(4):
            g = 16 * xd + 4 * k + yd
            block[0:rows, k * LANES : (k + 1) * LANES] = codes[:, g * LANES : (g + 1) * LANES].astype(F32)
            block[rows + k : rows + k + 1, 0:LANES] = turned[g : g + 1, :]
            block[rows + k : rows + k + 1, LANES : 2 * LANES] = turned[groups + g : groups + g + 1, :]
        out[p] = block[...].astype(BF16)


def weight_kernel(rows, own, other, table, place, base, diff, meta, base_acc, diff_acc):
    padded = own.shape[1]
    first = place[2] == 0
    turned = []
    for core in range(2):
        mine, theirs = (own, other) if core == 0 else (other, own)
        for p in range(16):
            tail = jnp.where(first, mine[p, padded - 8 : padded, :].astype(F32), theirs[p, padded - 8 : padded, :].astype(F32))
            meta[p * 4 : p * 4 + 4, :] = tail[4:, 0:LANES]
            meta[64 + p * 4 : 68 + p * 4, :] = tail[4:, LANES : 2 * LANES]
        index = meta[0:64, :]
        scale = jnp.zeros_like(index)
        for entry in range(table.shape[0]):
            scale = jnp.where(index == float(entry), table[entry], scale)
        meta[0:64, :] = scale
        turned.append(meta[...].T)
    blank = jnp.zeros((LANES - 2 * rows, own.shape[2]), F32)
    for yd in range(4):
        for xd in range(4):
            p = xd * 4 + yd
            top = (yd * 4 + xd) * LANES
            for core in range(2):
                mine, theirs = (own, other) if core == 0 else (other, own)
                start = top + core * rows
                for k in range(4):
                    cols = slice(k * LANES, (k + 1) * LANES)
                    code = jnp.where(first, mine[p, :, cols], theirs[p, :, cols]).astype(F32)
                    at = p * 4 + k
                    scale = turned[core][0:padded, at : at + 1]
                    held = turned[core][0:padded, 64 + at : 65 + at]
                    two = jnp.floor(code * 0.25) * 4.0 + 2.0
                    three = jnp.floor(code * 0.5) * 2.0 + 1.0
                    cand = jnp.where(held == 2.0, two, jnp.where(held == 3.0, three, code))
                    base_w = ((code - 8.0) * scale).astype(BF16).astype(F32)
                    cand_w = ((cand - 8.0) * scale).astype(BF16).astype(F32)
                    base_acc[start : start + padded, cols] = base_w
                    diff_acc[start : start + padded, cols] = cand_w - base_w
            base_acc[top + 2 * rows : top + LANES, :] = blank
            diff_acc[top + 2 * rows : top + LANES, :] = blank
    base[...] = base_acc[...].astype(BF16)
    diff[...] = diff_acc[...].astype(BF16)


def matmul_kernel(tokens, base_w, diff_w, out, left):
    rows, wide = tokens.shape[1:]
    factor = 1.0 / math.sqrt(HB * 16)
    for xd in range(4):
        s = [tokens[xd * 4 + yd].astype(F32) for yd in range(4)]
        a, b, c, d = s[0] + s[1], s[0] - s[1], s[2] + s[3], s[2] - s[3]
        for j, mixed in enumerate((a + c, b + d, a - c, b - d)):
            left[xd * rows : (xd + 1) * rows, j * wide : (j + 1) * wide] = (mixed * factor).astype(BF16)
    base = jnp.dot(left[...], base_w[...], preferred_element_type=F32).astype(BF16)
    diff = jnp.dot(left[...], diff_w[...], preferred_element_type=F32).astype(BF16)
    for xd in range(4):
        out[xd, 0:rows, :] = base[xd * rows : (xd + 1) * rows, :]
        out[xd, rows : 2 * rows, :] = diff[xd * rows : (xd + 1) * rows, :]


def near_kernel(parts, out, base, send):
    rows = parts.shape[1] // 2
    toks = rows // 4
    total = parts[0].astype(F32)
    for k in range(1, 4):
        total = total + parts[k].astype(F32)
    base[...] = total[0:rows, :]
    for zd in range(4):
        send[0:rows, :] = total[rows:, :]
        for yd in range(4):
            send[rows : rows + toks, yd * LANES : (yd + 1) * LANES] = base[
                yd * toks : (yd + 1) * toks, zd * LANES : (zd + 1) * LANES
            ]
        out[zd] = send[...].astype(BF16)


def far_kernel(parts, base, score, total):
    acc = parts[0].astype(F32)
    for k in range(1, 4):
        acc = acc + parts[k].astype(F32)
    total[...] = acc
    rows = score.shape[0]
    toks = rows // 4
    for yd in range(4):
        base[yd] = total[rows : rows + toks, yd * LANES : (yd + 1) * LANES].astype(BF16)
    gap = total[0:rows, :]
    score[...] = jnp.broadcast_to(jnp.sum(gap * gap, axis=1, keepdims=True), score.shape)


def trade(value, axis, bit, size=4):
    return lax.ppermute(value, axis, [(i, i ^ bit) for i in range(size)])


def local(activations, weight_codes, scale_index, scale_table, bit_widths):
  place = jnp.stack([lax.axis_index(a) for a in ("x", "zh", "c", "y")]).astype(jnp.int32)
  toks, feat = activations.shape
  store, width = weight_codes.shape
  part = width // 16
  padded = store + 4
  wire = call(
      pack_kernel, jax.ShapeDtypeStruct((16, padded, part), BF16), [VMEM] * 3,
      [pltpu.VMEM((128, 128), F32), pltpu.VMEM((128, 128), F32), pltpu.VMEM((padded, part), F32)],
      0, store * width * 6, 8,
  )(weight_codes, scale_index, bit_widths.reshape(store, -1))
  home = lax.all_to_all(wire, ("x", "y"), 0, 0, tiled=True)
  other = trade(home, "c", 1, 2)

  value = call(
      block_kernel, jax.ShapeDtypeStruct((4, toks, 4 * LANES), F32), [VMEM] * 2,
      (), 2 * toks * 4096 * HB, 1 << 20, 8,
  )(activations, jnp.asarray(SIGNS, BF16))
  for axis, bit in (("zl", 1), ("zl", 2)):
      sign = jnp.where(lax.axis_index(axis) & bit, -1.0, 1.0).astype(F32)
      value = trade(value, axis, bit) + sign * value
  value = lax.all_to_all(value.astype(BF16), "zh", 0, 0, tiled=True)
  value = value.reshape(4 * toks, 4 * LANES)
  tokens = lax.all_to_all(jnp.broadcast_to(value[None], (16,) + value.shape), ("x", "y"), 0, 0, tiled=True)

  base_w, diff_w = call(
      lambda *refs: weight_kernel(store, *refs),
      [jax.ShapeDtypeStruct((16 * LANES, part), BF16)] * 2, [VMEM, VMEM, SMEM, SMEM],
      [pltpu.VMEM((128, 128), F32)] + [pltpu.VMEM((16 * LANES, part), F32)] * 2,
      feat * part * 20, feat * part * 6, 24,
  )(home, other, scale_table, place)
  sums = call(
      matmul_kernel, jax.ShapeDtypeStruct((4, 8 * toks, part), BF16),
      [VMEM] * 3, [pltpu.VMEM((16 * toks, 16 * LANES), BF16)],
      4 * 16 * toks * feat * part, feat * part * 4 + 16 * toks * feat * 2, 20,
  )(tokens, base_w, diff_w)
  near = lax.all_to_all(sums, "zl", 0, 0, tiled=True)
  wave = call(
      near_kernel, jax.ShapeDtypeStruct((4, 5 * toks, part), BF16), [VMEM],
      [pltpu.VMEM((4 * toks, part), F32), pltpu.VMEM((5 * toks, part), F32)],
      32 * toks * part, 64 * toks * part, 8,
  )(near)
  far = lax.all_to_all(wave, "zh", 0, 0, tiled=True)
  pieces, score = call(
      far_kernel,
      [jax.ShapeDtypeStruct((4, toks, LANES), BF16), jax.ShapeDtypeStruct((4 * toks, LANES), F32)],
      [VMEM], [pltpu.VMEM((5 * toks, part), F32)], 32 * toks * part, 40 * toks * part, 8,
  )(far)
  mine = score[:, 0].reshape(1, 4, 1, 1, toks)
  spread = jnp.broadcast_to(mine, (4, 4, 2, 1, toks)).reshape(32, 1, toks)
  everyone = lax.all_to_all(spread, ("x", "y", "c"), 0, 0, tiled=True)
  scores = jnp.sum(everyone.reshape(16, 2 * toks), axis=0)[None] / SCORE_DIVISOR
  y, c = lax.axis_index("y"), lax.axis_index("c")
  got = []
  for r in range(4):
      pairs = []
      for cs in range(2):
          for ys in range(4):
              pairs.append((cs * 4 + ys, (ys // 2) * 4 + (2 * (ys % 2) + cs + r) % 4))
      piece = lax.dynamic_index_in_dim(pieces, lax.rem(2 * lax.rem(y, 2) + c + r, 4), 0, False)
      got.append(lax.ppermute(piece, ("c", "y"), pairs))
  got = jnp.stack(got)
  rows = []
  for cs in range(2):
      rows.append(jnp.concatenate(
          [lax.dynamic_index_in_dim(got, lax.rem(y - 2 * i - cs + 4, 4), 0, False) for i in range(2)], axis=1))
  base = jnp.concatenate(rows, axis=0)
  return base, scores


def solution(mesh):
    fine = Mesh(mesh.devices.reshape(SIZES), AXES)
    dp, tensor = ("x", "zh", "c"), ("zl", "y")
    return jax.shard_map(
        local, mesh=fine,
        in_specs=(P(dp, tensor), P(tensor + dp, None), P(tensor + dp, None), P(), P(None, tensor + dp, None)),
        out_specs=(P(tensor, dp), P(None, tensor)),
        check_vma=False,
    )
```

time: 190 us -> 173 us (0.911)
  starting transfers between devices: 97.8 us -> 66.6 us
  blocking collectives: 0 us -> 18.4 us
  Pallas kernels: 17.7 us -> 8.34 us
  local copies, waits for them, and re-layouts: 6.74 us -> 10.7 us
    ppermute x6 -> x4, starting transfers between devices: 38.7 us -> 11.7 us  [local(): got.append(lax.ppermute(piece, ('c', 'y'), pairs))]
    all_to_all x3 -> x5, waiting for transfers between devices: 27.4 us -> 50.7 us  [the longest x1 22.5 us: local(): far = lax.all_to_all(wave, 'zh', 0, 0, tiled=True)]
    all_to_all x0 -> x1, blocking collectives: none -> 18.4 us  [local(): near = lax.all_to_all(sums, 'zl', 0, 0, tiled=True)]
    ppermute x6 -> x3, waiting for transfers between devices: 27.6 us -> 10.2 us  [trade(): return lax.ppermute(value, axis, [(i, i ^ bit) for i in range(size)])]
    pallas_call x4 -> x5, Pallas kernels: 14.9 us -> 7.05 us  [the longest x1 4.16 us: local(): call(lambda *refs: weight_kernel(store, *refs), [jax.ShapeDtypeStruct((16...]
    ppermute x6 -> x3, starting transfers between devices: 20.7 us -> 15.1 us  [trade(): return lax.ppermute(value, axis, [(i, i ^ bit) for i in range(size)])]
    ppermute x6 -> x4, waiting for transfers between devices: 6.96 us -> 2.39 us  [local(): got.append(lax.ppermute(piece, ('c', 'y'), pairs))]
    unnamed x15 -> x21, local copies, waits for them, and re-layouts: 3.98 us -> 8.06 us
  transfers between devices with their start and end apart: 15 -> 12, of which waited for: 8 -> 8; matrix products, arithmetic and copies ran while one was open for 3% -> 1% of each run, Pallas kernels for 4% -> 3%
where the time goes in v2:
time: 173 us; the launch traced here: 171 us
  starting transfers between devices  66.6 us (38%)
  waiting for transfers between devices  63.3 us (37%)
  blocking collectives  18.4 us (11%)
  local copies, waits for them, and re-layouts  10.7 us (6%)
  Pallas kernels  8.34 us (5%)
  other arithmetic  2.62 us (2%)
    all_to_all x1, waiting for transfers between devices, local(): far = lax.all_to_all(wave, 'zh', 0, 0, tiled=True)  22.5 us
    all_to_all x1, blocking collectives, local(): near = lax.all_to_all(sums, 'zl', 0, 0, tiled=True)  18.4 us
    all_to_all x1, starting transfers between devices, local(): value = lax.all_to_all(value.astype(BF16), 'zh', 0, 0, tiled=True)  17.7 us
    ppermute x3, starting transfers between devices, trade(): return lax.ppermute(value, axis, [(i, i ^ bit) for i in range(size)])  15.1 us
    all_to_all x1, waiting for transfers between devices, local(): home = lax.all_to_all(wire, ('x', 'y'), 0, 0, tiled=True)  13.1 us
    ppermute x4, starting transfers between devices, local(): got.append(lax.ppermute(piece, ('c', 'y'), pairs))  11.7 us
    all_to_all x1, waiting for transfers between devices, local(): value = lax.all_to_all(value.astype(BF16), 'zh', 0, 0, tiled=True)  10.7 us
    ppermute x3, waiting for transfers between devices, trade(): return lax.ppermute(value, axis, [(i, i ^ bit) for i in range(size)])  10.2 us
  transfers between devices with their start and end apart: 12, of which 8 were waited for; matrix products, arithmetic and copies ran while one was open for 1% of the time, Pallas kernels for 3%

profile of v2, /device:TPU:1, one launch (start us, length us, event | category | flops | bytes accessed | tf_op | source)
XLA Modules:
  0.0 171.0 jit_solution(6171518745852706003)
XLA Ops:
  3.2 4.4 %collective-permute-start = (f32[4,20,512]{2,1,0:T(8,128)S(1)}, f32[4,20,512]{2,1,0:T(8,128)S(1)}, u32[]{:S(2)}, u32[]{:S(2)}) collective-permute-start(f32[4,20,512]{2,1,0:T(8,128)S(1)} %shard_map.77), channel_id=1, source_target_pairs={{0,4},{4,0},{8,12},{12,8},{1,5},{5,1},{9,13},{13,9},{2,6},{6,2},{1... | collective-permute-start | bytes 491528 | tf_op jit(solution)/shard_map/ppermute | solution.py:172
  7.5 3.0 %collective-permute-done = f32[4,20,512]{2,1,0:T(8,128)S(1)} collective-permute-done((f32[4,20,512]{2,1,0:T(8,128)S(1)}, f32[4,20,512]{2,1,0:T(8,128)S(1)}, u32[]{:S(2)}, u32[]{:S(2)}) %collective-permute-start) | collective-permute-done | bytes 163872 | tf_op jit(solution)/shard_map/ppermute | solution.py:172
  10.6 6.3 %collective-permute-start.1 = (f32[4,20,512]{2,1,0:T(8,128)S(1)}, f32[4,20,512]{2,1,0:T(8,128)S(1)}, u32[]{:S(2)}, u32[]{:S(2)}) collective-permute-start(f32[4,20,512]{2,1,0:T(8,128)S(1)} %multiply_add_fusion), channel_id=1, source_target_pairs={{0,8},{4,12},{8,0},{12,4},{1,9},{5,13},{9,1},{13,5},{2,10},{6,14},... | collective-permute-start | bytes 491528 | tf_op jit(solution)/shard_map/ppermute | solution.py:172
  17.0 5.1 %collective-permute-done.1 = f32[4,20,512]{2,1,0:T(8,128)S(1)} collective-permute-done((f32[4,20,512]{2,1,0:T(8,128)S(1)}, f32[4,20,512]{2,1,0:T(8,128)S(1)}, u32[]{:S(2)}, u32[]{:S(2)}) %collective-permute-start.1) | collective-permute-done | bytes 163872 | tf_op jit(solution)/shard_map/ppermute | solution.py:172
  22.8 17.7 %all-to-all-start = ((bf16[4,20,512]{2,1,0:T(8,128)(2,1)}), bf16[4,20,512]{2,1,0:T(8,128)(2,1)S(1)}, u32[]{:S(2)}, u32[]{:S(2)}) async-start(bf16[4,20,512]{2,1,0:T(8,128)(2,1)} %add_convert_fusion), calls=%async_computation | async-start | bytes 196608 | tf_op jit(solution)/shard_map/all_to_all | solution.py:196
  41.8 10.7 %all-to-all-done = bf16[4,20,512]{2,1,0:T(8,128)(2,1)S(1)} async-done(((bf16[4,20,512]{2,1,0:T(8,128)(2,1)}), bf16[4,20,512]{2,1,0:T(8,128)(2,1)S(1)}, u32[]{:S(2)}, u32[]{:S(2)}) %all-to-all-start) | async-done | bytes 81952 | tf_op jit(solution)/shard_map/all_to_all | solution.py:196
  52.6 6.8 %all-to-all-start.2 = ((bf16[16,56,512]{2,1,0:T(8,128)(2,1)}), bf16[16,56,512]{2,1,0:T(8,128)(2,1)S(1)}, u32[]{:S(2)}, u32[]{:S(2)}) async-start(bf16[16,56,512]{2,1,0:T(8,128)(2,1)} %shard_map.78), calls=%async_computation.2 | async-start | bytes 1835008 | tf_op jit(solution)/shard_map/all_to_all | solution.py:186
  59.4 13.1 %all-to-all-done.2.refs_0_ = bf16[16,56,512]{2,1,0:T(8,128)(2,1)S(1)} async-done(((bf16[16,56,512]{2,1,0:T(8,128)(2,1)}), bf16[16,56,512]{2,1,0:T(8,128)(2,1)S(1)}, u32[]{:S(2)}, u32[]{:S(2)}) %all-to-all-start.2) | async-done | bytes 917536 | tf_op jit(solution)/shard_map/all_to_all | solution.py:186
  73.7 4.8 %all-to-all-start.1 = ((bf16[16,80,512]{2,1,0:T(8,128)(2,1)}), bf16[16,80,512]{2,1,0:T(8,128)(2,1)S(1)}, u32[]{:S(2)}, u32[]{:S(2)}) async-start(bf16[16,80,512]{2,1,0:T(8,128)(2,1)} %broadcast_in_dim.18), calls=%async_computation.1 | async-start | bytes 2621440 | tf_op jit(solution)/shard_map/all_to_all | solution.py:198
  78.5 4.3 %collective-permute-start.2 = (bf16[16,56,512]{2,1,0:T(8,128)(2,1)S(1)}, bf16[16,56,512]{2,1,0:T(8,128)(2,1)S(1)}, u32[]{:S(2)}, u32[]{:S(2)}) collective-permute-start(bf16[16,56,512]{2,1,0:T(8,128)(2,1)S(1)} %all-to-all-done.2.refs_0_), channel_id=1, source_target_pairs={{0,16},{16,0},{1,17},{17,1},{2,18},{18,2},{3,19},{19,3},{4,20},{20... | collective-permute-start | bytes 2752520 | tf_op jit(solution)/shard_map/ppermute | solution.py:172
  82.9 2.0 %collective-permute-done.2.refs_1_ = bf16[16,56,512]{2,1,0:T(8,128)(2,1)S(1)} collective-permute-done((bf16[16,56,512]{2,1,0:T(8,128)(2,1)S(1)}, bf16[16,56,512]{2,1,0:T(8,128)(2,1)S(1)}, u32[]{:S(2)}, u32[]{:S(2)}) %collective-permute-start.2) | collective-permute-done | bytes 917536 | tf_op jit(solution)/shard_map/ppermute | solution.py:172
  84.9 4.2 %shard_map.79 = (bf16[2048,512]{1,0:T(8,128)(2,1)S(1)}, bf16[2048,512]{1,0:T(8,128)(2,1)S(1)}) custom-call(bf16[16,56,512]{2,1,0:T(8,128)(2,1)S(1)} %all-to-all-done.2.refs_0_, bf16[16,56,512]{2,1,0:T(8,128)(2,1)S(1)} %collective-permute-done.2.refs_1_, f32[16]{0:T(128)S(1)} %copy-done.8, s32[4]{0:T(128)S(1)} %pad_add_fusion.refs_3_), custom_call_target="tpu_custom_call" | custom-call | flops 17039360 | bytes 5111808 | tf_op jit(solution)/shard_map/pallas_call | solution.py:200
  91.7 4.4 %all-to-all-done.1.tokens = bf16[16,80,512]{2,1,0:T(8,128)(2,1)S(1)} async-done(((bf16[16,80,512]{2,1,0:T(8,128)(2,1)}), bf16[16,80,512]{2,1,0:T(8,128)(2,1)S(1)}, u32[]{:S(2)}, u32[]{:S(2)}) %all-to-all-start.1) | async-done | bytes 1310752 | tf_op jit(solution)/shard_map/all_to_all | solution.py:198
  96.1 1.6 copy-done.1
  97.7 1.6 copy-done.3
  100.9 18.4 %all_to_all.30.parts = bf16[4,160,512]{2,1,0:T(8,128)(2,1)S(1)} all-to-all(bf16[4,160,512]{2,1,0:T(8,128)(2,1)S(1)} %shard_map.80), channel_id=1, replica_groups=mesh['x'=4,'zh'=4,'c'=2,'zl'=4,'y'=4] {'zl'}, dimensions={0} | all-to-all | bytes 1310720 | tf_op jit(solution)/shard_map/all_to_all | solution.py:211
  120.2 3.5 %all-to-all-start.4 = ((bf16[4,100,512]{2,1,0:T(8,128)(2,1)}), bf16[4,100,512]{2,1,0:T(8,128)(2,1)S(1)}, u32[]{:S(2)}, u32[]{:S(2)}) async-start(bf16[4,100,512]{2,1,0:T(8,128)(2,1)} %shard_map.81), calls=%async_computation.4 | async-start | bytes 851968 | tf_op jit(solution)/shard_map/all_to_all | solution.py:217
  123.8 22.5 %all-to-all-done.4.parts = bf16[4,100,512]{2,1,0:T(8,128)(2,1)S(1)} async-done(((bf16[4,100,512]{2,1,0:T(8,128)(2,1)}), bf16[4,100,512]{2,1,0:T(8,128)(2,1)S(1)}, u32[]{:S(2)}, u32[]{:S(2)}) %all-to-all-start.4) | async-done | bytes 409632 | tf_op jit(solution)/shard_map/all_to_all | solution.py:217
  147.2 7.1 %all-to-all-start.5 = ((f32[32,1,20]{2,1,0:T(1,128)}), f32[32,1,20]{2,1,0:T(1,128)S(1)}, u32[]{:S(2)}, u32[]{:S(2)}) async-start(f32[32,1,20]{2,1,0:T(1,128)} %bitcast.16), calls=%async_computation.5 | async-start | bytes 32768 | tf_op jit(solution)/shard_map/all_to_all | solution.py:225
  154.4 2.1 %collective-permute-start.6 = (bf16[20,128]{1,0:T(8,128)(2,1)S(1)}, bf16[20,128]{1,0:T(8,128)(2,1)S(1)}, u32[]{:S(2)}, u32[]{:S(2)}) collective-permute-start(bf16[20,128]{1,0:T(8,128)(2,1)S(1)} %get-tuple-element.15), channel_id=1, source_target_pairs={{0,3},{1,1},{2,19},{3,17},{16,0},{17,2},{18,16},{19,18},{4,7},{5,5... | collective-permute-start | bytes 15368 | tf_op jit(solution)/shard_map/ppermute | solution.py:235
  156.6 2.1 %collective-permute-start.3 = (bf16[20,128]{1,0:T(8,128)(2,1)S(1)}, bf16[20,128]{1,0:T(8,128)(2,1)S(1)}, u32[]{:S(2)}, u32[]{:S(2)}) collective-permute-start(bf16[20,128]{1,0:T(8,128)(2,1)S(1)} %get-tuple-element.14), channel_id=1, source_target_pairs={{0,0},{1,2},{2,16},{3,18},{16,1},{17,3},{18,17},{19,19},{4,4},{5,6... | collective-permute-start | bytes 15368 | tf_op jit(solution)/shard_map/ppermute | solution.py:235
  158.6 5.6 %collective-permute-start.4 = (bf16[20,128]{1,0:T(8,128)(2,1)S(1)}, bf16[20,128]{1,0:T(8,128)(2,1)S(1)}, u32[]{:S(2)}, u32[]{:S(2)}) collective-permute-start(bf16[20,128]{1,0:T(8,128)(2,1)S(1)} %get-tuple-element.17), channel_id=1, source_target_pairs={{0,1},{1,3},{2,17},{3,19},{16,2},{17,0},{18,18},{19,16},{4,5},{5,7... | collective-permute-start | bytes 15368 | tf_op jit(solution)/shard_map/ppermute | solution.py:235
  164.2 1.9 %collective-permute-start.5 = (bf16[20,128]{1,0:T(8,128)(2,1)S(1)}, bf16[20,128]{1,0:T(8,128)(2,1)S(1)}, u32[]{:S(2)}, u32[]{:S(2)}) collective-permute-start(bf16[20,128]{1,0:T(8,128)(2,1)S(1)} %get-tuple-element.16), channel_id=1, source_target_pairs={{0,2},{1,0},{2,18},{3,16},{16,3},{17,1},{18,19},{19,17},{4,6},{5,4... | collective-permute-start | bytes 15368 | tf_op jit(solution)/shard_map/ppermute | solution.py:235
  168.0 2.4 %collective-permute-done.5 = bf16[20,128]{1,0:T(8,128)(2,1)S(1)} collective-permute-done((bf16[20,128]{1,0:T(8,128)(2,1)S(1)}, bf16[20,128]{1,0:T(8,128)(2,1)S(1)}, u32[]{:S(2)}, u32[]{:S(2)}) %collective-permute-start.5) | collective-permute-done | bytes 5152 | tf_op jit(solution)/shard_map/ppermute | solution.py:235
  (45 shorter events, 14.4 us)
Async XLA Ops:
  0.6 39.9 %copy-start.4 = (s32[52,8192]{1,0:T(8,128)S(1)}, s32[52,8192]{1,0:T(8,128)}, u32[]{:S(2)}) copy-start(s32[52,8192]{1,0:T(8,128)} %codes.1) | copy-start | bytes 5111812
  0.6 1.4 copy-start.5
  2.0 0.9 copy-start.6
  2.9 37.6 %copy-start.9 = (s32[1,52,64]{2,0,1:T(1,128)S(1)}, s32[1,52,64]{2,0,1:T(1,128)}, u32[]{:S(2)}) copy-start(s32[1,52,64]{2,0,1:T(1,128)} %param.10) | copy-start | bytes 39940
  2.9 37.6 %copy-start.7 = (s32[52,64]{1,0:T(8,128)S(1)}, s32[52,64]{1,0:T(8,128)}, u32[]{:S(2)}) copy-start(s32[52,64]{1,0:T(8,128)} %index.1) | copy-start | bytes 39940
  3.2 7.4 %collective-permute-start = (f32[4,20,512]{2,1,0:T(8,128)S(1)}, f32[4,20,512]{2,1,0:T(8,128)S(1)}, u32[]{:S(2)}, u32[]{:S(2)}) collective-permute-start(f32[4,20,512]{2,1,0:T(8,128)S(1)} %shard_map.77), channel_id=1, source_target_pairs={{0,4},{4,0},{8,12},{12,8},{1,5},{5,1},{9,13},{13,9},{2,6},{6,2},{1... | collective-permute-start | bytes 491528 | tf_op jit(solution)/shard_map/ppermute | solution.py:172
  10.6 11.5 %collective-permute-start.1 = (f32[4,20,512]{2,1,0:T(8,128)S(1)}, f32[4,20,512]{2,1,0:T(8,128)S(1)}, u32[]{:S(2)}, u32[]{:S(2)}) collective-permute-start(f32[4,20,512]{2,1,0:T(8,128)S(1)} %multiply_add_fusion), channel_id=1, source_target_pairs={{0,8},{4,12},{8,0},{12,4},{1,9},{5,13},{9,1},{13,5},{2,10},{6,14},... | collective-permute-start | bytes 491528 | tf_op jit(solution)/shard_map/ppermute | solution.py:172
  22.8 29.8 %all-to-all-start = ((bf16[4,20,512]{2,1,0:T(8,128)(2,1)}), bf16[4,20,512]{2,1,0:T(8,128)(2,1)S(1)}, u32[]{:S(2)}, u32[]{:S(2)}) async-start(bf16[4,20,512]{2,1,0:T(8,128)(2,1)} %add_convert_fusion), calls=%async_computation | async-start | bytes 196608 | tf_op jit(solution)/shard_map/all_to_all | solution.py:196
  52.6 19.9 %all-to-all-start.2 = ((bf16[16,56,512]{2,1,0:T(8,128)(2,1)}), bf16[16,56,512]{2,1,0:T(8,128)(2,1)S(1)}, u32[]{:S(2)}, u32[]{:S(2)}) async-start(bf16[16,56,512]{2,1,0:T(8,128)(2,1)} %shard_map.78), calls=%async_computation.2 | async-start | bytes 1835008 | tf_op jit(solution)/shard_map/all_to_all | solution.py:186
  59.4 25.6 %copy-start.8 = (f32[16]{0:T(128)S(1)}, f32[16]{0:T(128)}, u32[]{:S(2)}) copy-start(f32[16]{0:T(128)} %refs_2_.1) | copy-start | bytes 196
  73.7 22.4 %all-to-all-start.1 = ((bf16[16,80,512]{2,1,0:T(8,128)(2,1)}), bf16[16,80,512]{2,1,0:T(8,128)(2,1)S(1)}, u32[]{:S(2)}, u32[]{:S(2)}) async-start(bf16[16,80,512]{2,1,0:T(8,128)(2,1)} %broadcast_in_dim.18), calls=%async_computation.1 | async-start | bytes 2621440 | tf_op jit(solution)/shard_map/all_to_all | solution.py:198
  78.5 6.4 %collective-permute-start.2 = (bf16[16,56,512]{2,1,0:T(8,128)(2,1)S(1)}, bf16[16,56,512]{2,1,0:T(8,128)(2,1)S(1)}, u32[]{:S(2)}, u32[]{:S(2)}) collective-permute-start(bf16[16,56,512]{2,1,0:T(8,128)(2,1)S(1)} %all-to-all-done.2.refs_0_), channel_id=1, source_target_pairs={{0,16},{16,0},{1,17},{17,1},{2,18},{18,2},{3,19},{19,3},{4,20},{20... | collective-permute-start | bytes 2752520 | tf_op jit(solution)/shard_map/ppermute | solution.py:172
  89.1 1.3 copy-start
  90.4 1.3 copy-start.2
  96.1 1.6 copy-start.1
  97.7 1.6 copy-start.3
  120.2 26.0 %all-to-all-start.4 = ((bf16[4,100,512]{2,1,0:T(8,128)(2,1)}), bf16[4,100,512]{2,1,0:T(8,128)(2,1)S(1)}, u32[]{:S(2)}, u32[]{:S(2)}) async-start(bf16[4,100,512]{2,1,0:T(8,128)(2,1)} %shard_map.81), calls=%async_computation.4 | async-start | bytes 851968 | tf_op jit(solution)/shard_map/all_to_all | solution.py:217
  147.2 18.9 %all-to-all-start.5 = ((f32[32,1,20]{2,1,0:T(1,128)}), f32[32,1,20]{2,1,0:T(1,128)S(1)}, u32[]{:S(2)}, u32[]{:S(2)}) async-start(f32[32,1,20]{2,1,0:T(1,128)} %bitcast.16), calls=%async_computation.5 | async-start | bytes 32768 | tf_op jit(solution)/shard_map/all_to_all | solution.py:225
  154.4 13.6 %collective-permute-start.6 = (bf16[20,128]{1,0:T(8,128)(2,1)S(1)}, bf16[20,128]{1,0:T(8,128)(2,1)S(1)}, u32[]{:S(2)}, u32[]{:S(2)}) collective-permute-start(bf16[20,128]{1,0:T(8,128)(2,1)S(1)} %get-tuple-element.15), channel_id=1, source_target_pairs={{0,3},{1,1},{2,19},{3,17},{16,0},{17,2},{18,16},{19,18},{4,7},{5,5... | collective-permute-start | bytes 15368 | tf_op jit(solution)/shard_map/ppermute | solution.py:235
  156.6 11.4 %collective-permute-start.3 = (bf16[20,128]{1,0:T(8,128)(2,1)S(1)}, bf16[20,128]{1,0:T(8,128)(2,1)S(1)}, u32[]{:S(2)}, u32[]{:S(2)}) collective-permute-start(bf16[20,128]{1,0:T(8,128)(2,1)S(1)} %get-tuple-element.14), channel_id=1, source_target_pairs={{0,0},{1,2},{2,16},{3,18},{16,1},{17,3},{18,17},{19,19},{4,4},{5,6... | collective-permute-start | bytes 15368 | tf_op jit(solution)/shard_map/ppermute | solution.py:235
  158.6 9.3 %collective-permute-start.4 = (bf16[20,128]{1,0:T(8,128)(2,1)S(1)}, bf16[20,128]{1,0:T(8,128)(2,1)S(1)}, u32[]{:S(2)}, u32[]{:S(2)}) collective-permute-start(bf16[20,128]{1,0:T(8,128)(2,1)S(1)} %get-tuple-element.17), channel_id=1, source_target_pairs={{0,1},{1,3},{2,17},{3,19},{16,2},{17,0},{18,18},{19,16},{4,5},{5,7... | collective-permute-start | bytes 15368 | tf_op jit(solution)/shard_map/ppermute | solution.py:235
  164.2 6.2 %collective-permute-start.5 = (bf16[20,128]{1,0:T(8,128)(2,1)S(1)}, bf16[20,128]{1,0:T(8,128)(2,1)S(1)}, u32[]{:S(2)}, u32[]{:S(2)}) collective-permute-start(bf16[20,128]{1,0:T(8,128)(2,1)S(1)} %get-tuple-element.16), channel_id=1, source_target_pairs={{0,2},{1,0},{2,18},{3,16},{16,3},{17,1},{18,19},{19,17},{4,6},{5,4... | collective-permute-start | bytes 15368 | tf_op jit(solution)/shard_map/ppermute | solution.py:235

commit v3 on v2

--- a/solution.py
+++ b/solution.py
@@ -66,19 +66,25 @@
 def pack_kernel(codes, index, bits, out, meta, turned, block):
     rows = codes.shape[0]
     groups = index.shape[1]
-    meta[...] = jnp.zeros_like(meta)
-    meta[0:rows, 0:groups] = index[...].astype(F32)
-    meta[0:rows, groups : 2 * groups] = bits[...].astype(F32)
-    turned[...] = meta[...].T
-    block[...] = jnp.zeros_like(block)
-    for p in range(16):
-        xd, yd = divmod(p, 4)
+    xd = pl.program_id(0)
+
+    @pl.when(xd == 0)
+    def _():
+        meta[...] = jnp.zeros_like(meta)
+        meta[0:rows, 0:groups] = index[...].astype(F32)
+        meta[0:rows, groups : 2 * groups] = bits[...].astype(F32)
+        turned[...] = meta[...].T
+        block[...] = jnp.zeros_like(block)
+
+    index_rows = turned[pl.ds(pl.multiple_of(16 * xd, 16), 16), :]
+    bits_rows = turned[pl.ds(pl.multiple_of(groups + 16 * xd, 16), 16), :]
+    for yd in range(4):
         for k in range(4):
-            g = 16 * xd + 4 * k + yd
+            g = 4 * k + yd
             block[0:rows, k * LANES : (k + 1) * LANES] = codes[:, g * LANES : (g + 1) * LANES].astype(F32)
-            block[rows + k : rows + k + 1, 0:LANES] = turned[g : g + 1, :]
-            block[rows + k : rows + k + 1, LANES : 2 * LANES] = turned[groups + g : groups + g + 1, :]
-        out[p] = block[...].astype(BF16)
+            block[rows + k : rows + k + 1, 0:LANES] = index_rows[g : g + 1, :]
+            block[rows + k : rows + k + 1, LANES : 2 * LANES] = bits_rows[g : g + 1, :]
+        out[yd] = block[...].astype(BF16)
 
 
 def weight_kernel(rows, own, other, table, place, base, diff, meta, base_acc, diff_acc):
@@ -155,17 +161,50 @@
         out[zd] = send[...].astype(BF16)
 
 
-def far_kernel(parts, base, score, total):
+def far_kernel(parts, out, total, turn, block):
     acc = parts[0].astype(F32)
     for k in range(1, 4):
         acc = acc + parts[k].astype(F32)
     total[...] = acc
-    rows = score.shape[0]
+    rows = parts.shape[1] * 4 // 5
     toks = rows // 4
+    gap = total[0:rows, :]
+    turn[rows:, :] = jnp.zeros((LANES - rows, LANES), F32)
+    turn[0:rows, :] = jnp.broadcast_to(jnp.sum(gap * gap, axis=1, keepdims=True), (rows, LANES))
+    score = turn[...].T[0:1, :]
+    high = score.astype(BF16).astype(F32)
+    middle = (score - high).astype(BF16).astype(F32)
+    low = score - high - middle
+    block[toks : toks + 1, :] = high
+    block[toks + 1 : toks + 2, :] = middle
+    block[toks + 2 : toks + 3, :] = low
+    block[toks + 3 : toks + 4, :] = jnp.zeros((1, LANES), F32)
     for yd in range(4):
-        base[yd] = total[rows : rows + toks, yd * LANES : (yd + 1) * LANES].astype(BF16)
-    gap = total[0:rows, :]
-    score[...] = jnp.broadcast_to(jnp.sum(gap * gap, axis=1, keepdims=True), score.shape)
+        block[0:toks, :] = total[rows : rows + toks, yd * LANES : (yd + 1) * LANES]
+        wire = block[...].astype(BF16)
+        for xd in range(4):
+            for cd in range(2):
+                out[(xd * 4 + yd) * 2 + cd] = wire
+
+
+def last_kernel(parts, place, base, score, held):
+    toks = parts.shape[1] - 4
+    x, c, y = place[0], place[2], place[3]
+    lane = lax.broadcasted_iota(jnp.int32, (LANES, LANES), 0)
+    slot = lax.broadcasted_iota(jnp.int32, (LANES, LANES), 1)
+    final = jnp.zeros((8, LANES), F32)
+    for cs in range(2):
+        total = jnp.zeros((8, LANES), F32)
+        for k in range(16):
+            total = total + parts[2 * k + cs, toks - 4 : toks + 4, :].astype(F32)
+        row = total[4:5, :] + total[5:6, :] + total[6:7, :]
+        pick = jnp.where((lane == y * toks + slot - cs * toks) & (slot >= cs * toks) & (slot < (cs + 1) * toks), 1.0, 0.0)
+        final = final + jnp.dot(jnp.broadcast_to(row, (8, LANES)), pick, precision=lax.Precision.HIGHEST, preferred_element_type=F32)
+        for i in range(2):
+            piece = parts[(x * 4 + 2 * c + i) * 2 + cs]
+            held[cs * toks : (cs + 1) * toks, i * LANES : (i + 1) * LANES] = piece[0:toks, :].astype(F32)
+    base[...] = held[...].astype(BF16)
+    score[...] = final[0:1, 0 : 2 * toks] * (1.0 / SCORE_DIVISOR)
 
 
 def trade(value, axis, bit, size=4):
@@ -178,10 +217,18 @@
   store, width = weight_codes.shape
   part = width // 16
   padded = store + 4
-  wire = call(
-      pack_kernel, jax.ShapeDtypeStruct((16, padded, part), BF16), [VMEM] * 3,
-      [pltpu.VMEM((128, 128), F32), pltpu.VMEM((128, 128), F32), pltpu.VMEM((padded, part), F32)],
-      0, store * width * 6, 8,
+  whole = lambda i: (0, 0)
+  wire = pl.pallas_call(
+      pack_kernel, out_shape=jax.ShapeDtypeStruct((16, padded, part), BF16), grid=(4,),
+      in_specs=[
+          pl.BlockSpec((store, width // 4), lambda i: (0, i)),
+          pl.BlockSpec(scale_index.shape, whole),
+          pl.BlockSpec(scale_index.shape, whole),
+      ],
+      out_specs=pl.BlockSpec((4, padded, part), lambda i: (i, 0, 0)),
+      scratch_shapes=[pltpu.VMEM((128, 128), F32), pltpu.VMEM((128, 128), F32), pltpu.VMEM((padded, part), F32)],
+      name="pack", compiler_params=pltpu.CompilerParams(vmem_limit_bytes=60 << 20),
+      cost_estimate=pl.CostEstimate(flops=0, bytes_accessed=store * width * 6, transcendentals=0),
   )(weight_codes, scale_index, bit_widths.reshape(store, -1))
   home = lax.all_to_all(wire, ("x", "y"), 0, 0, tiled=True)
   other = trade(home, "c", 1, 2)
@@ -201,12 +248,12 @@
       lambda *refs: weight_kernel(store, *refs),
       [jax.ShapeDtypeStruct((16 * LANES, part), BF16)] * 2, [VMEM, VMEM, SMEM, SMEM],
       [pltpu.VMEM((128, 128), F32)] + [pltpu.VMEM((16 * LANES, part), F32)] * 2,
-      feat * part * 20, feat * part * 6, 24,
+      feat * part * 20, feat * part * 6, 16,
   )(home, other, scale_table, place)
   sums = call(
       matmul_kernel, jax.ShapeDtypeStruct((4, 8 * toks, part), BF16),
       [VMEM] * 3, [pltpu.VMEM((16 * toks, 16 * LANES), BF16)],
-      4 * 16 * toks * feat * part, feat * part * 4 + 16 * toks * feat * 2, 20,
+      4 * 16 * toks * feat * part, feat * part * 4 + 16 * toks * feat * 2, 10,
   )(tokens, base_w, diff_w)
   near = lax.all_to_all(sums, "zl", 0, 0, tiled=True)
   wave = call(
@@ -215,30 +262,17 @@
       32 * toks * part, 64 * toks * part, 8,
   )(near)
   far = lax.all_to_all(wave, "zh", 0, 0, tiled=True)
-  pieces, score = call(
-      far_kernel,
-      [jax.ShapeDtypeStruct((4, toks, LANES), BF16), jax.ShapeDtypeStruct((4 * toks, LANES), F32)],
-      [VMEM], [pltpu.VMEM((5 * toks, part), F32)], 32 * toks * part, 40 * toks * part, 8,
+  wire = call(
+      far_kernel, jax.ShapeDtypeStruct((32, toks + 4, LANES), BF16), [VMEM],
+      [pltpu.VMEM((5 * toks, part), F32), pltpu.VMEM((LANES, LANES), F32), pltpu.VMEM((toks + 4, LANES), F32)],
+      32 * toks * part, 40 * toks * part, 4,
   )(far)
-  mine = score[:, 0].reshape(1, 4, 1, 1, toks)
-  spread = jnp.broadcast_to(mine, (4, 4, 2, 1, toks)).reshape(32, 1, toks)
-  everyone = lax.all_to_all(spread, ("x", "y", "c"), 0, 0, tiled=True)
-  scores = jnp.sum(everyone.reshape(16, 2 * toks), axis=0)[None] / SCORE_DIVISOR
-  y, c = lax.axis_index("y"), lax.axis_index("c")
-  got = []
-  for r in range(4):
-      pairs = []
-      for cs in range(2):
-          for ys in range(4):
-              pairs.append((cs * 4 + ys, (ys // 2) * 4 + (2 * (ys % 2) + cs + r) % 4))
-      piece = lax.dynamic_index_in_dim(pieces, lax.rem(2 * lax.rem(y, 2) + c + r, 4), 0, False)
-      got.append(lax.ppermute(piece, ("c", "y"), pairs))
-  got = jnp.stack(got)
-  rows = []
-  for cs in range(2):
-      rows.append(jnp.concatenate(
-          [lax.dynamic_index_in_dim(got, lax.rem(y - 2 * i - cs + 4, 4), 0, False) for i in range(2)], axis=1))
-  base = jnp.concatenate(rows, axis=0)
+  everyone = lax.all_to_all(wire, ("x", "y", "c"), 0, 0, tiled=True)
+  base, scores = call(
+      last_kernel,
+      [jax.ShapeDtypeStruct((2 * toks, 2 * LANES), BF16), jax.ShapeDtypeStruct((1, 2 * toks), F32)],
+      [VMEM, SMEM], [pltpu.VMEM((2 * toks, 2 * LANES), F32)], 1 << 20, 1 << 18, 4,
+  )(everyone, place)
   return base, scores
 
 

time: 173 us -> 166 us (0.960)
  blocking collectives: 18.4 us -> 63.3 us
  waiting for transfers between devices: 63.3 us -> 35.3 us
  starting transfers between devices: 66.6 us -> 44.3 us
  Pallas kernels: 8.34 us -> 11.4 us
  other arithmetic: 2.62 us -> 0.77 us
    all_to_all x0 -> x2, blocking collectives: none -> 44.8 us  [the longest x1 26.8 us: local(): far = lax.all_to_all(wave, 'zh', 0, 0, tiled=True)]
    all_to_all x2 -> x0, waiting for transfers between devices: 22.5 us -> none  [the longest x1 22.5 us: local(): far = lax.all_to_all(wave, 'zh', 0, 0, tiled=True)]
    ppermute x4 -> x0, starting transfers between devices: 11.7 us -> none  [local(): got.append(lax.ppermute(piece, ('c', 'y'), pairs))]
    all_to_all x2 -> x0, starting transfers between devices: 10.6 us -> none  [the longest x1 7.15 us: local(): everyone = lax.all_to_all(spread, ('x', 'y', 'c'), 0, 0, tiled=True)]
    pallas_call x2 -> x3, Pallas kernels: 1.42 us -> 5.25 us  [the longest x1 3.73 us: local(): pl.pallas_call(pack_kernel, out_shape=jax.ShapeDtypeStruct((16, padded, p...]
    all_to_all x1, waiting for transfers between devices: 10.7 us -> 7.72 us  [local(): value = lax.all_to_all(value.astype(BF16), 'zh', 0, 0, tiled=True)]
    ppermute x4 -> x0, waiting for transfers between devices: 2.39 us -> none  [local(): got.append(lax.ppermute(piece, ('c', 'y'), pairs))]
    unnamed x21 -> x17, local copies, waits for them, and re-layouts: 8.06 us -> 8.56 us
  transfers between devices with their start and end apart: 12 -> 6, of which waited for: 8 -> 6; matrix products, arithmetic and copies ran while one was open for 1% -> 0% of each run, Pallas kernels for 3% -> 5%
where the time goes in v3:
time: 166 us
  blocking collectives  63.3 us (38%)
  starting transfers between devices  44.3 us (27%)
  waiting for transfers between devices  35.3 us (21%)
  Pallas kernels  11.4 us (7%)
  local copies, waits for them, and re-layouts  9.81 us (6%)
    all_to_all x1, blocking collectives, local(): far = lax.all_to_all(wave, 'zh', 0, 0, tiled=True)  26.8 us
    all_to_all x1, blocking collectives, local(): near = lax.all_to_all(sums, 'zl', 0, 0, tiled=True)  18.5 us
    all_to_all x1, blocking collectives, local(): everyone = lax.all_to_all(wire, ('x', 'y', 'c'), 0, 0, tiled=True)  18 us
    all_to_all x1, starting transfers between devices, local(): value = lax.all_to_all(value.astype(BF16), 'zh', 0, 0, tiled=True)  17.7 us
    ppermute x3, starting transfers between devices, trade(): return lax.ppermute(value, axis, [(i, i ^ bit) for i in range(size)])  15.1 us
    all_to_all x1, waiting for transfers between devices, local(): home = lax.all_to_all(wire, ('x', 'y'), 0, 0, tiled=True)  13.1 us
    ppermute x3, waiting for transfers between devices, trade(): return lax.ppermute(value, axis, [(i, i ^ bit) for i in range(size)])  10.2 us
    unnamed x17, local copies, waits for them, and re-layouts  8.56 us
  transfers between devices with their start and end apart: 6, of which 6 were waited for; matrix products, arithmetic and copies ran while one was open for 0% of the time, Pallas kernels for 5%

profile of v3, /device:TPU:1, one launch (start us, length us, event | category | flops | bytes accessed | tf_op | source)
XLA Modules:
  0.0 165.7 jit_solution(9315225964533141060)
XLA Ops:
  3.0 4.4 %collective-permute-start = (f32[4,20,512]{2,1,0:T(8,128)S(1)}, f32[4,20,512]{2,1,0:T(8,128)S(1)}, u32[]{:S(2)}, u32[]{:S(2)}) collective-permute-start(f32[4,20,512]{2,1,0:T(8,128)S(1)} %shard_map.77), channel_id=1, source_target_pairs={{0,4},{4,0},{8,12},{12,8},{1,5},{5,1},{9,13},{13,9},{2,6},{6,2},{1... | collective-permute-start | bytes 491528 | tf_op jit(solution)/shard_map/ppermute | solution.py:211
  7.4 3.0 %collective-permute-done = f32[4,20,512]{2,1,0:T(8,128)S(1)} collective-permute-done((f32[4,20,512]{2,1,0:T(8,128)S(1)}, f32[4,20,512]{2,1,0:T(8,128)S(1)}, u32[]{:S(2)}, u32[]{:S(2)}) %collective-permute-start) | collective-permute-done | bytes 163872 | tf_op jit(solution)/shard_map/ppermute | solution.py:211
  10.5 6.3 %collective-permute-start.1 = (f32[4,20,512]{2,1,0:T(8,128)S(1)}, f32[4,20,512]{2,1,0:T(8,128)S(1)}, u32[]{:S(2)}, u32[]{:S(2)}) collective-permute-start(f32[4,20,512]{2,1,0:T(8,128)S(1)} %multiply_add_fusion), channel_id=1, source_target_pairs={{0,8},{4,12},{8,0},{12,4},{1,9},{5,13},{9,1},{13,5},{2,10},{6,14},... | collective-permute-start | bytes 491528 | tf_op jit(solution)/shard_map/ppermute | solution.py:211
  16.8 5.1 %collective-permute-done.1 = f32[4,20,512]{2,1,0:T(8,128)S(1)} collective-permute-done((f32[4,20,512]{2,1,0:T(8,128)S(1)}, f32[4,20,512]{2,1,0:T(8,128)S(1)}, u32[]{:S(2)}, u32[]{:S(2)}) %collective-permute-start.1) | collective-permute-done | bytes 163872 | tf_op jit(solution)/shard_map/ppermute | solution.py:211
  22.6 17.7 %all-to-all-start = ((bf16[4,20,512]{2,1,0:T(8,128)(2,1)}), bf16[4,20,512]{2,1,0:T(8,128)(2,1)S(1)}, u32[]{:S(2)}, u32[]{:S(2)}) async-start(bf16[4,20,512]{2,1,0:T(8,128)(2,1)} %add_convert_fusion), calls=%async_computation | async-start | bytes 196608 | tf_op jit(solution)/shard_map/all_to_all | solution.py:243
  41.0 3.7 %pack.1 = bf16[16,56,512]{2,1,0:T(8,128)(2,1)} custom-call(s32[52,8192]{1,0:T(8,128)} %codes.1, s32[52,64]{1,0:T(8,128)} %index.1, s32[52,64]{1,0:T(8,128)} %bitcast.7), custom_call_target="tpu_custom_call" | custom-call | bytes 2555904 | tf_op jit(solution)/shard_map/pack/pallas_call | solution.py:221
  44.7 7.7 %all-to-all-done = bf16[4,20,512]{2,1,0:T(8,128)(2,1)S(1)} async-done(((bf16[4,20,512]{2,1,0:T(8,128)(2,1)}), bf16[4,20,512]{2,1,0:T(8,128)(2,1)S(1)}, u32[]{:S(2)}, u32[]{:S(2)}) %all-to-all-start) | async-done | bytes 81952 | tf_op jit(solution)/shard_map/all_to_all | solution.py:243
  52.4 6.7 %all-to-all-start.2 = ((bf16[16,56,512]{2,1,0:T(8,128)(2,1)}), bf16[16,56,512]{2,1,0:T(8,128)(2,1)S(1)}, u32[]{:S(2)}, u32[]{:S(2)}) async-start(bf16[16,56,512]{2,1,0:T(8,128)(2,1)} %pack.1), calls=%async_computation.2 | async-start | bytes 1835008 | tf_op jit(solution)/shard_map/all_to_all | solution.py:233
  59.2 13.1 %all-to-all-done.2.refs_0_ = bf16[16,56,512]{2,1,0:T(8,128)(2,1)S(1)} async-done(((bf16[16,56,512]{2,1,0:T(8,128)(2,1)}), bf16[16,56,512]{2,1,0:T(8,128)(2,1)S(1)}, u32[]{:S(2)}, u32[]{:S(2)}) %all-to-all-start.2) | async-done | bytes 917536 | tf_op jit(solution)/shard_map/all_to_all | solution.py:233
  72.3 1.2 broadcast_in_dim.8
  73.6 4.8 %all-to-all-start.1 = ((bf16[16,80,512]{2,1,0:T(8,128)(2,1)}), bf16[16,80,512]{2,1,0:T(8,128)(2,1)S(1)}, u32[]{:S(2)}, u32[]{:S(2)}) async-start(bf16[16,80,512]{2,1,0:T(8,128)(2,1)} %broadcast_in_dim.8), calls=%async_computation.1 | async-start | bytes 2621440 | tf_op jit(solution)/shard_map/all_to_all | solution.py:245
  78.3 4.4 %collective-permute-start.2 = (bf16[16,56,512]{2,1,0:T(8,128)(2,1)S(1)}, bf16[16,56,512]{2,1,0:T(8,128)(2,1)S(1)}, u32[]{:S(2)}, u32[]{:S(2)}) collective-permute-start(bf16[16,56,512]{2,1,0:T(8,128)(2,1)S(1)} %all-to-all-done.2.refs_0_), channel_id=1, source_target_pairs={{0,16},{16,0},{1,17},{17,1},{2,18},{18,2},{3,19},{19,3},{4,20},{20... | collective-permute-start | bytes 2752520 | tf_op jit(solution)/shard_map/ppermute | solution.py:211
  82.8 2.0 %collective-permute-done.2.refs_1_ = bf16[16,56,512]{2,1,0:T(8,128)(2,1)S(1)} collective-permute-done((bf16[16,56,512]{2,1,0:T(8,128)(2,1)S(1)}, bf16[16,56,512]{2,1,0:T(8,128)(2,1)S(1)}, u32[]{:S(2)}, u32[]{:S(2)}) %collective-permute-start.2) | collective-permute-done | bytes 917536 | tf_op jit(solution)/shard_map/ppermute | solution.py:211
  84.8 4.2 %shard_map.78 = (bf16[2048,512]{1,0:T(8,128)(2,1)S(1)}, bf16[2048,512]{1,0:T(8,128)(2,1)S(1)}) custom-call(bf16[16,56,512]{2,1,0:T(8,128)(2,1)S(1)} %all-to-all-done.2.refs_0_, bf16[16,56,512]{2,1,0:T(8,128)(2,1)S(1)} %collective-permute-done.2.refs_1_, f32[16]{0:T(128)S(1)} %copy-done.6, s32[4]{0:T(128)S(1)} %pad_add_fusion.refs_3_.place), custom_call_target="tpu_custom_call" | custom-call | flops 17039360 | bytes 5111808 | tf_op jit(solution)/shard_map/pallas_call | solution.py:247
  89.0 1.3 copy-done
  90.3 1.3 copy-done.2
  91.6 4.3 %all-to-all-done.1.tokens = bf16[16,80,512]{2,1,0:T(8,128)(2,1)S(1)} async-done(((bf16[16,80,512]{2,1,0:T(8,128)(2,1)}), bf16[16,80,512]{2,1,0:T(8,128)(2,1)S(1)}, u32[]{:S(2)}, u32[]{:S(2)}) %all-to-all-start.1) | async-done | bytes 1310752 | tf_op jit(solution)/shard_map/all_to_all | solution.py:245
  95.9 1.6 copy-done.1
  97.5 1.6 copy-done.3
  99.1 1.6 shard_map.79
  100.7 18.5 %all_to_all.30.parts = bf16[4,160,512]{2,1,0:T(8,128)(2,1)S(1)} all-to-all(bf16[4,160,512]{2,1,0:T(8,128)(2,1)S(1)} %shard_map.79), channel_id=1, replica_groups=mesh['x'=4,'zh'=4,'c'=2,'zl'=4,'y'=4] {'zl'}, dimensions={0} | all-to-all | bytes 1310720 | tf_op jit(solution)/shard_map/all_to_all | solution.py:258
  119.4 26.8 %all_to_all.31.parts = bf16[4,100,512]{2,1,0:T(8,128)(2,1)S(1)} all-to-all(bf16[4,100,512]{2,1,0:T(8,128)(2,1)S(1)} %shard_map.80), channel_id=1, replica_groups=mesh['x'=4,'zh'=4,'c'=2,'zl'=4,'y'=4] {'zh'}, dimensions={0} | all-to-all | bytes 819200 | tf_op jit(solution)/shard_map/all_to_all | solution.py:264
  146.4 18.0 %all_to_all.32.parts = bf16[32,24,128]{2,1,0:T(8,128)(2,1)S(1)} all-to-all(bf16[32,24,128]{2,1,0:T(8,128)(2,1)S(1)} %shard_map.81), channel_id=1, replica_groups=mesh['x'=4,'zh'=4,'c'=2,'zl'=4,'y'=4] {'x','y','c'}, dimensions={0} | all-to-all | bytes 393216 | tf_op jit(solution)/shard_map/all_to_all | solution.py:270
  164.4 1.3 shard_map.82
  (20 shorter events, 4.1 us)
Async XLA Ops:
  0.6 1.2 copy-start.4
  1.9 0.9 copy-start.5
  2.7 37.6 %copy-start.7 = (s32[1,52,64]{2,0,1:T(1,128)S(1)}, s32[1,52,64]{2,0,1:T(1,128)}, u32[]{:S(2)}) copy-start(s32[1,52,64]{2,0,1:T(1,128)} %param.10) | copy-start | bytes 39940
  3.0 7.4 %collective-permute-start = (f32[4,20,512]{2,1,0:T(8,128)S(1)}, f32[4,20,512]{2,1,0:T(8,128)S(1)}, u32[]{:S(2)}, u32[]{:S(2)}) collective-permute-start(f32[4,20,512]{2,1,0:T(8,128)S(1)} %shard_map.77), channel_id=1, source_target_pairs={{0,4},{4,0},{8,12},{12,8},{1,5},{5,1},{9,13},{13,9},{2,6},{6,2},{1... | collective-permute-start | bytes 491528 | tf_op jit(solution)/shard_map/ppermute | solution.py:211
  10.5 11.5 %collective-permute-start.1 = (f32[4,20,512]{2,1,0:T(8,128)S(1)}, f32[4,20,512]{2,1,0:T(8,128)S(1)}, u32[]{:S(2)}, u32[]{:S(2)}) collective-permute-start(f32[4,20,512]{2,1,0:T(8,128)S(1)} %multiply_add_fusion), channel_id=1, source_target_pairs={{0,8},{4,12},{8,0},{12,4},{1,9},{5,13},{9,1},{13,5},{2,10},{6,14},... | collective-permute-start | bytes 491528 | tf_op jit(solution)/shard_map/ppermute | solution.py:211
  22.6 29.8 %all-to-all-start = ((bf16[4,20,512]{2,1,0:T(8,128)(2,1)}), bf16[4,20,512]{2,1,0:T(8,128)(2,1)S(1)}, u32[]{:S(2)}, u32[]{:S(2)}) async-start(bf16[4,20,512]{2,1,0:T(8,128)(2,1)} %add_convert_fusion), calls=%async_computation | async-start | bytes 196608 | tf_op jit(solution)/shard_map/all_to_all | solution.py:243
  52.4 19.9 %all-to-all-start.2 = ((bf16[16,56,512]{2,1,0:T(8,128)(2,1)}), bf16[16,56,512]{2,1,0:T(8,128)(2,1)S(1)}, u32[]{:S(2)}, u32[]{:S(2)}) async-start(bf16[16,56,512]{2,1,0:T(8,128)(2,1)} %pack.1), calls=%async_computation.2 | async-start | bytes 1835008 | tf_op jit(solution)/shard_map/all_to_all | solution.py:233
  59.2 25.6 %copy-start.6 = (f32[16]{0:T(128)S(1)}, f32[16]{0:T(128)}, u32[]{:S(2)}) copy-start(f32[16]{0:T(128)} %refs_2_.1) | copy-start | bytes 196
  73.6 22.4 %all-to-all-start.1 = ((bf16[16,80,512]{2,1,0:T(8,128)(2,1)}), bf16[16,80,512]{2,1,0:T(8,128)(2,1)S(1)}, u32[]{:S(2)}, u32[]{:S(2)}) async-start(bf16[16,80,512]{2,1,0:T(8,128)(2,1)} %broadcast_in_dim.8), calls=%async_computation.1 | async-start | bytes 2621440 | tf_op jit(solution)/shard_map/all_to_all | solution.py:245
  78.3 6.4 %collective-permute-start.2 = (bf16[16,56,512]{2,1,0:T(8,128)(2,1)S(1)}, bf16[16,56,512]{2,1,0:T(8,128)(2,1)S(1)}, u32[]{:S(2)}, u32[]{:S(2)}) collective-permute-start(bf16[16,56,512]{2,1,0:T(8,128)(2,1)S(1)} %all-to-all-done.2.refs_0_), channel_id=1, source_target_pairs={{0,16},{16,0},{1,17},{17,1},{2,18},{18,2},{3,19},{19,3},{4,20},{20... | collective-permute-start | bytes 2752520 | tf_op jit(solution)/shard_map/ppermute | solution.py:211
  88.9 1.3 copy-start
  90.3 1.3 copy-start.2
  95.9 1.6 copy-start.1
  97.5 1.6 copy-start.3

commit v4 on v2

--- a/solution.py
+++ b/solution.py
@@ -60,25 +60,32 @@
     for m in range(16):
         xd, zd = divmod(m, 4)
         piece = jnp.dot(act[:, FIRST[m] : FIRST[m] + 2 * HB], signs[m], preferred_element_type=F32)
-        out[zd, :, xd * LANES : (xd + 1) * LANES] = piece
-
-
-def pack_kernel(codes, index, bits, out, meta, turned, block):
-    rows = codes.shape[0]
+        out[zd, :, xd * LANES : (xd + 1) * LANES] = piece.astype(BF16)
+
+
+def pack_kernel(codes_hbm, index, bits, out, codes, meta, turned, block, sems):
+    rows, width = codes.shape
+    quarter = width // 4
     groups = index.shape[1]
+    copies = []
+    for xd in range(4):
+        cols = pl.ds(xd * quarter, quarter)
+        copies.append(pltpu.make_async_copy(codes_hbm.at[:, cols], codes.at[:, cols], sems.at[xd]))
+        copies[-1].start()
     meta[...] = jnp.zeros_like(meta)
     meta[0:rows, 0:groups] = index[...].astype(F32)
-    meta[0:rows, groups : 2 * groups] = bits[...].astype(F32)
+    meta[0:rows, groups : 2 * groups] = bits[:, 0, :].astype(F32)
     turned[...] = meta[...].T
     block[...] = jnp.zeros_like(block)
-    for p in range(16):
-        xd, yd = divmod(p, 4)
-        for k in range(4):
-            g = 16 * xd + 4 * k + yd
-            block[0:rows, k * LANES : (k + 1) * LANES] = codes[:, g * LANES : (g + 1) * LANES].astype(F32)
-            block[rows + k : rows + k + 1, 0:LANES] = turned[g : g + 1, :]
-            block[rows + k : rows + k + 1, LANES : 2 * LANES] = turned[groups + g : groups + g + 1, :]
-        out[p] = block[...].astype(BF16)
+    for xd in range(4):
+        copies[xd].wait()
+        for yd in range(4):
+            for k in range(4):
+                g = 16 * xd + 4 * k + yd
+                block[0:rows, k * LANES : (k + 1) * LANES] = codes[:, g * LANES : (g + 1) * LANES].astype(F32)
+                block[rows + k : rows + k + 1, 0:LANES] = turned[g : g + 1, :]
+                block[rows + k : rows + k + 1, LANES : 2 * LANES] = turned[groups + g : groups + g + 1, :]
+            out[xd * 4 + yd] = block[...].astype(BF16)
 
 
 def weight_kernel(rows, own, other, table, place, base, diff, meta, base_acc, diff_acc):
@@ -124,48 +131,88 @@
     diff[...] = diff_acc[...].astype(BF16)
 
 
-def matmul_kernel(tokens, base_w, diff_w, out, left):
+def matmul_kernel(tokens, base_hbm, diff_hbm, out, left, base_w, diff_w, sems):
     rows, wide = tokens.shape[1:]
+    copies = [
+        pltpu.make_async_copy(base_hbm, base_w, sems.at[0]),
+        pltpu.make_async_copy(diff_hbm, diff_w, sems.at[1]),
+    ]
+    for copy in copies:
+        copy.start()
     factor = 1.0 / math.sqrt(HB * 16)
     for xd in range(4):
         s = [tokens[xd * 4 + yd].astype(F32) for yd in range(4)]
         a, b, c, d = s[0] + s[1], s[0] - s[1], s[2] + s[3], s[2] - s[3]
         for j, mixed in enumerate((a + c, b + d, a - c, b - d)):
             left[xd * rows : (xd + 1) * rows, j * wide : (j + 1) * wide] = (mixed * factor).astype(BF16)
+    copies[0].wait()
     base = jnp.dot(left[...], base_w[...], preferred_element_type=F32).astype(BF16)
+    copies[1].wait()
     diff = jnp.dot(left[...], diff_w[...], preferred_element_type=F32).astype(BF16)
     for xd in range(4):
         out[xd, 0:rows, :] = base[xd * rows : (xd + 1) * rows, :]
         out[xd, rows : 2 * rows, :] = diff[xd * rows : (xd + 1) * rows, :]
 
 
-def near_kernel(parts, out, base, send):
-    rows = parts.shape[1] // 2
-    toks = rows // 4
+def unpad_kernel(parts, out):
+    toks = parts.shape[1]
+    for k in range(4):
+        out[k * toks : (k + 1) * toks, :] = parts[k].astype(F32)
+
+
+def spread_kernel(got, value, sign, out):
+    mixed = (got[...] + sign[0] * value[...]).astype(BF16)
+    for k in range(out.shape[0]):
+        out[k] = mixed
+
+
+def near_kernel(parts, out):
     total = parts[0].astype(F32)
     for k in range(1, 4):
         total = total + parts[k].astype(F32)
-    base[...] = total[0:rows, :]
     for zd in range(4):
-        send[0:rows, :] = total[rows:, :]
-        for yd in range(4):
-            send[rows : rows + toks, yd * LANES : (yd + 1) * LANES] = base[
-                yd * toks : (yd + 1) * toks, zd * LANES : (zd + 1) * LANES
-            ]
-        out[zd] = send[...].astype(BF16)
-
-
-def far_kernel(parts, base, score, total):
+        out[zd] = total[:, zd * LANES : (zd + 1) * LANES].astype(BF16)
+
+
+def far_kernel(parts, place, p0, p1, p2, p3, score, total, turn, pieces):
     acc = parts[0].astype(F32)
     for k in range(1, 4):
         acc = acc + parts[k].astype(F32)
     total[...] = acc
-    rows = score.shape[0]
+    rows = parts.shape[1] // 2
     toks = rows // 4
+    gap = total[rows:, :]
+    turn[rows:, :] = jnp.zeros((LANES - rows, LANES), F32)
+    turn[0:rows, :] = jnp.broadcast_to(jnp.sum(gap * gap, axis=1, keepdims=True), (rows, LANES))
+    line = turn[...].T[0:1, :]
+    for k in range(score.shape[0]):
+        score[k] = line
     for yd in range(4):
-        base[yd] = total[rows : rows + toks, yd * LANES : (yd + 1) * LANES].astype(BF16)
-    gap = total[0:rows, :]
-    score[...] = jnp.broadcast_to(jnp.sum(gap * gap, axis=1, keepdims=True), score.shape)
+        pieces[yd] = total[yd * toks : (yd + 1) * toks, :]
+    first = 2 * lax.rem(place[3], 2) + place[2]
+    for r, out in enumerate((p0, p1, p2, p3)):
+        out[...] = pieces[lax.rem(first + r, 4)].astype(BF16)
+
+
+def last_kernel(lines, g0, g1, g2, g3, place, base, score, pieces, held):
+    toks = g0.shape[0]
+    y = place[3]
+    lane = lax.broadcasted_iota(jnp.int32, (LANES, LANES), 0)
+    slot = lax.broadcasted_iota(jnp.int32, (LANES, LANES), 1)
+    for r, got in enumerate((g0, g1, g2, g3)):
+        pieces[r] = got[...].astype(F32)
+    final = jnp.zeros((8, LANES), F32)
+    for cs in range(2):
+        row = jnp.zeros((1, LANES), F32)
+        for k in range(16):
+            for ys in range(4):
+                row = row + lines[(2 * k + cs) * 4 + ys]
+        pick = jnp.where((lane == y * toks + slot - cs * toks) & (slot >= cs * toks) & (slot < (cs + 1) * toks), 1.0, 0.0)
+        final = final + jnp.dot(jnp.broadcast_to(row, (8, LANES)), pick, precision=lax.Precision.HIGHEST, preferred_element_type=F32)
+        for i in range(2):
+            held[cs * toks : (cs + 1) * toks, i * LANES : (i + 1) * LANES] = pieces[lax.rem(y - 2 * i - cs + 4, 4)]
+    base[...] = held[...].astype(BF16)
+    score[...] = final[0:1, 0 : 2 * toks] * (1.0 / SCORE_DIVISOR)
 
 
 def trade(value, axis, bit, size=4):
@@ -179,66 +226,69 @@
   part = width // 16
   padded = store + 4
   wire = call(
-      pack_kernel, jax.ShapeDtypeStruct((16, padded, part), BF16), [VMEM] * 3,
-      [pltpu.VMEM((128, 128), F32), pltpu.VMEM((128, 128), F32), pltpu.VMEM((padded, part), F32)],
-      0, store * width * 6, 8,
-  )(weight_codes, scale_index, bit_widths.reshape(store, -1))
+      pack_kernel, jax.ShapeDtypeStruct((16, padded, part), BF16),
+      [pl.BlockSpec(memory_space=pl.ANY), VMEM, VMEM],
+      [pltpu.VMEM((store, width), jnp.int32), pltpu.VMEM((128, 128), F32), pltpu.VMEM((128, 128), F32),
+       pltpu.VMEM((padded, part), F32), pltpu.SemaphoreType.DMA((4,))],
+      0, store * width * 6, 60,
+  )(weight_codes, scale_index, bit_widths.reshape(store, 1, -1))
   home = lax.all_to_all(wire, ("x", "y"), 0, 0, tiled=True)
   other = trade(home, "c", 1, 2)
 
   value = call(
-      block_kernel, jax.ShapeDtypeStruct((4, toks, 4 * LANES), F32), [VMEM] * 2,
+      block_kernel, jax.ShapeDtypeStruct((4, toks, 4 * LANES), BF16), [VMEM] * 2,
       (), 2 * toks * 4096 * HB, 1 << 20, 8,
   )(activations, jnp.asarray(SIGNS, BF16))
-  for axis, bit in (("zl", 1), ("zl", 2)):
-      sign = jnp.where(lax.axis_index(axis) & bit, -1.0, 1.0).astype(F32)
-      value = trade(value, axis, bit) + sign * value
-  value = lax.all_to_all(value.astype(BF16), "zh", 0, 0, tiled=True)
-  value = value.reshape(4 * toks, 4 * LANES)
-  tokens = lax.all_to_all(jnp.broadcast_to(value[None], (16,) + value.shape), ("x", "y"), 0, 0, tiled=True)
+  value = lax.all_to_all(value, "zh", 0, 0, tiled=True)
+  value = call(unpad_kernel, jax.ShapeDtypeStruct((4 * toks, 4 * LANES), F32), [VMEM], (), 0, 1 << 18, 4)(value)
+  sign = jnp.where(lax.axis_index("zl") & 1, -1.0, 1.0).astype(F32)
+  value = trade(value, "zl", 1) + sign * value
+  got = trade(value, "zl", 2)
+  sign = jnp.where(lax.axis_index("zl") & 2, -1.0, 1.0).astype(F32).reshape(1)
+  value = call(
+      spread_kernel, jax.ShapeDtypeStruct((16,) + value.shape, BF16), [VMEM, VMEM, SMEM], (), 0, 1 << 21, 8,
+  )(got, value, sign)
+  tokens = lax.all_to_all(value, ("x", "y"), 0, 0, tiled=True)
 
   base_w, diff_w = call(
       lambda *refs: weight_kernel(store, *refs),
       [jax.ShapeDtypeStruct((16 * LANES, part), BF16)] * 2, [VMEM, VMEM, SMEM, SMEM],
       [pltpu.VMEM((128, 128), F32)] + [pltpu.VMEM((16 * LANES, part), F32)] * 2,
-      feat * part * 20, feat * part * 6, 24,
+      feat * part * 20, feat * part * 6, 16,
   )(home, other, scale_table, place)
   sums = call(
       matmul_kernel, jax.ShapeDtypeStruct((4, 8 * toks, part), BF16),
-      [VMEM] * 3, [pltpu.VMEM((16 * toks, 16 * LANES), BF16)],
-      4 * 16 * toks * feat * part, feat * part * 4 + 16 * toks * feat * 2, 20,
+      [VMEM] + [pl.BlockSpec(memory_space=pl.ANY)] * 2,
+      [pltpu.VMEM((16 * toks, 16 * LANES), BF16)] + [pltpu.VMEM((16 * LANES, part), BF16)] * 2
+      + [pltpu.SemaphoreType.DMA((2,))],
+      4 * 16 * toks * feat * part, feat * part * 4 + 16 * toks * feat * 2, 58,
   )(tokens, base_w, diff_w)
   near = lax.all_to_all(sums, "zl", 0, 0, tiled=True)
   wave = call(
-      near_kernel, jax.ShapeDtypeStruct((4, 5 * toks, part), BF16), [VMEM],
-      [pltpu.VMEM((4 * toks, part), F32), pltpu.VMEM((5 * toks, part), F32)],
+      near_kernel, jax.ShapeDtypeStruct((4, 8 * toks, LANES), BF16), [VMEM], (),
       32 * toks * part, 64 * toks * part, 8,
   )(near)
   far = lax.all_to_all(wave, "zh", 0, 0, tiled=True)
-  pieces, score = call(
+  *pieces, line = call(
       far_kernel,
-      [jax.ShapeDtypeStruct((4, toks, LANES), BF16), jax.ShapeDtypeStruct((4 * toks, LANES), F32)],
-      [VMEM], [pltpu.VMEM((5 * toks, part), F32)], 32 * toks * part, 40 * toks * part, 8,
-  )(far)
-  mine = score[:, 0].reshape(1, 4, 1, 1, toks)
-  spread = jnp.broadcast_to(mine, (4, 4, 2, 1, toks)).reshape(32, 1, toks)
-  everyone = lax.all_to_all(spread, ("x", "y", "c"), 0, 0, tiled=True)
-  scores = jnp.sum(everyone.reshape(16, 2 * toks), axis=0)[None] / SCORE_DIVISOR
-  y, c = lax.axis_index("y"), lax.axis_index("c")
+      [jax.ShapeDtypeStruct((toks, LANES), BF16)] * 4 + [jax.ShapeDtypeStruct((128, 1, LANES), F32)],
+      [VMEM, SMEM],
+      [pltpu.VMEM((8 * toks, LANES), F32), pltpu.VMEM((LANES, LANES), F32), pltpu.VMEM((4, toks, LANES), F32)],
+      32 * toks * part, 40 * toks * part, 4,
+  )(far, place)
+  lines = lax.all_to_all(line, ("x", "zh", "c", "y"), 0, 0, tiled=True)
   got = []
-  for r in range(4):
-      pairs = []
-      for cs in range(2):
-          for ys in range(4):
-              pairs.append((cs * 4 + ys, (ys // 2) * 4 + (2 * (ys % 2) + cs + r) % 4))
-      piece = lax.dynamic_index_in_dim(pieces, lax.rem(2 * lax.rem(y, 2) + c + r, 4), 0, False)
+  for r, piece in enumerate(pieces):
+      pairs = [
+          (cs * 4 + ys, (ys // 2) * 4 + (2 * (ys % 2) + cs + r) % 4) for cs in range(2) for ys in range(4)
+      ]
       got.append(lax.ppermute(piece, ("c", "y"), pairs))
-  got = jnp.stack(got)
-  rows = []
-  for cs in range(2):
-      rows.append(jnp.concatenate(
-          [lax.dynamic_index_in_dim(got, lax.rem(y - 2 * i - cs + 4, 4), 0, False) for i in range(2)], axis=1))
-  base = jnp.concatenate(rows, axis=0)
+  base, scores = call(
+      last_kernel,
+      [jax.ShapeDtypeStruct((2 * toks, 2 * LANES), BF16), jax.ShapeDtypeStruct((1, 2 * toks), F32)],
+      [VMEM] * 5 + [SMEM],
+      [pltpu.VMEM((4, toks, LANES), F32), pltpu.VMEM((2 * toks, 2 * LANES), F32)], 1 << 20, 1 << 18, 4,
+  )(lines, *got, place)
   return base, scores
 
 

time: 173 us -> 154 us (0.89)
  waiting for transfers between devices: 63.3 us -> 25.2 us
  blocking collectives: 18.4 us -> 34.5 us
  Pallas kernels: 8.34 us -> 17.8 us
  local copies, waits for them, and re-layouts: 10.7 us -> 5.83 us
  starting transfers between devices: 66.6 us -> 69.3 us
  other arithmetic: 2.62 us -> 0.1 us
    all_to_all x4 -> x3, waiting for transfers between devices: 37.6 us -> 10.7 us  [the longest x1 9.35 us: local(): value = lax.all_to_all(value, 'zh', 0, 0, tiled=True)]
    all_to_all x0 -> x1, blocking collectives: none -> 15.4 us  [local(): far = lax.all_to_all(wave, 'zh', 0, 0, tiled=True)]
    all_to_all x1, waiting for transfers between devices: 13.1 us -> 0.01 us  [local(): home = lax.all_to_all(wire, ('x', 'y'), 0, 0, tiled=True)]
    pallas_call x4 -> x7, Pallas kernels: 2.6 us -> 8.17 us  [the longest x1 3.24 us: local(): call(pack_kernel, jax.ShapeDtypeStruct((16, padded, part), BF16), [pl.Blo...]
    all_to_all x4 -> x3, starting transfers between devices: 33.1 us -> 37.3 us  [the longest x1 15.6 us: local(): value = lax.all_to_all(value, 'zh', 0, 0, tiled=True)]
    pallas_call x1, Pallas kernels: 1.59 us -> 5.46 us  [local(): call(matmul_kernel, jax.ShapeDtypeStruct((4, 8 * toks, part), BF16), [VME...]
    ppermute x3, starting transfers between devices: 15.1 us -> 11.8 us  [trade(): return lax.ppermute(value, axis, [(i, i ^ bit) for i in range(size)])]
    ppermute x3, waiting for transfers between devices: 10.2 us -> 12.8 us  [trade(): return lax.ppermute(value, axis, [(i, i ^ bit) for i in range(size)])]
  transfers between devices with their start and end apart: 12 -> 11, of which waited for: 8 -> 6; matrix products, arithmetic and copies ran while one was open for 1% -> 0% of each run, Pallas kernels for 3% -> 6%
where the time goes in v4:
time: 154 us
  starting transfers between devices  69.3 us (45%)
  blocking collectives  34.5 us (22%)
  waiting for transfers between devices  25.2 us (16%)
  Pallas kernels  17.8 us (12%)
  local copies, waits for them, and re-layouts  5.83 us (4%)
    all_to_all x1, blocking collectives, local(): near = lax.all_to_all(sums, 'zl', 0, 0, tiled=True)  19 us
    all_to_all x1, starting transfers between devices, local(): value = lax.all_to_all(value, 'zh', 0, 0, tiled=True)  15.6 us
    all_to_all x1, blocking collectives, local(): far = lax.all_to_all(wave, 'zh', 0, 0, tiled=True)  15.4 us
    all_to_all x1, starting transfers between devices, local(): lines = lax.all_to_all(line, ('x', 'zh', 'c', 'y'), 0, 0, tiled=True)  15.3 us
    ppermute x4, starting transfers between devices, local(): got.append(lax.ppermute(piece, ('c', 'y'), pairs))  13.5 us
    ppermute x3, waiting for transfers between devices, trade(): return lax.ppermute(value, axis, [(i, i ^ bit) for i in range(size)])  12.8 us
    ppermute x3, starting transfers between devices, trade(): return lax.ppermute(value, axis, [(i, i ^ bit) for i in range(size)])  11.8 us
    all_to_all x1, waiting for transfers between devices, local(): value = lax.all_to_all(value, 'zh', 0, 0, tiled=True)  9.35 us
  transfers between devices with their start and end apart: 11, of which 6 were waited for; matrix products, arithmetic and copies ran while one was open for 0% of the time, Pallas kernels for 6%

profile of v4, /device:TPU:1, one launch (start us, length us, event | category | flops | bytes accessed | tf_op | source)
XLA Modules:
  0.0 153.6 jit_solution(17830596304007291692)
XLA Ops:
  3.6 15.6 %all-to-all-start = ((bf16[4,20,512]{2,1,0:T(8,128)(2,1)}), bf16[4,20,512]{2,1,0:T(8,128)(2,1)S(1)}, u32[]{:S(2)}, u32[]{:S(2)}) async-start(bf16[4,20,512]{2,1,0:T(8,128)(2,1)} %shard_map.77), calls=%async_computation | async-start | bytes 196608 | tf_op jit(solution)/shard_map/all_to_all | solution.py:242
  19.3 3.2 %shard_map.80 = bf16[16,56,512]{2,1,0:T(8,128)(2,1)} custom-call(s32[52,8192]{1,0:T(8,128)} %codes_hbm.1, s32[52,64]{1,0:T(8,128)} %index.1, s32[52,1,64]{2,1,0:T(1,128)} %bitcast.6), custom_call_target="tpu_custom_call" | custom-call | bytes 2555904 | tf_op jit(solution)/shard_map/pallas_call | solution.py:228
  22.5 9.4 %all-to-all-done.parts = bf16[4,20,512]{2,1,0:T(8,128)(2,1)S(1)} async-done(((bf16[4,20,512]{2,1,0:T(8,128)(2,1)}), bf16[4,20,512]{2,1,0:T(8,128)(2,1)S(1)}, u32[]{:S(2)}, u32[]{:S(2)}) %all-to-all-start) | async-done | bytes 81952 | tf_op jit(solution)/shard_map/all_to_all | solution.py:242
  31.9 6.8 %all-to-all-start.2 = ((bf16[16,56,512]{2,1,0:T(8,128)(2,1)}), bf16[16,56,512]{2,1,0:T(8,128)(2,1)S(1)}, u32[]{:S(2)}, u32[]{:S(2)}) async-start(bf16[16,56,512]{2,1,0:T(8,128)(2,1)} %shard_map.80), calls=%async_computation.2 | async-start | bytes 1835008 | tf_op jit(solution)/shard_map/all_to_all | solution.py:235
  38.7 1.9 %collective-permute-start = (f32[80,512]{1,0:T(8,128)S(1)}, f32[80,512]{1,0:T(8,128)S(1)}, u32[]{:S(2)}, u32[]{:S(2)}) collective-permute-start(f32[80,512]{1,0:T(8,128)S(1)} %shard_map.78), channel_id=1, source_target_pairs={{0,4},{4,0},{8,12},{12,8},{1,5},{5,1},{9,13},{13,9},{2,6},{6,2},{1... | collective-permute-start | bytes 491528 | tf_op jit(solution)/shard_map/ppermute | solution.py:219
  40.6 4.4 %collective-permute-done = f32[80,512]{1,0:T(8,128)S(1)} collective-permute-done((f32[80,512]{1,0:T(8,128)S(1)}, f32[80,512]{1,0:T(8,128)S(1)}, u32[]{:S(2)}, u32[]{:S(2)}) %collective-permute-start) | collective-permute-done | bytes 163872 | tf_op jit(solution)/shard_map/ppermute | solution.py:219
  45.0 2.4 %collective-permute-start.1 = (f32[80,512]{1,0:T(8,128)S(1)}, f32[80,512]{1,0:T(8,128)S(1)}, u32[]{:S(2)}, u32[]{:S(2)}) collective-permute-start(f32[80,512]{1,0:T(8,128)S(1)} %multiply_add_fusion.value), channel_id=1, source_target_pairs={{0,8},{4,12},{8,0},{12,4},{1,9},{5,13},{9,1},{13,5},{2,10},{6,14},... | collective-permute-start | bytes 491528 | tf_op jit(solution)/shard_map/ppermute | solution.py:219
  47.4 6.3 %collective-permute-done.1.got = f32[80,512]{1,0:T(8,128)S(1)} collective-permute-done((f32[80,512]{1,0:T(8,128)S(1)}, f32[80,512]{1,0:T(8,128)S(1)}, u32[]{:S(2)}, u32[]{:S(2)}) %collective-permute-start.1) | collective-permute-done | bytes 163872 | tf_op jit(solution)/shard_map/ppermute | solution.py:219
  55.0 6.4 %all-to-all-start.1 = ((bf16[16,80,512]{2,1,0:T(8,128)(2,1)}), bf16[16,80,512]{2,1,0:T(8,128)(2,1)S(1)}, u32[]{:S(2)}, u32[]{:S(2)}) async-start(bf16[16,80,512]{2,1,0:T(8,128)(2,1)} %shard_map.79), calls=%async_computation.1 | async-start | bytes 2621440 | tf_op jit(solution)/shard_map/all_to_all | solution.py:251
  61.4 7.5 %collective-permute-start.2 = (bf16[16,56,512]{2,1,0:T(8,128)(2,1)S(1)}, bf16[16,56,512]{2,1,0:T(8,128)(2,1)S(1)}, u32[]{:S(2)}, u32[]{:S(2)}) collective-permute-start(bf16[16,56,512]{2,1,0:T(8,128)(2,1)S(1)} %all-to-all-done.2.refs_0_), channel_id=1, source_target_pairs={{0,16},{16,0},{1,17},{17,1},{2,18},{18,2},{3,19},{19,3},{4,20},{20... | collective-permute-start | bytes 2752520 | tf_op jit(solution)/shard_map/ppermute | solution.py:219
  69.0 2.0 %collective-permute-done.2.refs_1_ = bf16[16,56,512]{2,1,0:T(8,128)(2,1)S(1)} collective-permute-done((bf16[16,56,512]{2,1,0:T(8,128)(2,1)S(1)}, bf16[16,56,512]{2,1,0:T(8,128)(2,1)S(1)}, u32[]{:S(2)}, u32[]{:S(2)}) %collective-permute-start.2) | collective-permute-done | bytes 917536 | tf_op jit(solution)/shard_map/ppermute | solution.py:219
  71.0 4.2 %shard_map.81 = (bf16[2048,512]{1,0:T(8,128)(2,1)S(1)}, bf16[2048,512]{1,0:T(8,128)(2,1)S(1)}) custom-call(bf16[16,56,512]{2,1,0:T(8,128)(2,1)S(1)} %all-to-all-done.2.refs_0_, bf16[16,56,512]{2,1,0:T(8,128)(2,1)S(1)} %collective-permute-done.2.refs_1_, f32[16]{0:T(128)S(1)} %copy-done.4, s32[4]{0:T(128)S(1)} %pad_add_fusion.refs_3_.place), custom_call_target="tpu_custom_call" | custom-call | flops 17039360 | bytes 5111808 | tf_op jit(solution)/shard_map/pallas_call | solution.py:253
  75.2 1.3 copy-done
  78.9 5.5 %shard_map.82 = bf16[4,160,512]{2,1,0:T(8,128)(2,1)} custom-call(bf16[16,80,512]{2,1,0:T(8,128)(2,1)} %copy-done.5, bf16[2048,512]{1,0:T(8,128)(2,1)} %copy-done, bf16[2048,512]{1,0:T(8,128)(2,1)} %copy-done.1), custom_call_target="tpu_custom_call" | custom-call | flops 1090519040 | bytes 4472832 | tf_op jit(solution)/shard_map/pallas_call | solution.py:259
  84.3 19.0 %all_to_all.30.parts = bf16[4,160,512]{2,1,0:T(8,128)(2,1)S(1)} all-to-all(bf16[4,160,512]{2,1,0:T(8,128)(2,1)} %shard_map.82), channel_id=1, replica_groups=mesh['x'=4,'zh'=4,'c'=2,'zl'=4,'y'=4] {'zl'}, dimensions={0} | all-to-all | bytes 1310720 | tf_op jit(solution)/shard_map/all_to_all | solution.py:266
  103.4 15.4 %all_to_all.31.parts = bf16[4,160,128]{2,1,0:T(8,128)(2,1)S(1)} all-to-all(bf16[4,160,128]{2,1,0:T(8,128)(2,1)S(1)} %shard_map.83), channel_id=1, replica_groups=mesh['x'=4,'zh'=4,'c'=2,'zl'=4,'y'=4] {'zh'}, dimensions={0} | all-to-all | bytes 327680 | tf_op jit(solution)/shard_map/all_to_all | solution.py:271
  118.9 1.3 shard_map.84
  120.2 15.3 %all-to-all-start.5 = ((f32[128,1,128]{2,1,0:T(1,128)}), f32[128,1,128]{2,1,0:T(1,128)S(1)}, u32[]{:S(2)}, u32[]{:S(2)}) async-start(f32[128,1,128]{2,1,0:T(1,128)} %get-tuple-element.11), calls=%async_computation.5 | async-start | bytes 131072 | tf_op jit(solution)/shard_map/all_to_all | solution.py:279
  135.5 3.5 %collective-permute-start.3 = (bf16[20,128]{1,0:T(8,128)(2,1)S(1)}, bf16[20,128]{1,0:T(8,128)(2,1)S(1)}, u32[]{:S(2)}, u32[]{:S(2)}) collective-permute-start(bf16[20,128]{1,0:T(8,128)(2,1)S(1)} %get-tuple-element.12), channel_id=1, source_target_pairs={{0,0},{1,2},{2,16},{3,18},{16,1},{17,3},{18,17},{19,19},{4,4},{5,6... | collective-permute-start | bytes 15368 | tf_op jit(solution)/shard_map/ppermute | solution.py:285
  139.1 3.5 %collective-permute-start.4 = (bf16[20,128]{1,0:T(8,128)(2,1)S(1)}, bf16[20,128]{1,0:T(8,128)(2,1)S(1)}, u32[]{:S(2)}, u32[]{:S(2)}) collective-permute-start(bf16[20,128]{1,0:T(8,128)(2,1)S(1)} %get-tuple-element.13), channel_id=1, source_target_pairs={{0,1},{1,3},{2,17},{3,19},{16,2},{17,0},{18,18},{19,16},{4,5},{5,7... | collective-permute-start | bytes 15368 | tf_op jit(solution)/shard_map/ppermute | solution.py:285
  142.6 2.1 %collective-permute-start.5 = (bf16[20,128]{1,0:T(8,128)(2,1)S(1)}, bf16[20,128]{1,0:T(8,128)(2,1)S(1)}, u32[]{:S(2)}, u32[]{:S(2)}) collective-permute-start(bf16[20,128]{1,0:T(8,128)(2,1)S(1)} %get-tuple-element.14), channel_id=1, source_target_pairs={{0,2},{1,0},{2,18},{3,16},{16,3},{17,1},{18,19},{19,17},{4,6},{5,4... | collective-permute-start | bytes 15368 | tf_op jit(solution)/shard_map/ppermute | solution.py:285
  144.7 4.4 %collective-permute-start.6 = (bf16[20,128]{1,0:T(8,128)(2,1)S(1)}, bf16[20,128]{1,0:T(8,128)(2,1)S(1)}, u32[]{:S(2)}, u32[]{:S(2)}) collective-permute-start(bf16[20,128]{1,0:T(8,128)(2,1)S(1)} %get-tuple-element.15), channel_id=1, source_target_pairs={{0,3},{1,1},{2,19},{3,17},{16,0},{17,2},{18,16},{19,18},{4,7},{5,5... | collective-permute-start | bytes 15368 | tf_op jit(solution)/shard_map/ppermute | solution.py:285
  149.1 1.8 %collective-permute-done.6.g3 = bf16[20,128]{1,0:T(8,128)(2,1)S(1)} collective-permute-done((bf16[20,128]{1,0:T(8,128)(2,1)S(1)}, bf16[20,128]{1,0:T(8,128)(2,1)S(1)}, u32[]{:S(2)}, u32[]{:S(2)}) %collective-permute-start.6) | collective-permute-done | bytes 5152 | tf_op jit(solution)/shard_map/ppermute | solution.py:285
  152.2 1.3 shard_map.85
  (23 shorter events, 8.2 us)
Async XLA Ops:
  0.6 1.2 copy-start.2
  1.9 0.9 copy-start.3
  3.6 28.2 %all-to-all-start = ((bf16[4,20,512]{2,1,0:T(8,128)(2,1)}), bf16[4,20,512]{2,1,0:T(8,128)(2,1)S(1)}, u32[]{:S(2)}, u32[]{:S(2)}) async-start(bf16[4,20,512]{2,1,0:T(8,128)(2,1)} %shard_map.77), calls=%async_computation | async-start | bytes 196608 | tf_op jit(solution)/shard_map/all_to_all | solution.py:242
  31.9 23.2 %all-to-all-start.2 = ((bf16[16,56,512]{2,1,0:T(8,128)(2,1)}), bf16[16,56,512]{2,1,0:T(8,128)(2,1)S(1)}, u32[]{:S(2)}, u32[]{:S(2)}) async-start(bf16[16,56,512]{2,1,0:T(8,128)(2,1)} %shard_map.80), calls=%async_computation.2 | async-start | bytes 1835008 | tf_op jit(solution)/shard_map/all_to_all | solution.py:235
  38.7 6.4 %collective-permute-start = (f32[80,512]{1,0:T(8,128)S(1)}, f32[80,512]{1,0:T(8,128)S(1)}, u32[]{:S(2)}, u32[]{:S(2)}) collective-permute-start(f32[80,512]{1,0:T(8,128)S(1)} %shard_map.78), channel_id=1, source_target_pairs={{0,4},{4,0},{8,12},{12,8},{1,5},{5,1},{9,13},{13,9},{2,6},{6,2},{1... | collective-permute-start | bytes 491528 | tf_op jit(solution)/shard_map/ppermute | solution.py:219
  45.0 8.7 %collective-permute-start.1 = (f32[80,512]{1,0:T(8,128)S(1)}, f32[80,512]{1,0:T(8,128)S(1)}, u32[]{:S(2)}, u32[]{:S(2)}) collective-permute-start(f32[80,512]{1,0:T(8,128)S(1)} %multiply_add_fusion.value), channel_id=1, source_target_pairs={{0,8},{4,12},{8,0},{12,4},{1,9},{5,13},{9,1},{13,5},{2,10},{6,14},... | collective-permute-start | bytes 491528 | tf_op jit(solution)/shard_map/ppermute | solution.py:219
  53.8 17.2 %copy-start.4 = (f32[16]{0:T(128)S(1)}, f32[16]{0:T(128)}, u32[]{:S(2)}) copy-start(f32[16]{0:T(128)} %refs_2_.1) | copy-start | bytes 196
  55.0 22.8 %all-to-all-start.1 = ((bf16[16,80,512]{2,1,0:T(8,128)(2,1)}), bf16[16,80,512]{2,1,0:T(8,128)(2,1)S(1)}, u32[]{:S(2)}, u32[]{:S(2)}) async-start(bf16[16,80,512]{2,1,0:T(8,128)(2,1)} %shard_map.79), calls=%async_computation.1 | async-start | bytes 2621440 | tf_op jit(solution)/shard_map/all_to_all | solution.py:251
  61.4 9.6 %collective-permute-start.2 = (bf16[16,56,512]{2,1,0:T(8,128)(2,1)S(1)}, bf16[16,56,512]{2,1,0:T(8,128)(2,1)S(1)}, u32[]{:S(2)}, u32[]{:S(2)}) collective-permute-start(bf16[16,56,512]{2,1,0:T(8,128)(2,1)S(1)} %all-to-all-done.2.refs_0_), channel_id=1, source_target_pairs={{0,16},{16,0},{1,17},{17,1},{2,18},{18,2},{3,19},{19,3},{4,20},{20... | collective-permute-start | bytes 2752520 | tf_op jit(solution)/shard_map/ppermute | solution.py:219
  75.1 1.3 copy-start
  76.5 1.3 copy-start.1
  77.8 1.1 copy-start.5
  120.2 32.0 %all-to-all-start.5 = ((f32[128,1,128]{2,1,0:T(1,128)}), f32[128,1,128]{2,1,0:T(1,128)S(1)}, u32[]{:S(2)}, u32[]{:S(2)}) async-start(f32[128,1,128]{2,1,0:T(1,128)} %get-tuple-element.11), calls=%async_computation.5 | async-start | bytes 131072 | tf_op jit(solution)/shard_map/all_to_all | solution.py:279
  135.5 13.5 %collective-permute-start.3 = (bf16[20,128]{1,0:T(8,128)(2,1)S(1)}, bf16[20,128]{1,0:T(8,128)(2,1)S(1)}, u32[]{:S(2)}, u32[]{:S(2)}) collective-permute-start(bf16[20,128]{1,0:T(8,128)(2,1)S(1)} %get-tuple-element.12), channel_id=1, source_target_pairs={{0,0},{1,2},{2,16},{3,18},{16,1},{17,3},{18,17},{19,19},{4,4},{5,6... | collective-permute-start | bytes 15368 | tf_op jit(solution)/shard_map/ppermute | solution.py:285
  139.1 10.0 %collective-permute-start.4 = (bf16[20,128]{1,0:T(8,128)(2,1)S(1)}, bf16[20,128]{1,0:T(8,128)(2,1)S(1)}, u32[]{:S(2)}, u32[]{:S(2)}) collective-permute-start(bf16[20,128]{1,0:T(8,128)(2,1)S(1)} %get-tuple-element.13), channel_id=1, source_target_pairs={{0,1},{1,3},{2,17},{3,19},{16,2},{17,0},{18,18},{19,16},{4,5},{5,7... | collective-permute-start | bytes 15368 | tf_op jit(solution)/shard_map/ppermute | solution.py:285
  142.6 6.5 %collective-permute-start.5 = (bf16[20,128]{1,0:T(8,128)(2,1)S(1)}, bf16[20,128]{1,0:T(8,128)(2,1)S(1)}, u32[]{:S(2)}, u32[]{:S(2)}) collective-permute-start(bf16[20,128]{1,0:T(8,128)(2,1)S(1)} %get-tuple-element.14), channel_id=1, source_target_pairs={{0,2},{1,0},{2,18},{3,16},{16,3},{17,1},{18,19},{19,17},{4,6},{5,4... | collective-permute-start | bytes 15368 | tf_op jit(solution)/shard_map/ppermute | solution.py:285
  144.7 6.2 %collective-permute-start.6 = (bf16[20,128]{1,0:T(8,128)(2,1)S(1)}, bf16[20,128]{1,0:T(8,128)(2,1)S(1)}, u32[]{:S(2)}, u32[]{:S(2)}) collective-permute-start(bf16[20,128]{1,0:T(8,128)(2,1)S(1)} %get-tuple-element.15), channel_id=1, source_target_pairs={{0,3},{1,1},{2,19},{3,17},{16,0},{17,2},{18,16},{19,18},{4,7},{5,5... | collective-permute-start | bytes 15368 | tf_op jit(solution)/shard_map/ppermute | solution.py:285

commit v5 on v4

--- a/solution.py
+++ b/solution.py
@@ -19,28 +19,19 @@
 BF16 = jnp.bfloat16
 VMEM = pl.BlockSpec(memory_space=pltpu.VMEM)
 SMEM = pl.BlockSpec(memory_space=pltpu.SMEM)
-
-
-def chunk_signs():
+HBM = pl.BlockSpec(memory_space=pltpu.HBM)
+
+
+def block_signs():
     at = np.arange(HB)
     both = at[:, None] & at[None, :]
     parity = np.zeros((HB, HB), np.int64)
     for bit in range(7):
         parity ^= both >> bit & 1
-    block = 1 - 2 * parity
-    signs = np.zeros((16, 2 * HB, LANES), np.float32)
-    first = []
-    for m in range(16):
-        n0 = min(CHUNK * m // HB, 11)
-        first.append(n0 * HB)
-        for w in range(CHUNK):
-            h = CHUNK * m + w
-            row = (h // HB - n0) * HB
-            signs[m, row : row + HB, w] = block[:, h % HB]
-    return signs, first
-
-
-SIGNS, FIRST = chunk_signs()
+    return (1 - 2 * parity).astype(np.float32)
+
+
+SIGNS = block_signs()
 
 
 def call(kernel, out_shape, in_specs, scratch=(), flops=0, moved=0, limit=16):
@@ -51,16 +42,27 @@
         in_specs=in_specs,
         out_specs=[VMEM] * len(out_shape) if multi else VMEM,
         scratch_shapes=list(scratch),
-        compiler_params=pltpu.CompilerParams(vmem_limit_bytes=limit << 20),
+        compiler_params=pltpu.CompilerParams(vmem_limit_bytes=int(limit * (1 << 20))),
         cost_estimate=pl.CostEstimate(flops=flops, bytes_accessed=moved, transcendentals=0),
     )
 
 
-def block_kernel(act, signs, out):
+def block_kernel(act, signs, out, work):
+    toks = act.shape[0]
+    blocks = act.shape[1] // HB
+    for n in range(blocks):
+        work[n, 0:toks, :] = jnp.dot(act[:, n * HB : (n + 1) * HB], signs[...], preferred_element_type=F32)
+    lane = lax.broadcasted_iota(jnp.int32, work.shape[1:], 1)
     for m in range(16):
         xd, zd = divmod(m, 4)
-        piece = jnp.dot(act[:, FIRST[m] : FIRST[m] + 2 * HB], signs[m], preferred_element_type=F32)
-        out[zd, :, xd * LANES : (xd + 1) * LANES] = piece.astype(BF16)
+        n, offset = divmod(CHUNK * m, HB)
+        piece = work[n]
+        if offset:
+            piece = pltpu.roll(piece, HB - offset, 1)
+            if offset + CHUNK > HB:
+                piece = jnp.where(lane < HB - offset, piece, pltpu.roll(work[n + 1], HB - offset, 1))
+        piece = jnp.where(lane < CHUNK, piece, 0.0)
+        out[zd, :, xd * LANES : (xd + 1) * LANES] = piece[0:toks, :].astype(BF16)
 
 
 def pack_kernel(codes_hbm, index, bits, out, codes, meta, turned, block, sems):
@@ -88,7 +90,7 @@
             out[xd * 4 + yd] = block[...].astype(BF16)
 
 
-def weight_kernel(rows, own, other, table, place, base, diff, meta, base_acc, diff_acc):
+def weight_kernel(rows, own, other, table, place, base_hbm, diff_hbm, meta, base_acc, diff_acc, base, diff, sems):
     padded = own.shape[1]
     first = place[2] == 0
     turned = []
@@ -105,6 +107,7 @@
         meta[0:64, :] = scale
         turned.append(meta[...].T)
     blank = jnp.zeros((LANES - 2 * rows, own.shape[2]), F32)
+    copies = []
     for yd in range(4):
         for xd in range(4):
             p = xd * 4 + yd
@@ -127,8 +130,15 @@
                     diff_acc[start : start + padded, cols] = cand_w - base_w
             base_acc[top + 2 * rows : top + LANES, :] = blank
             diff_acc[top + 2 * rows : top + LANES, :] = blank
-    base[...] = base_acc[...].astype(BF16)
-    diff[...] = diff_acc[...].astype(BF16)
+        block = pl.ds(yd * 4 * LANES, 4 * LANES)
+        base[block, :] = base_acc[block, :].astype(BF16)
+        diff[block, :] = diff_acc[block, :].astype(BF16)
+        copies.append(pltpu.make_async_copy(base.at[block, :], base_hbm.at[block, :], sems.at[2 * yd]))
+        copies.append(pltpu.make_async_copy(diff.at[block, :], diff_hbm.at[block, :], sems.at[2 * yd + 1]))
+        copies[-2].start()
+        copies[-1].start()
+    for copy in copies:
+        copy.wait()
 
 
 def matmul_kernel(tokens, base_hbm, diff_hbm, out, left, base_w, diff_w, sems):
@@ -174,7 +184,7 @@
         out[zd] = total[:, zd * LANES : (zd + 1) * LANES].astype(BF16)
 
 
-def far_kernel(parts, place, p0, p1, p2, p3, score, total, turn, pieces):
+def far_kernel(parts, out, total, turn, block):
     acc = parts[0].astype(F32)
     for k in range(1, 4):
         acc = acc + parts[k].astype(F32)
@@ -184,35 +194,45 @@
     gap = total[rows:, :]
     turn[rows:, :] = jnp.zeros((LANES - rows, LANES), F32)
     turn[0:rows, :] = jnp.broadcast_to(jnp.sum(gap * gap, axis=1, keepdims=True), (rows, LANES))
-    line = turn[...].T[0:1, :]
-    for k in range(score.shape[0]):
-        score[k] = line
+    score = turn[...].T[0:1, :]
+    high = score.astype(BF16).astype(F32)
+    middle = (score - high).astype(BF16).astype(F32)
+    block[toks : toks + 1, :] = high
+    block[toks + 1 : toks + 2, :] = middle
+    block[toks + 2 : toks + 3, :] = score - high - middle
+    block[toks + 3 : toks + 4, :] = jnp.zeros((1, LANES), F32)
     for yd in range(4):
-        pieces[yd] = total[yd * toks : (yd + 1) * toks, :]
-    first = 2 * lax.rem(place[3], 2) + place[2]
-    for r, out in enumerate((p0, p1, p2, p3)):
-        out[...] = pieces[lax.rem(first + r, 4)].astype(BF16)
-
-
-def last_kernel(lines, g0, g1, g2, g3, place, base, score, pieces, held):
-    toks = g0.shape[0]
-    y = place[3]
+        block[0:toks, :] = total[yd * toks : (yd + 1) * toks, :]
+        wire = block[...].astype(BF16)
+        out[yd] = wire
+        out[4 + yd] = wire
+
+
+def join_kernel(parts, place, base, line, held):
+    toks = parts.shape[1] - 4
+    c, y = place[2], place[3]
     lane = lax.broadcasted_iota(jnp.int32, (LANES, LANES), 0)
     slot = lax.broadcasted_iota(jnp.int32, (LANES, LANES), 1)
-    for r, got in enumerate((g0, g1, g2, g3)):
-        pieces[r] = got[...].astype(F32)
     final = jnp.zeros((8, LANES), F32)
     for cs in range(2):
-        row = jnp.zeros((1, LANES), F32)
-        for k in range(16):
-            for ys in range(4):
-                row = row + lines[(2 * k + cs) * 4 + ys]
+        total = jnp.zeros((8, LANES), F32)
+        for ys in range(4):
+            total = total + parts[4 * cs + ys, toks - 4 : toks + 4, :].astype(F32)
+        row = total[4:5, :] + total[5:6, :] + total[6:7, :]
         pick = jnp.where((lane == y * toks + slot - cs * toks) & (slot >= cs * toks) & (slot < (cs + 1) * toks), 1.0, 0.0)
         final = final + jnp.dot(jnp.broadcast_to(row, (8, LANES)), pick, precision=lax.Precision.HIGHEST, preferred_element_type=F32)
         for i in range(2):
-            held[cs * toks : (cs + 1) * toks, i * LANES : (i + 1) * LANES] = pieces[lax.rem(y - 2 * i - cs + 4, 4)]
+            held[cs * toks : (cs + 1) * toks, i * LANES : (i + 1) * LANES] = parts[4 * cs + 2 * c + i][0:toks, :].astype(F32)
     base[...] = held[...].astype(BF16)
-    score[...] = final[0:1, 0 : 2 * toks] * (1.0 / SCORE_DIVISOR)
+    for k in range(line.shape[0]):
+        line[k] = final[0:1, :]
+
+
+def last_kernel(lines, score):
+    row = lines[0]
+    for k in range(1, lines.shape[0]):
+        row = row + lines[k]
+    score[...] = row[:, 0 : score.shape[1]] * (1.0 / SCORE_DIVISOR)
 
 
 def trade(value, axis, bit, size=4):
@@ -237,7 +257,7 @@
 
   value = call(
       block_kernel, jax.ShapeDtypeStruct((4, toks, 4 * LANES), BF16), [VMEM] * 2,
-      (), 2 * toks * 4096 * HB, 1 << 20, 8,
+      [pltpu.VMEM((feat // HB, toks + 4, HB), F32)], 2 * toks * 4096 * HB, 1 << 18, 4,
   )(activations, jnp.asarray(SIGNS, BF16))
   value = lax.all_to_all(value, "zh", 0, 0, tiled=True)
   value = call(unpad_kernel, jax.ShapeDtypeStruct((4 * toks, 4 * LANES), F32), [VMEM], (), 0, 1 << 18, 4)(value)
@@ -250,18 +270,21 @@
   )(got, value, sign)
   tokens = lax.all_to_all(value, ("x", "y"), 0, 0, tiled=True)
 
-  base_w, diff_w = call(
+  base_w, diff_w = pl.pallas_call(
       lambda *refs: weight_kernel(store, *refs),
-      [jax.ShapeDtypeStruct((16 * LANES, part), BF16)] * 2, [VMEM, VMEM, SMEM, SMEM],
-      [pltpu.VMEM((128, 128), F32)] + [pltpu.VMEM((16 * LANES, part), F32)] * 2,
-      feat * part * 20, feat * part * 6, 16,
+      out_shape=[jax.ShapeDtypeStruct((16 * LANES, part), BF16)] * 2,
+      in_specs=[VMEM, VMEM, SMEM, SMEM], out_specs=[HBM, HBM],
+      scratch_shapes=[pltpu.VMEM((128, 128), F32)] + [pltpu.VMEM((16 * LANES, part), F32)] * 2
+      + [pltpu.VMEM((16 * LANES, part), BF16)] * 2 + [pltpu.SemaphoreType.DMA((8,))],
+      name="weights", compiler_params=pltpu.CompilerParams(vmem_limit_bytes=int(62.05 * (1 << 20))),
+      cost_estimate=pl.CostEstimate(flops=feat * part * 20, bytes_accessed=feat * part * 6, transcendentals=0),
   )(home, other, scale_table, place)
   sums = call(
       matmul_kernel, jax.ShapeDtypeStruct((4, 8 * toks, part), BF16),
-      [VMEM] + [pl.BlockSpec(memory_space=pl.ANY)] * 2,
+      [VMEM, HBM, HBM],
       [pltpu.VMEM((16 * toks, 16 * LANES), BF16)] + [pltpu.VMEM((16 * LANES, part), BF16)] * 2
       + [pltpu.SemaphoreType.DMA((2,))],
-      4 * 16 * toks * feat * part, feat * part * 4 + 16 * toks * feat * 2, 58,
+      4 * 16 * toks * feat * part, feat * part * 4 + 16 * toks * feat * 2, 52,
   )(tokens, base_w, diff_w)
   near = lax.all_to_all(sums, "zl", 0, 0, tiled=True)
   wave = call(
@@ -269,26 +292,19 @@
       32 * toks * part, 64 * toks * part, 8,
   )(near)
   far = lax.all_to_all(wave, "zh", 0, 0, tiled=True)
-  *pieces, line = call(
-      far_kernel,
-      [jax.ShapeDtypeStruct((toks, LANES), BF16)] * 4 + [jax.ShapeDtypeStruct((128, 1, LANES), F32)],
-      [VMEM, SMEM],
-      [pltpu.VMEM((8 * toks, LANES), F32), pltpu.VMEM((LANES, LANES), F32), pltpu.VMEM((4, toks, LANES), F32)],
+  wire = call(
+      far_kernel, jax.ShapeDtypeStruct((8, toks + 4, LANES), BF16), [VMEM],
+      [pltpu.VMEM((8 * toks, LANES), F32), pltpu.VMEM((LANES, LANES), F32), pltpu.VMEM((toks + 4, LANES), F32)],
       32 * toks * part, 40 * toks * part, 4,
-  )(far, place)
-  lines = lax.all_to_all(line, ("x", "zh", "c", "y"), 0, 0, tiled=True)
-  got = []
-  for r, piece in enumerate(pieces):
-      pairs = [
-          (cs * 4 + ys, (ys // 2) * 4 + (2 * (ys % 2) + cs + r) % 4) for cs in range(2) for ys in range(4)
-      ]
-      got.append(lax.ppermute(piece, ("c", "y"), pairs))
-  base, scores = call(
-      last_kernel,
-      [jax.ShapeDtypeStruct((2 * toks, 2 * LANES), BF16), jax.ShapeDtypeStruct((1, 2 * toks), F32)],
-      [VMEM] * 5 + [SMEM],
-      [pltpu.VMEM((4, toks, LANES), F32), pltpu.VMEM((2 * toks, 2 * LANES), F32)], 1 << 20, 1 << 18, 4,
-  )(lines, *got, place)
+  )(far)
+  wire = lax.all_to_all(wire, ("c", "y"), 0, 0, tiled=True)
+  base, line = call(
+      join_kernel,
+      [jax.ShapeDtypeStruct((2 * toks, 2 * LANES), BF16), jax.ShapeDtypeStruct((16, 1, LANES), F32)],
+      [VMEM, SMEM], [pltpu.VMEM((2 * toks, 2 * LANES), F32)], 1 << 20, 1 << 18, 4,
+  )(wire, place)
+  lines = lax.all_to_all(line, ("x", "zh"), 0, 0, tiled=True)
+  scores = call(last_kernel, jax.ShapeDtypeStruct((1, 2 * toks), F32), [VMEM], (), 1 << 12, 1 << 14, 4)(lines)
   return base, scores
 
 

time: 154 us -> 151 us (0.981)
  blocking collectives: 34.5 us -> 68.1 us
  starting transfers between devices: 69.3 us -> 40.8 us
  local copies, waits for them, and re-layouts: 5.83 us -> 1.64 us
  waiting for transfers between devices: 25.2 us -> 21.5 us
    all_to_all x0 -> x2, blocking collectives: none -> 34.1 us  [the longest x1 20.5 us: local(): lines = lax.all_to_all(line, ('x', 'zh'), 0, 0, tiled=True)]
    all_to_all x1 -> x0, starting transfers between devices: 15.3 us -> none  [local(): lines = lax.all_to_all(line, ('x', 'zh', 'c', 'y'), 0, 0, tiled=True)]
    ppermute x4 -> x0, starting transfers between devices: 13.5 us -> none  [local(): got.append(lax.ppermute(piece, ('c', 'y'), pairs))]
    unnamed x12 -> x8, local copies, waits for them, and re-layouts: 5.83 us -> 1.64 us
    all_to_all x1, blocking collectives: 19 us -> 15.8 us  [local(): near = lax.all_to_all(sums, 'zl', 0, 0, tiled=True)]
    all_to_all x1, blocking collectives: 15.4 us -> 18.1 us  [local(): far = lax.all_to_all(wave, 'zh', 0, 0, tiled=True)]
    pallas_call x1, Pallas kernels: 5.46 us -> 3.32 us  [local(): call(matmul_kernel, jax.ShapeDtypeStruct((4, 8 * toks, part), BF16), [VME...]
    ppermute x4 -> x0, waiting for transfers between devices: 1.78 us -> none  [local(): got.append(lax.ppermute(piece, ('c', 'y'), pairs))]
  transfers between devices with their start and end apart: 11 -> 6, of which waited for: 6 -> 4; matrix products, arithmetic and copies ran while one was open for 0% -> 0% of each run, Pallas kernels for 6% -> 7%
where the time goes in v5:
time: 151 us; the launch traced here: 150 us
  blocking collectives  68.1 us (45%)
  starting transfers between devices  40.8 us (27%)
  waiting for transfers between devices  21.5 us (14%)
  Pallas kernels  16.9 us (11%)
  local copies, waits for them, and re-layouts  1.64 us (1%)
    all_to_all x1, blocking collectives, local(): lines = lax.all_to_all(line, ('x', 'zh'), 0, 0, tiled=True)  20.5 us
    all_to_all x1, blocking collectives, local(): far = lax.all_to_all(wave, 'zh', 0, 0, tiled=True)  18.1 us
    all_to_all x1, blocking collectives, local(): near = lax.all_to_all(sums, 'zl', 0, 0, tiled=True)  15.8 us
    all_to_all x1, starting transfers between devices, local(): value = lax.all_to_all(value, 'zh', 0, 0, tiled=True)  15.6 us
    all_to_all x1, blocking collectives, local(): wire = lax.all_to_all(wire, ('c', 'y'), 0, 0, tiled=True)  13.6 us
    ppermute x3, waiting for transfers between devices, trade(): return lax.ppermute(value, axis, [(i, i ^ bit) for i in range(size)])  12.1 us
    ppermute x3, starting transfers between devices, trade(): return lax.ppermute(value, axis, [(i, i ^ bit) for i in range(size)])  12.1 us
    all_to_all x1, waiting for transfers between devices, local(): value = lax.all_to_all(value, 'zh', 0, 0, tiled=True)  9.37 us
  transfers between devices with their start and end apart: 6, of which 4 were waited for; matrix products, arithmetic and copies ran while one was open for 0% of the time, Pallas kernels for 7%

profile of v5, /device:TPU:1, one launch (start us, length us, event | category | flops | bytes accessed | tf_op | source)
XLA Modules:
  0.0 150.3 jit_solution(6187879058379769175)
XLA Ops:
  0.6 0.9 copy-done
  1.5 0.8 copy-done.1
  2.3 0.9 shard_map.77
  3.2 15.6 %all-to-all-start = ((bf16[4,20,512]{2,1,0:T(8,128)(2,1)}), bf16[4,20,512]{2,1,0:T(8,128)(2,1)S(1)}, u32[]{:S(2)}, u32[]{:S(2)}) async-start(bf16[4,20,512]{2,1,0:T(8,128)(2,1)} %shard_map.77), calls=%async_computation | async-start | bytes 196608 | tf_op jit(solution)/shard_map/all_to_all | solution.py:262
  18.8 3.2 %shard_map.80 = bf16[16,56,512]{2,1,0:T(8,128)(2,1)} custom-call(s32[52,8192]{1,0:T(8,128)} %codes_hbm.1, s32[52,64]{1,0:T(8,128)} %index.1, s32[52,1,64]{2,1,0:T(1,128)} %bitcast.6), custom_call_target="tpu_custom_call" | custom-call | bytes 2555904 | tf_op jit(solution)/shard_map/pallas_call | solution.py:248
  22.1 9.4 %all-to-all-done.parts = bf16[4,20,512]{2,1,0:T(8,128)(2,1)S(1)} async-done(((bf16[4,20,512]{2,1,0:T(8,128)(2,1)}), bf16[4,20,512]{2,1,0:T(8,128)(2,1)S(1)}, u32[]{:S(2)}, u32[]{:S(2)}) %all-to-all-start) | async-done | bytes 81952 | tf_op jit(solution)/shard_map/all_to_all | solution.py:262
  31.4 6.8 %all-to-all-start.2 = ((bf16[16,56,512]{2,1,0:T(8,128)(2,1)}), bf16[16,56,512]{2,1,0:T(8,128)(2,1)S(1)}, u32[]{:S(2)}, u32[]{:S(2)}) async-start(bf16[16,56,512]{2,1,0:T(8,128)(2,1)} %shard_map.80), calls=%async_computation.2 | async-start | bytes 1835008 | tf_op jit(solution)/shard_map/all_to_all | solution.py:255
  38.2 1.9 %collective-permute-start = (f32[80,512]{1,0:T(8,128)S(1)}, f32[80,512]{1,0:T(8,128)S(1)}, u32[]{:S(2)}, u32[]{:S(2)}) collective-permute-start(f32[80,512]{1,0:T(8,128)S(1)} %shard_map.78), channel_id=1, source_target_pairs={{0,4},{4,0},{8,12},{12,8},{1,5},{5,1},{9,13},{13,9},{2,6},{6,2},{1... | collective-permute-start | bytes 491528 | tf_op jit(solution)/shard_map/ppermute | solution.py:239
  40.2 4.1 %collective-permute-done = f32[80,512]{1,0:T(8,128)S(1)} collective-permute-done((f32[80,512]{1,0:T(8,128)S(1)}, f32[80,512]{1,0:T(8,128)S(1)}, u32[]{:S(2)}, u32[]{:S(2)}) %collective-permute-start) | collective-permute-done | bytes 163872 | tf_op jit(solution)/shard_map/ppermute | solution.py:239
  44.3 2.7 %collective-permute-start.1 = (f32[80,512]{1,0:T(8,128)S(1)}, f32[80,512]{1,0:T(8,128)S(1)}, u32[]{:S(2)}, u32[]{:S(2)}) collective-permute-start(f32[80,512]{1,0:T(8,128)S(1)} %multiply_add_fusion.value), channel_id=1, source_target_pairs={{0,8},{4,12},{8,0},{12,4},{1,9},{5,13},{9,1},{13,5},{2,10},{6,14},... | collective-permute-start | bytes 491528 | tf_op jit(solution)/shard_map/ppermute | solution.py:239
  47.0 6.3 %collective-permute-done.1.got = f32[80,512]{1,0:T(8,128)S(1)} collective-permute-done((f32[80,512]{1,0:T(8,128)S(1)}, f32[80,512]{1,0:T(8,128)S(1)}, u32[]{:S(2)}, u32[]{:S(2)}) %collective-permute-start.1) | collective-permute-done | bytes 163872 | tf_op jit(solution)/shard_map/ppermute | solution.py:239
  53.3 1.2 shard_map.79
  54.6 6.4 %all-to-all-start.1 = ((bf16[16,80,512]{2,1,0:T(8,128)(2,1)}), bf16[16,80,512]{2,1,0:T(8,128)(2,1)S(1)}, u32[]{:S(2)}, u32[]{:S(2)}) async-start(bf16[16,80,512]{2,1,0:T(8,128)(2,1)} %shard_map.79), calls=%async_computation.1 | async-start | bytes 2621440 | tf_op jit(solution)/shard_map/all_to_all | solution.py:271
  61.0 7.5 %collective-permute-start.2 = (bf16[16,56,512]{2,1,0:T(8,128)(2,1)S(1)}, bf16[16,56,512]{2,1,0:T(8,128)(2,1)}, u32[]{:S(2)}, u32[]{:S(2)}) collective-permute-start(bf16[16,56,512]{2,1,0:T(8,128)(2,1)S(1)} %all-to-all-done.2.refs_0_), channel_id=1, source_target_pairs={{0,16},{16,0},{1,17},{17,1},{2,18},{18,2},{3,19},{19,3},{4,20},{20... | collective-permute-start | bytes 2752520 | tf_op jit(solution)/shard_map/ppermute | solution.py:239
  68.5 0.6 pad_add_fusion.refs_3_.place
  69.0 1.6 %collective-permute-done.2.refs_1_ = bf16[16,56,512]{2,1,0:T(8,128)(2,1)} collective-permute-done((bf16[16,56,512]{2,1,0:T(8,128)(2,1)S(1)}, bf16[16,56,512]{2,1,0:T(8,128)(2,1)}, u32[]{:S(2)}, u32[]{:S(2)}) %collective-permute-start.2) | collective-permute-done | bytes 917536 | tf_op jit(solution)/shard_map/ppermute | solution.py:239
  70.7 6.1 %weights.1 = (bf16[2048,512]{1,0:T(8,128)(2,1)}, bf16[2048,512]{1,0:T(8,128)(2,1)}) custom-call(bf16[16,56,512]{2,1,0:T(8,128)(2,1)} %copy-done.3, bf16[16,56,512]{2,1,0:T(8,128)(2,1)} %collective-permute-done.2.refs_1_, f32[16]{0:T(128)} %refs_2_.1, s32[4]{0:T(128)} %pad_add_fusion.refs_3_.place), custom_call_target="tpu_custom_call" | custom-call | flops 17039360 | bytes 5111808 | tf_op jit(solution)/shard_map/weights/pallas_call | solution.py:273
  76.8 3.3 %shard_map.81 = bf16[4,160,512]{2,1,0:T(8,128)(2,1)S(1)} custom-call(bf16[16,80,512]{2,1,0:T(8,128)(2,1)S(1)} %all-to-all-done.1.tokens, bf16[2048,512]{1,0:T(8,128)(2,1)} %get-tuple-element.6.base_hbm, bf16[2048,512]{1,0:T(8,128)(2,1)} %get-tuple-element.7.diff_hbm), custom_call_target="tpu_custom_call" | custom-call | flops 1090519040 | bytes 4472832 | tf_op jit(solution)/shard_map/pallas_call | solution.py:282
  80.1 15.8 %all_to_all.35.parts = bf16[4,160,512]{2,1,0:T(8,128)(2,1)S(1)} all-to-all(bf16[4,160,512]{2,1,0:T(8,128)(2,1)S(1)} %shard_map.81), channel_id=1, replica_groups=mesh['x'=4,'zh'=4,'c'=2,'zl'=4,'y'=4] {'zl'}, dimensions={0} | all-to-all | bytes 1310720 | tf_op jit(solution)/shard_map/all_to_all | solution.py:289
  96.0 18.1 %all_to_all.36.parts = bf16[4,160,128]{2,1,0:T(8,128)(2,1)S(1)} all-to-all(bf16[4,160,128]{2,1,0:T(8,128)(2,1)S(1)} %shard_map.82), channel_id=1, replica_groups=mesh['x'=4,'zh'=4,'c'=2,'zl'=4,'y'=4] {'zh'}, dimensions={0} | all-to-all | bytes 327680 | tf_op jit(solution)/shard_map/all_to_all | solution.py:294
  114.3 13.6 %all_to_all.37.parts = bf16[8,24,128]{2,1,0:T(8,128)(2,1)S(1)} all-to-all(bf16[8,24,128]{2,1,0:T(8,128)(2,1)S(1)} %shard_map.83), channel_id=1, replica_groups=mesh['x'=4,'zh'=4,'c'=2,'zl'=4,'y'=4] {'c','y'}, dimensions={0} | all-to-all | bytes 98304 | tf_op jit(solution)/shard_map/all_to_all | solution.py:300
  128.0 1.3 shard_map.84
  129.2 20.5 %all_to_all.38.lines = f32[16,1,128]{2,1,0:T(1,128)S(1)} all-to-all(f32[16,1,128]{2,1,0:T(1,128)S(1)} %get-tuple-element.9), channel_id=1, replica_groups=mesh['x'=4,'zh'=4,'c'=2,'zl'=4,'y'=4] {'x','zh'}, dimensions={0} | all-to-all | bytes 16384 | tf_op jit(solution)/shard_map/all_to_all | solution.py:306
  149.8 0.5 shard_map.85
  (12 shorter events, 0.3 us)
Async XLA Ops:
  0.6 0.9 copy-start
  1.5 0.8 copy-start.1
  3.2 28.2 %all-to-all-start = ((bf16[4,20,512]{2,1,0:T(8,128)(2,1)}), bf16[4,20,512]{2,1,0:T(8,128)(2,1)S(1)}, u32[]{:S(2)}, u32[]{:S(2)}) async-start(bf16[4,20,512]{2,1,0:T(8,128)(2,1)} %shard_map.77), calls=%async_computation | async-start | bytes 196608 | tf_op jit(solution)/shard_map/all_to_all | solution.py:262
  31.4 23.1 %all-to-all-start.2 = ((bf16[16,56,512]{2,1,0:T(8,128)(2,1)}), bf16[16,56,512]{2,1,0:T(8,128)(2,1)S(1)}, u32[]{:S(2)}, u32[]{:S(2)}) async-start(bf16[16,56,512]{2,1,0:T(8,128)(2,1)} %shard_map.80), calls=%async_computation.2 | async-start | bytes 1835008 | tf_op jit(solution)/shard_map/all_to_all | solution.py:255
  38.2 6.1 %collective-permute-start = (f32[80,512]{1,0:T(8,128)S(1)}, f32[80,512]{1,0:T(8,128)S(1)}, u32[]{:S(2)}, u32[]{:S(2)}) collective-permute-start(f32[80,512]{1,0:T(8,128)S(1)} %shard_map.78), channel_id=1, source_target_pairs={{0,4},{4,0},{8,12},{12,8},{1,5},{5,1},{9,13},{13,9},{2,6},{6,2},{1... | collective-permute-start | bytes 491528 | tf_op jit(solution)/shard_map/ppermute | solution.py:239
  44.3 9.0 %collective-permute-start.1 = (f32[80,512]{1,0:T(8,128)S(1)}, f32[80,512]{1,0:T(8,128)S(1)}, u32[]{:S(2)}, u32[]{:S(2)}) collective-permute-start(f32[80,512]{1,0:T(8,128)S(1)} %multiply_add_fusion.value), channel_id=1, source_target_pairs={{0,8},{4,12},{8,0},{12,4},{1,9},{5,13},{9,1},{13,5},{2,10},{6,14},... | collective-permute-start | bytes 491528 | tf_op jit(solution)/shard_map/ppermute | solution.py:239
  54.6 6.4 %copy-start.3 = (bf16[16,56,512]{2,1,0:T(8,128)(2,1)}, bf16[16,56,512]{2,1,0:T(8,128)(2,1)S(1)}, u32[]{:S(2)}) copy-start(bf16[16,56,512]{2,1,0:T(8,128)(2,1)S(1)} %all-to-all-done.2.refs_0_) | copy-start | bytes 2752516
  54.6 22.2 %all-to-all-start.1 = ((bf16[16,80,512]{2,1,0:T(8,128)(2,1)}), bf16[16,80,512]{2,1,0:T(8,128)(2,1)S(1)}, u32[]{:S(2)}, u32[]{:S(2)}) async-start(bf16[16,80,512]{2,1,0:T(8,128)(2,1)} %shard_map.79), calls=%async_computation.1 | async-start | bytes 2621440 | tf_op jit(solution)/shard_map/all_to_all | solution.py:271
  61.0 9.7 %collective-permute-start.2 = (bf16[16,56,512]{2,1,0:T(8,128)(2,1)S(1)}, bf16[16,56,512]{2,1,0:T(8,128)(2,1)}, u32[]{:S(2)}, u32[]{:S(2)}) collective-permute-start(bf16[16,56,512]{2,1,0:T(8,128)(2,1)S(1)} %all-to-all-done.2.refs_0_), channel_id=1, source_target_pairs={{0,16},{16,0},{1,17},{17,1},{2,18},{18,2},{3,19},{19,3},{4,20},{20... | collective-permute-start | bytes 2752520 | tf_op jit(solution)/shard_map/ppermute | solution.py:239
  80.1 47.9 %copy-start.2 = (s32[4]{0:T(128)S(1)}, s32[4]{0:T(128)}, u32[]{:S(2)}) copy-start(s32[4]{0:T(128)} %pad_add_fusion.refs_3_.place) | copy-start | bytes 52

commit v6 on v5

--- a/solution.py
+++ b/solution.py
@@ -164,75 +164,73 @@
         out[xd, rows : 2 * rows, :] = diff[xd * rows : (xd + 1) * rows, :]
 
 
-def unpad_kernel(parts, out):
+def unpad_kernel(parts, out, work):
     toks = parts.shape[1]
     for k in range(4):
-        out[k * toks : (k + 1) * toks, :] = parts[k].astype(F32)
-
-
-def spread_kernel(got, value, sign, out):
-    mixed = (got[...] + sign[0] * value[...]).astype(BF16)
+        work[k * toks : (k + 1) * toks, :] = parts[k].astype(F32)
+    out[...] = work[...].astype(BF16)
+
+
+def spread_kernel(own, g1, g2, g3, signs, out):
+    mixed = signs[0] * own[...].astype(F32)
+    for k, got in enumerate((g1, g2, g3)):
+        mixed = mixed + signs[k + 1] * got[...].astype(F32)
+    mixed = mixed.astype(BF16)
     for k in range(out.shape[0]):
         out[k] = mixed
 
 
-def near_kernel(parts, out):
-    total = parts[0].astype(F32)
-    for k in range(1, 4):
-        total = total + parts[k].astype(F32)
-    for zd in range(4):
-        out[zd] = total[:, zd * LANES : (zd + 1) * LANES].astype(BF16)
-
-
-def far_kernel(parts, out, total, turn, block):
+def near_kernel(parts, out, total, both):
     acc = parts[0].astype(F32)
     for k in range(1, 4):
         acc = acc + parts[k].astype(F32)
     total[...] = acc
     rows = parts.shape[1] // 2
     toks = rows // 4
-    gap = total[rows:, :]
-    turn[rows:, :] = jnp.zeros((LANES - rows, LANES), F32)
-    turn[0:rows, :] = jnp.broadcast_to(jnp.sum(gap * gap, axis=1, keepdims=True), (rows, LANES))
-    score = turn[...].T[0:1, :]
-    high = score.astype(BF16).astype(F32)
-    middle = (score - high).astype(BF16).astype(F32)
-    block[toks : toks + 1, :] = high
-    block[toks + 1 : toks + 2, :] = middle
-    block[toks + 2 : toks + 3, :] = score - high - middle
-    block[toks + 3 : toks + 4, :] = jnp.zeros((1, LANES), F32)
-    for yd in range(4):
-        block[0:toks, :] = total[yd * toks : (yd + 1) * toks, :]
-        wire = block[...].astype(BF16)
-        out[yd] = wire
-        out[4 + yd] = wire
-
-
-def join_kernel(parts, place, base, line, held):
-    toks = parts.shape[1] - 4
-    c, y = place[2], place[3]
-    lane = lax.broadcasted_iota(jnp.int32, (LANES, LANES), 0)
-    slot = lax.broadcasted_iota(jnp.int32, (LANES, LANES), 1)
-    final = jnp.zeros((8, LANES), F32)
+    for zd in range(4):
+        cols = slice(zd * LANES, (zd + 1) * LANES)
+        for yd in range(4):
+            both[0:toks, :] = total[yd * toks : (yd + 1) * toks, cols]
+            both[toks : 2 * toks, :] = total[rows + yd * toks : rows + (yd + 1) * toks, cols]
+            out[zd * 4 + yd] = both[...].astype(BF16)
+
+
+def far_kernel(parts, place, line, keep, send, both, turn, halves):
+    toks = parts.shape[1] // 2
+    score = jnp.zeros((toks, LANES), F32)
+    for ys in range(4):
+        acc = parts[ys].astype(F32)
+        for zs in range(1, 4):
+            acc = acc + parts[zs * 4 + ys].astype(F32)
+        both[...] = acc
+        gap = both[toks : 2 * toks, :]
+        score = score + gap * gap
+        halves[ys // 2, :, (ys % 2) * LANES : (ys % 2 + 1) * LANES] = both[0:toks, :]
+    turn[...] = jnp.zeros_like(turn)
+    turn[0:toks, :] = jnp.broadcast_to(jnp.sum(score, axis=1, keepdims=True), (toks, LANES))
+    row = turn[...].T[0:1, :]
+    for k in range(line.shape[0]):
+        line[k] = row
+    keep[...] = halves[place[2]].astype(BF16)
+    send[...] = halves[1 - place[2]].astype(BF16)
+
+
+def last_kernel(lines, keep, got, place, base, score, held):
+    toks = keep.shape[0]
+    first = place[2] == 0
+    mine, theirs = keep[...].astype(F32), got[...].astype(F32)
+    held[0:toks, :] = jnp.where(first, mine, theirs)
+    held[toks : 2 * toks, :] = jnp.where(first, theirs, mine)
+    base[...] = held[...].astype(BF16)
+    rows = []
     for cs in range(2):
-        total = jnp.zeros((8, LANES), F32)
-        for ys in range(4):
-            total = total + parts[4 * cs + ys, toks - 4 : toks + 4, :].astype(F32)
-        row = total[4:5, :] + total[5:6, :] + total[6:7, :]
-        pick = jnp.where((lane == y * toks + slot - cs * toks) & (slot >= cs * toks) & (slot < (cs + 1) * toks), 1.0, 0.0)
-        final = final + jnp.dot(jnp.broadcast_to(row, (8, LANES)), pick, precision=lax.Precision.HIGHEST, preferred_element_type=F32)
-        for i in range(2):
-            held[cs * toks : (cs + 1) * toks, i * LANES : (i + 1) * LANES] = parts[4 * cs + 2 * c + i][0:toks, :].astype(F32)
-    base[...] = held[...].astype(BF16)
-    for k in range(line.shape[0]):
-        line[k] = final[0:1, :]
-
-
-def last_kernel(lines, score):
-    row = lines[0]
-    for k in range(1, lines.shape[0]):
-        row = row + lines[k]
-    score[...] = row[:, 0 : score.shape[1]] * (1.0 / SCORE_DIVISOR)
+        row = lines[cs]
+        for k in range(1, lines.shape[0] // 2):
+            row = row + lines[2 * k + cs]
+        rows.append(row)
+    lane = lax.broadcasted_iota(jnp.int32, rows[0].shape, 1)
+    both = jnp.where(lane < toks, rows[0], pltpu.roll(rows[1], toks, 1))
+    score[...] = both[:, 0 : 2 * toks] * (1.0 / SCORE_DIVISOR)
 
 
 def trade(value, axis, bit, size=4):
@@ -257,17 +255,22 @@
 
   value = call(
       block_kernel, jax.ShapeDtypeStruct((4, toks, 4 * LANES), BF16), [VMEM] * 2,
-      [pltpu.VMEM((feat // HB, toks + 4, HB), F32)], 2 * toks * 4096 * HB, 1 << 18, 4,
+      [pltpu.VMEM((feat // HB, toks + 4, HB), F32)], 2 * toks * 4096 * HB, 1 << 18, 61,
   )(activations, jnp.asarray(SIGNS, BF16))
   value = lax.all_to_all(value, "zh", 0, 0, tiled=True)
-  value = call(unpad_kernel, jax.ShapeDtypeStruct((4 * toks, 4 * LANES), F32), [VMEM], (), 0, 1 << 18, 4)(value)
-  sign = jnp.where(lax.axis_index("zl") & 1, -1.0, 1.0).astype(F32)
-  value = trade(value, "zl", 1) + sign * value
-  got = trade(value, "zl", 2)
-  sign = jnp.where(lax.axis_index("zl") & 2, -1.0, 1.0).astype(F32).reshape(1)
   value = call(
-      spread_kernel, jax.ShapeDtypeStruct((16,) + value.shape, BF16), [VMEM, VMEM, SMEM], (), 0, 1 << 21, 8,
-  )(got, value, sign)
+      unpad_kernel, jax.ShapeDtypeStruct((4 * toks, 4 * LANES), BF16), [VMEM],
+      [pltpu.VMEM((4 * toks, 4 * LANES), F32)], 0, 1 << 18, 4,
+  )(value)
+  got = []
+  for k in (1, 2, 3):
+      got.append(trade(value, "zl", k))
+  zl = lax.axis_index("zl")
+  common = [zl & (zl ^ k) for k in range(4)]
+  signs = jnp.stack([1 - 2 * ((v ^ (v >> 1)) & 1) for v in common]).astype(F32)
+  value = call(
+      spread_kernel, jax.ShapeDtypeStruct((16,) + value.shape, BF16), [VMEM] * 4 + [SMEM], (), 0, 1 << 21, 8,
+  )(value, *got, signs)
   tokens = lax.all_to_all(value, ("x", "y"), 0, 0, tiled=True)
 
   base_w, diff_w = pl.pallas_call(
@@ -288,23 +291,25 @@
   )(tokens, base_w, diff_w)
   near = lax.all_to_all(sums, "zl", 0, 0, tiled=True)
   wave = call(
-      near_kernel, jax.ShapeDtypeStruct((4, 8 * toks, LANES), BF16), [VMEM], (),
+      near_kernel, jax.ShapeDtypeStruct((16, 2 * toks, LANES), BF16), [VMEM],
+      [pltpu.VMEM((8 * toks, part), F32), pltpu.VMEM((2 * toks, LANES), F32)],
       32 * toks * part, 64 * toks * part, 8,
   )(near)
-  far = lax.all_to_all(wave, "zh", 0, 0, tiled=True)
-  wire = call(
-      far_kernel, jax.ShapeDtypeStruct((8, toks + 4, LANES), BF16), [VMEM],
-      [pltpu.VMEM((8 * toks, LANES), F32), pltpu.VMEM((LANES, LANES), F32), pltpu.VMEM((toks + 4, LANES), F32)],
+  far = lax.all_to_all(wave, ("zh", "y"), 0, 0, tiled=True)
+  line, keep, send = call(
+      far_kernel,
+      [jax.ShapeDtypeStruct((32, 1, LANES), F32)] + [jax.ShapeDtypeStruct((toks, 2 * LANES), BF16)] * 2,
+      [VMEM, SMEM],
+      [pltpu.VMEM((2 * toks, LANES), F32), pltpu.VMEM((LANES, LANES), F32), pltpu.VMEM((2, toks, 2 * LANES), F32)],
       32 * toks * part, 40 * toks * part, 4,
-  )(far)
-  wire = lax.all_to_all(wire, ("c", "y"), 0, 0, tiled=True)
-  base, line = call(
-      join_kernel,
-      [jax.ShapeDtypeStruct((2 * toks, 2 * LANES), BF16), jax.ShapeDtypeStruct((16, 1, LANES), F32)],
-      [VMEM, SMEM], [pltpu.VMEM((2 * toks, 2 * LANES), F32)], 1 << 20, 1 << 18, 4,
-  )(wire, place)
-  lines = lax.all_to_all(line, ("x", "zh"), 0, 0, tiled=True)
-  scores = call(last_kernel, jax.ShapeDtypeStruct((1, 2 * toks), F32), [VMEM], (), 1 << 12, 1 << 14, 4)(lines)
+  )(far, place)
+  lines = lax.all_to_all(line, ("x", "zh", "c"), 0, 0, tiled=True)
+  got = trade(send, "c", 1, 2)
+  base, scores = call(
+      last_kernel,
+      [jax.ShapeDtypeStruct((2 * toks, 2 * LANES), BF16), jax.ShapeDtypeStruct((1, 2 * toks), F32)],
+      [VMEM] * 3 + [SMEM], [pltpu.VMEM((2 * toks, 2 * LANES), F32)], 1 << 16, 1 << 16, 4,
+  )(lines, keep, got, place)
   return base, scores
 
 

time: 151 us -> 144 us (0.954)
  blocking collectives: 68.1 us -> 36.6 us
  starting transfers between devices: 40.8 us -> 58.3 us
  waiting for transfers between devices: 21.5 us -> 28.3 us
  Pallas kernels: 16.9 us -> 18.9 us
  local copies, waits for them, and re-layouts: 1.64 us -> 0.01 us
    all_to_all x3 -> x1, blocking collectives: 52.3 us -> 20.7 us  [local(): far = lax.all_to_all(wave, ('zh', 'y'), 0, 0, tiled=True)]
    all_to_all x0 -> x1, starting transfers between devices: none -> 12 us  [local(): lines = lax.all_to_all(line, ('x', 'zh', 'c'), 0, 0, tiled=True)]
    all_to_all x0 -> x1, waiting for transfers between devices: none -> 11 us  [local(): lines = lax.all_to_all(line, ('x', 'zh', 'c'), 0, 0, tiled=True)]
    ppermute x3 -> x5, waiting for transfers between devices: 12.1 us -> 5.29 us  [trade(): return lax.ppermute(value, axis, [(i, i ^ bit) for i in range(size)])]
    ppermute x3 -> x5, starting transfers between devices: 12.1 us -> 17 us  [trade(): return lax.ppermute(value, axis, [(i, i ^ bit) for i in range(size)])]
    all_to_all x1, waiting for transfers between devices: 0.01 us -> 2.61 us  [local(): tokens = lax.all_to_all(value, ('x', 'y'), 0, 0, tiled=True)]
    unnamed x8 -> x4, local copies, waits for them, and re-layouts: 1.64 us -> 0.01 us
  transfers between devices with their start and end apart: 6 -> 9, of which waited for: 4 -> 7; matrix products, arithmetic and copies ran while one was open for 0% -> 1% of each run, Pallas kernels for 7% -> 8%
where the time goes in v6:
time: 144 us
  starting transfers between devices  58.3 us (40%)
  blocking collectives  36.6 us (25%)
  waiting for transfers between devices  28.3 us (20%)
  Pallas kernels  18.9 us (13%)
    all_to_all x1, blocking collectives, local(): far = lax.all_to_all(wave, ('zh', 'y'), 0, 0, tiled=True)  20.7 us
    ppermute x5, starting transfers between devices, trade(): return lax.ppermute(value, axis, [(i, i ^ bit) for i in range(size)])  17 us
    all_to_all x1, blocking collectives, local(): near = lax.all_to_all(sums, 'zl', 0, 0, tiled=True)  15.9 us
    all_to_all x1, starting transfers between devices, local(): value = lax.all_to_all(value, 'zh', 0, 0, tiled=True)  15.6 us
    all_to_all x1, starting transfers between devices, local(): lines = lax.all_to_all(line, ('x', 'zh', 'c'), 0, 0, tiled=True)  12 us
    all_to_all x1, waiting for transfers between devices, local(): lines = lax.all_to_all(line, ('x', 'zh', 'c'), 0, 0, tiled=True)  11 us
    all_to_all x1, waiting for transfers between devices, local(): value = lax.all_to_all(value, 'zh', 0, 0, tiled=True)  9.37 us
    all_to_all x1, starting transfers between devices, local(): tokens = lax.all_to_all(value, ('x', 'y'), 0, 0, tiled=True)  6.87 us
  transfers between devices with their start and end apart: 9, of which 7 were waited for; matrix products, arithmetic and copies ran while one was open for 1% of the time, Pallas kernels for 8%

profile of v6, /device:TPU:1, one launch (start us, length us, event | category | flops | bytes accessed | tf_op | source)
XLA Modules:
  0.0 143.7 jit_solution(11450836321368346189)
XLA Ops:
  0.6 1.8 %shard_map.77 = bf16[4,20,512]{2,1,0:T(8,128)(2,1)} custom-call(bf16[20,1664]{1,0:T(8,128)(2,1)} %act.1, bf16[128,128]{1,0:T(8,128)(2,1)} %constant.29.clone.signs), custom_call_target="tpu_custom_call" | custom-call | flops 20971520 | bytes 262144 | tf_op jit(solution)/shard_map/pallas_call | solution.py:256
  2.5 15.6 %all-to-all-start = ((bf16[4,20,512]{2,1,0:T(8,128)(2,1)}), bf16[4,20,512]{2,1,0:T(8,128)(2,1)S(1)}, u32[]{:S(2)}, u32[]{:S(2)}) async-start(bf16[4,20,512]{2,1,0:T(8,128)(2,1)} %shard_map.77), calls=%async_computation | async-start | bytes 196608 | tf_op jit(solution)/shard_map/all_to_all | solution.py:260
  18.1 3.2 %shard_map.80 = bf16[16,56,512]{2,1,0:T(8,128)(2,1)} custom-call(s32[52,8192]{1,0:T(8,128)} %codes_hbm.1, s32[52,64]{1,0:T(8,128)} %index.1, s32[52,1,64]{2,1,0:T(1,128)} %bitcast.9), custom_call_target="tpu_custom_call" | custom-call | bytes 2555904 | tf_op jit(solution)/shard_map/pallas_call | solution.py:246
  21.3 9.4 %all-to-all-done.parts = bf16[4,20,512]{2,1,0:T(8,128)(2,1)S(1)} async-done(((bf16[4,20,512]{2,1,0:T(8,128)(2,1)}), bf16[4,20,512]{2,1,0:T(8,128)(2,1)S(1)}, u32[]{:S(2)}, u32[]{:S(2)}) %all-to-all-start) | async-done | bytes 81952 | tf_op jit(solution)/shard_map/all_to_all | solution.py:260
  30.7 6.8 %all-to-all-start.2 = ((bf16[16,56,512]{2,1,0:T(8,128)(2,1)}), bf16[16,56,512]{2,1,0:T(8,128)(2,1)S(1)}, u32[]{:S(2)}, u32[]{:S(2)}) async-start(bf16[16,56,512]{2,1,0:T(8,128)(2,1)} %shard_map.80), calls=%async_computation.2 | async-start | bytes 1835008 | tf_op jit(solution)/shard_map/all_to_all | solution.py:253
  37.5 3.6 %collective-permute-start.2 = (bf16[80,512]{1,0:T(8,128)(2,1)S(1)}, bf16[80,512]{1,0:T(8,128)(2,1)S(1)}, u32[]{:S(2)}, u32[]{:S(2)}) collective-permute-start(bf16[80,512]{1,0:T(8,128)(2,1)S(1)} %shard_map.78.own), channel_id=1, source_target_pairs={{0,12},{4,8},{8,4},{12,0},{1,13},{5,9},{9,5},{13,1},{2,14},{6,10},... | collective-permute-start | bytes 245768 | tf_op jit(solution)/shard_map/ppermute | solution.py:237
  41.1 1.9 %collective-permute-start.1 = (bf16[80,512]{1,0:T(8,128)(2,1)S(1)}, bf16[80,512]{1,0:T(8,128)(2,1)S(1)}, u32[]{:S(2)}, u32[]{:S(2)}) collective-permute-start(bf16[80,512]{1,0:T(8,128)(2,1)S(1)} %shard_map.78.own), channel_id=1, source_target_pairs={{0,8},{4,12},{8,0},{12,4},{1,9},{5,13},{9,1},{13,5},{2,10},{6,14},... | collective-permute-start | bytes 245768 | tf_op jit(solution)/shard_map/ppermute | solution.py:237
  43.0 3.8 %collective-permute-start = (bf16[80,512]{1,0:T(8,128)(2,1)S(1)}, bf16[80,512]{1,0:T(8,128)(2,1)S(1)}, u32[]{:S(2)}, u32[]{:S(2)}) collective-permute-start(bf16[80,512]{1,0:T(8,128)(2,1)S(1)} %shard_map.78.own), channel_id=1, source_target_pairs={{0,4},{4,0},{8,12},{12,8},{1,5},{5,1},{9,13},{13,9},{2,6},{6,2},{1... | collective-permute-start | bytes 245768 | tf_op jit(solution)/shard_map/ppermute | solution.py:237
  46.9 1.9 %collective-permute-done.1.g2 = bf16[80,512]{1,0:T(8,128)(2,1)S(1)} collective-permute-done((bf16[80,512]{1,0:T(8,128)(2,1)S(1)}, bf16[80,512]{1,0:T(8,128)(2,1)S(1)}, u32[]{:S(2)}, u32[]{:S(2)}) %collective-permute-start.1) | collective-permute-done | bytes 81952 | tf_op jit(solution)/shard_map/ppermute | solution.py:237
  49.7 1.8 %shard_map.79 = bf16[16,80,512]{2,1,0:T(8,128)(2,1)} custom-call(bf16[80,512]{1,0:T(8,128)(2,1)S(1)} %shard_map.78.own, bf16[80,512]{1,0:T(8,128)(2,1)S(1)} %collective-permute-done.g1, bf16[80,512]{1,0:T(8,128)(2,1)S(1)} %collective-permute-done.1.g2, bf16[80,512]{1,0:T(8,128)(2,1)S(1)} %collective-permute-done.2.g3, f32[4]{0:T(128)S(1)} %add_convert_fusion.signs), custom_call_target="tpu_custom_call" | custom-call | bytes 2097152 | tf_op jit(solution)/shard_map/pallas_call | solution.py:271
  51.5 6.9 %all-to-all-start.1 = ((bf16[16,80,512]{2,1,0:T(8,128)(2,1)}), bf16[16,80,512]{2,1,0:T(8,128)(2,1)S(1)}, u32[]{:S(2)}, u32[]{:S(2)}) async-start(bf16[16,80,512]{2,1,0:T(8,128)(2,1)} %shard_map.79), calls=%async_computation.1 | async-start | bytes 2621440 | tf_op jit(solution)/shard_map/all_to_all | solution.py:274
  58.4 5.6 %collective-permute-start.3 = (bf16[16,56,512]{2,1,0:T(8,128)(2,1)S(1)}, bf16[16,56,512]{2,1,0:T(8,128)(2,1)}, u32[]{:S(2)}, u32[]{:S(2)}) collective-permute-start(bf16[16,56,512]{2,1,0:T(8,128)(2,1)S(1)} %all-to-all-done.2.refs_0_), channel_id=1, source_target_pairs={{0,16},{16,0},{1,17},{17,1},{2,18},{18,2},{3,19},{19,3},{4,20},{20... | collective-permute-start | bytes 2752520 | tf_op jit(solution)/shard_map/ppermute | solution.py:237
  64.6 1.6 %collective-permute-done.3.refs_1_ = bf16[16,56,512]{2,1,0:T(8,128)(2,1)} collective-permute-done((bf16[16,56,512]{2,1,0:T(8,128)(2,1)S(1)}, bf16[16,56,512]{2,1,0:T(8,128)(2,1)}, u32[]{:S(2)}, u32[]{:S(2)}) %collective-permute-start.3) | collective-permute-done | bytes 917536 | tf_op jit(solution)/shard_map/ppermute | solution.py:237
  66.2 6.1 %weights.1 = (bf16[2048,512]{1,0:T(8,128)(2,1)}, bf16[2048,512]{1,0:T(8,128)(2,1)}) custom-call(bf16[16,56,512]{2,1,0:T(8,128)(2,1)} %copy-done.1, bf16[16,56,512]{2,1,0:T(8,128)(2,1)} %collective-permute-done.3.refs_1_, f32[16]{0:T(128)} %refs_2_.1, s32[4]{0:T(128)} %pad_add_fusion.refs_3_.place), custom_call_target="tpu_custom_call" | custom-call | flops 17039360 | bytes 5111808 | tf_op jit(solution)/shard_map/weights/pallas_call | solution.py:276
  72.3 2.6 %all-to-all-done.1.tokens = bf16[16,80,512]{2,1,0:T(8,128)(2,1)S(1)} async-done(((bf16[16,80,512]{2,1,0:T(8,128)(2,1)}), bf16[16,80,512]{2,1,0:T(8,128)(2,1)S(1)}, u32[]{:S(2)}, u32[]{:S(2)}) %all-to-all-start.1) | async-done | bytes 1310752 | tf_op jit(solution)/shard_map/all_to_all | solution.py:274
  74.9 3.3 %shard_map.81 = bf16[4,160,512]{2,1,0:T(8,128)(2,1)S(1)} custom-call(bf16[16,80,512]{2,1,0:T(8,128)(2,1)S(1)} %all-to-all-done.1.tokens, bf16[2048,512]{1,0:T(8,128)(2,1)} %get-tuple-element.7.base_hbm, bf16[2048,512]{1,0:T(8,128)(2,1)} %get-tuple-element.8.diff_hbm), custom_call_target="tpu_custom_call" | custom-call | flops 1090519040 | bytes 4472832 | tf_op jit(solution)/shard_map/pallas_call | solution.py:285
  78.2 15.9 %all_to_all.30.parts = bf16[4,160,512]{2,1,0:T(8,128)(2,1)S(1)} all-to-all(bf16[4,160,512]{2,1,0:T(8,128)(2,1)S(1)} %shard_map.81), channel_id=1, replica_groups=mesh['x'=4,'zh'=4,'c'=2,'zl'=4,'y'=4] {'zl'}, dimensions={0} | all-to-all | bytes 1310720 | tf_op jit(solution)/shard_map/all_to_all | solution.py:292
  94.3 20.7 %all_to_all.31.parts = bf16[16,40,128]{2,1,0:T(8,128)(2,1)S(1)} all-to-all(bf16[16,40,128]{2,1,0:T(8,128)(2,1)S(1)} %shard_map.82), channel_id=1, replica_groups=mesh['x'=4,'zh'=4,'c'=2,'zl'=4,'y'=4] {'zh','y'}, dimensions={0} | all-to-all | bytes 327680 | tf_op jit(solution)/shard_map/all_to_all | solution.py:298
  115.1 1.3 shard_map.83
  116.4 12.0 %all-to-all-start.5 = ((f32[32,1,128]{2,1,0:T(1,128)}), f32[32,1,128]{2,1,0:T(1,128)S(1)}, u32[]{:S(2)}, u32[]{:S(2)}) async-start(f32[32,1,128]{2,1,0:T(1,128)} %get-tuple-element.9), calls=%async_computation.5 | async-start | bytes 32768 | tf_op jit(solution)/shard_map/all_to_all | solution.py:306
  128.4 2.1 %collective-permute-start.4 = (bf16[20,256]{1,0:T(8,128)(2,1)S(1)}, bf16[20,256]{1,0:T(8,128)(2,1)S(1)}, u32[]{:S(2)}, u32[]{:S(2)}) collective-permute-start(bf16[20,256]{1,0:T(8,128)(2,1)S(1)} %get-tuple-element.11), channel_id=1, source_target_pairs={{0,16},{16,0},{1,17},{17,1},{2,18},{18,2},{3,19},{19,3},{4,20},{20... | collective-permute-start | bytes 30728 | tf_op jit(solution)/shard_map/ppermute | solution.py:237
  130.6 0.9 collective-permute-done.4.got
  131.5 11.0 %all-to-all-done.5.lines = f32[32,1,128]{2,1,0:T(1,128)S(1)} async-done(((f32[32,1,128]{2,1,0:T(1,128)}), f32[32,1,128]{2,1,0:T(1,128)S(1)}, u32[]{:S(2)}, u32[]{:S(2)}) %all-to-all-start.5) | async-done | bytes 16416 | tf_op jit(solution)/shard_map/all_to_all | solution.py:306
  142.5 1.2 shard_map.84
  (11 shorter events, 1.8 us)
Async XLA Ops:
  2.5 28.2 %all-to-all-start = ((bf16[4,20,512]{2,1,0:T(8,128)(2,1)}), bf16[4,20,512]{2,1,0:T(8,128)(2,1)S(1)}, u32[]{:S(2)}, u32[]{:S(2)}) async-start(bf16[4,20,512]{2,1,0:T(8,128)(2,1)} %shard_map.77), calls=%async_computation | async-start | bytes 196608 | tf_op jit(solution)/shard_map/all_to_all | solution.py:260
  30.7 20.8 %all-to-all-start.2 = ((bf16[16,56,512]{2,1,0:T(8,128)(2,1)}), bf16[16,56,512]{2,1,0:T(8,128)(2,1)S(1)}, u32[]{:S(2)}, u32[]{:S(2)}) async-start(bf16[16,56,512]{2,1,0:T(8,128)(2,1)} %shard_map.80), calls=%async_computation.2 | async-start | bytes 1835008 | tf_op jit(solution)/shard_map/all_to_all | solution.py:253
  37.5 9.4 %collective-permute-start.2 = (bf16[80,512]{1,0:T(8,128)(2,1)S(1)}, bf16[80,512]{1,0:T(8,128)(2,1)S(1)}, u32[]{:S(2)}, u32[]{:S(2)}) collective-permute-start(bf16[80,512]{1,0:T(8,128)(2,1)S(1)} %shard_map.78.own), channel_id=1, source_target_pairs={{0,12},{4,8},{8,4},{12,0},{1,13},{5,9},{9,5},{13,1},{2,14},{6,10},... | collective-permute-start | bytes 245768 | tf_op jit(solution)/shard_map/ppermute | solution.py:237
  41.1 7.8 %collective-permute-start.1 = (bf16[80,512]{1,0:T(8,128)(2,1)S(1)}, bf16[80,512]{1,0:T(8,128)(2,1)S(1)}, u32[]{:S(2)}, u32[]{:S(2)}) collective-permute-start(bf16[80,512]{1,0:T(8,128)(2,1)S(1)} %shard_map.78.own), channel_id=1, source_target_pairs={{0,8},{4,12},{8,0},{12,4},{1,9},{5,13},{9,1},{13,5},{2,10},{6,14},... | collective-permute-start | bytes 245768 | tf_op jit(solution)/shard_map/ppermute | solution.py:237
  43.0 6.7 %collective-permute-start = (bf16[80,512]{1,0:T(8,128)(2,1)S(1)}, bf16[80,512]{1,0:T(8,128)(2,1)S(1)}, u32[]{:S(2)}, u32[]{:S(2)}) collective-permute-start(bf16[80,512]{1,0:T(8,128)(2,1)S(1)} %shard_map.78.own), channel_id=1, source_target_pairs={{0,4},{4,0},{8,12},{12,8},{1,5},{5,1},{9,13},{13,9},{2,6},{6,2},{1... | collective-permute-start | bytes 245768 | tf_op jit(solution)/shard_map/ppermute | solution.py:237
  51.5 6.9 %copy-start.1 = (bf16[16,56,512]{2,1,0:T(8,128)(2,1)}, bf16[16,56,512]{2,1,0:T(8,128)(2,1)S(1)}, u32[]{:S(2)}) copy-start(bf16[16,56,512]{2,1,0:T(8,128)(2,1)S(1)} %all-to-all-done.2.refs_0_) | copy-start | bytes 2752516
  51.5 23.4 %all-to-all-start.1 = ((bf16[16,80,512]{2,1,0:T(8,128)(2,1)}), bf16[16,80,512]{2,1,0:T(8,128)(2,1)S(1)}, u32[]{:S(2)}, u32[]{:S(2)}) async-start(bf16[16,80,512]{2,1,0:T(8,128)(2,1)} %shard_map.79), calls=%async_computation.1 | async-start | bytes 2621440 | tf_op jit(solution)/shard_map/all_to_all | solution.py:274
  58.4 7.8 %collective-permute-start.3 = (bf16[16,56,512]{2,1,0:T(8,128)(2,1)S(1)}, bf16[16,56,512]{2,1,0:T(8,128)(2,1)}, u32[]{:S(2)}, u32[]{:S(2)}) collective-permute-start(bf16[16,56,512]{2,1,0:T(8,128)(2,1)S(1)} %all-to-all-done.2.refs_0_), channel_id=1, source_target_pairs={{0,16},{16,0},{1,17},{17,1},{2,18},{18,2},{3,19},{19,3},{4,20},{20... | collective-permute-start | bytes 2752520 | tf_op jit(solution)/shard_map/ppermute | solution.py:237
  78.2 36.8 %copy-start = (s32[4]{0:T(128)S(1)}, s32[4]{0:T(128)}, u32[]{:S(2)}) copy-start(s32[4]{0:T(128)} %pad_add_fusion.refs_3_.place) | copy-start | bytes 52
  116.4 26.1 %all-to-all-start.5 = ((f32[32,1,128]{2,1,0:T(1,128)}), f32[32,1,128]{2,1,0:T(1,128)S(1)}, u32[]{:S(2)}, u32[]{:S(2)}) async-start(f32[32,1,128]{2,1,0:T(1,128)} %get-tuple-element.9), calls=%async_computation.5 | async-start | bytes 32768 | tf_op jit(solution)/shard_map/all_to_all | solution.py:306
  128.4 3.1 %collective-permute-start.4 = (bf16[20,256]{1,0:T(8,128)(2,1)S(1)}, bf16[20,256]{1,0:T(8,128)(2,1)S(1)}, u32[]{:S(2)}, u32[]{:S(2)}) collective-permute-start(bf16[20,256]{1,0:T(8,128)(2,1)S(1)} %get-tuple-element.11), channel_id=1, source_target_pairs={{0,16},{16,0},{1,17},{17,1},{2,18},{18,2},{3,19},{19,3},{4,20},{20... | collective-permute-start | bytes 30728 | tf_op jit(solution)/shard_map/ppermute | solution.py:237

commit v7 on v6

--- a/solution.py
+++ b/solution.py
@@ -141,27 +141,33 @@
         copy.wait()
 
 
-def matmul_kernel(tokens, base_hbm, diff_hbm, out, left, base_w, diff_w, sems):
+def matmul_kernel(tokens, base_hbm, diff_hbm, out, left, base_w, diff_w, base_acc, diff_acc, both, sems):
     rows, wide = tokens.shape[1:]
-    copies = [
-        pltpu.make_async_copy(base_hbm, base_w, sems.at[0]),
-        pltpu.make_async_copy(diff_hbm, diff_w, sems.at[1]),
-    ]
-    for copy in copies:
-        copy.start()
+    toks = rows // 4
+    copies = []
+    for j in range(4):
+        block = pl.ds(j * wide, wide)
+        for source, target in ((base_hbm, base_w), (diff_hbm, diff_w)):
+            copies.append(pltpu.make_async_copy(source.at[block, :], target.at[block, :], sems.at[len(copies)]))
+            copies[-1].start()
     factor = 1.0 / math.sqrt(HB * 16)
     for xd in range(4):
         s = [tokens[xd * 4 + yd].astype(F32) for yd in range(4)]
         a, b, c, d = s[0] + s[1], s[0] - s[1], s[2] + s[3], s[2] - s[3]
         for j, mixed in enumerate((a + c, b + d, a - c, b - d)):
             left[xd * rows : (xd + 1) * rows, j * wide : (j + 1) * wide] = (mixed * factor).astype(BF16)
-    copies[0].wait()
-    base = jnp.dot(left[...], base_w[...], preferred_element_type=F32).astype(BF16)
-    copies[1].wait()
-    diff = jnp.dot(left[...], diff_w[...], preferred_element_type=F32).astype(BF16)
+    for j in range(4):
+        block = slice(j * wide, (j + 1) * wide)
+        for k, (weight, total) in enumerate(((base_w, base_acc), (diff_w, diff_acc))):
+            copies[2 * j + k].wait()
+            part = jnp.dot(left[:, block], weight[block, :], preferred_element_type=F32)
+            total[...] = part if j == 0 else total[...] + part
     for xd in range(4):
-        out[xd, 0:rows, :] = base[xd * rows : (xd + 1) * rows, :]
-        out[xd, rows : 2 * rows, :] = diff[xd * rows : (xd + 1) * rows, :]
+        for yd in range(4):
+            start = xd * rows + yd * toks
+            both[0:toks, :] = base_acc[start : start + toks, :]
+            both[toks : 2 * toks, :] = diff_acc[start : start + toks, :]
+            out[xd * 4 + yd] = both[...].astype(BF16)
 
 
 def unpad_kernel(parts, out, work):
@@ -180,28 +186,25 @@
         out[k] = mixed
 
 
-def near_kernel(parts, out, total, both):
-    acc = parts[0].astype(F32)
-    for k in range(1, 4):
-        acc = acc + parts[k].astype(F32)
-    total[...] = acc
-    rows = parts.shape[1] // 2
-    toks = rows // 4
-    for zd in range(4):
-        cols = slice(zd * LANES, (zd + 1) * LANES)
-        for yd in range(4):
-            both[0:toks, :] = total[yd * toks : (yd + 1) * toks, cols]
-            both[toks : 2 * toks, :] = total[rows + yd * toks : rows + (yd + 1) * toks, cols]
-            out[zd * 4 + yd] = both[...].astype(BF16)
-
-
-def far_kernel(parts, place, line, keep, send, both, turn, halves):
-    toks = parts.shape[1] // 2
-    score = jnp.zeros((toks, LANES), F32)
+def near_kernel(parts, out):
+    rows = parts.shape[1]
     for ys in range(4):
         acc = parts[ys].astype(F32)
         for zs in range(1, 4):
             acc = acc + parts[zs * 4 + ys].astype(F32)
+        for zd in range(4):
+            out[zd, ys * rows : (ys + 1) * rows, :] = acc[:, zd * LANES : (zd + 1) * LANES].astype(BF16)
+
+
+def far_kernel(parts, place, line, keep, send, both, turn, halves):
+    rows = parts.shape[1] // 4
+    toks = rows // 2
+    score = jnp.zeros((toks, LANES), F32)
+    for ys in range(4):
+        block = slice(ys * rows, (ys + 1) * rows)
+        acc = parts[0, block, :].astype(F32)
+        for zs in range(1, 4):
+            acc = acc + parts[zs, block, :].astype(F32)
         both[...] = acc
         gap = both[toks : 2 * toks, :]
         score = score + gap * gap
@@ -215,13 +218,17 @@
     send[...] = halves[1 - place[2]].astype(BF16)
 
 
-def last_kernel(lines, keep, got, place, base, score, held):
+def base_kernel(keep, got, place, base, held):
     toks = keep.shape[0]
     first = place[2] == 0
     mine, theirs = keep[...].astype(F32), got[...].astype(F32)
     held[0:toks, :] = jnp.where(first, mine, theirs)
     held[toks : 2 * toks, :] = jnp.where(first, theirs, mine)
     base[...] = held[...].astype(BF16)
+
+
+def last_kernel(lines, score):
+    toks = score.shape[1] // 2
     rows = []
     for cs in range(2):
         row = lines[cs]
@@ -283,19 +290,18 @@
       cost_estimate=pl.CostEstimate(flops=feat * part * 20, bytes_accessed=feat * part * 6, transcendentals=0),
   )(home, other, scale_table, place)
   sums = call(
-      matmul_kernel, jax.ShapeDtypeStruct((4, 8 * toks, part), BF16),
+      matmul_kernel, jax.ShapeDtypeStruct((16, 2 * toks, part), BF16),
       [VMEM, HBM, HBM],
       [pltpu.VMEM((16 * toks, 16 * LANES), BF16)] + [pltpu.VMEM((16 * LANES, part), BF16)] * 2
-      + [pltpu.SemaphoreType.DMA((2,))],
+      + [pltpu.VMEM((16 * toks, part), F32)] * 2 + [pltpu.VMEM((2 * toks, part), F32), pltpu.SemaphoreType.DMA((8,))],
       4 * 16 * toks * feat * part, feat * part * 4 + 16 * toks * feat * 2, 52,
   )(tokens, base_w, diff_w)
-  near = lax.all_to_all(sums, "zl", 0, 0, tiled=True)
+  near = lax.all_to_all(sums, ("zl", "y"), 0, 0, tiled=True)
   wave = call(
-      near_kernel, jax.ShapeDtypeStruct((16, 2 * toks, LANES), BF16), [VMEM],
-      [pltpu.VMEM((8 * toks, part), F32), pltpu.VMEM((2 * toks, LANES), F32)],
+      near_kernel, jax.ShapeDtypeStruct((4, 8 * toks, LANES), BF16), [VMEM], (),
       32 * toks * part, 64 * toks * part, 8,
   )(near)
-  far = lax.all_to_all(wave, ("zh", "y"), 0, 0, tiled=True)
+  far = lax.all_to_all(wave, "zh", 0, 0, tiled=True)
   line, keep, send = call(
       far_kernel,
       [jax.ShapeDtypeStruct((32, 1, LANES), F32)] + [jax.ShapeDtypeStruct((toks, 2 * LANES), BF16)] * 2,
@@ -305,11 +311,11 @@
   )(far, place)
   lines = lax.all_to_all(line, ("x", "zh", "c"), 0, 0, tiled=True)
   got = trade(send, "c", 1, 2)
-  base, scores = call(
-      last_kernel,
-      [jax.ShapeDtypeStruct((2 * toks, 2 * LANES), BF16), jax.ShapeDtypeStruct((1, 2 * toks), F32)],
-      [VMEM] * 3 + [SMEM], [pltpu.VMEM((2 * toks, 2 * LANES), F32)], 1 << 16, 1 << 16, 4,
-  )(lines, keep, got, place)
+  base = call(
+      base_kernel, jax.ShapeDtypeStruct((2 * toks, 2 * LANES), BF16), [VMEM, VMEM, SMEM],
+      [pltpu.VMEM((2 * toks, 2 * LANES), F32)], 1 << 12, 1 << 16, 4,
+  )(keep, got, place)
+  scores = call(last_kernel, jax.ShapeDtypeStruct((1, 2 * toks), F32), [VMEM], (), 1 << 12, 1 << 14, 4)(lines)
   return base, scores
 
 

time: 144 us -> 144 us (level)
    pallas_call x3 -> x4, Pallas kernels: 4.69 us -> 5 us  [the longest x1 3.16 us: local(): call(matmul_kernel, jax.ShapeDtypeStruct((16, 2 * toks, part), BF16), [VM...]
  transfers between devices with their start and end apart: 9 -> 9, of which waited for: 7 -> 7; matrix products, arithmetic and copies ran while one was open for 1% -> 1% of each run, Pallas kernels for 8% -> 9%
where the time goes in v7:
time: 144 us; the launch traced here: 143 us
  starting transfers between devices  58.1 us (40%)
  blocking collectives  37.1 us (26%)
  waiting for transfers between devices  27.2 us (19%)
  Pallas kernels  19.2 us (13%)
    all_to_all x1, blocking collectives, local(): near = lax.all_to_all(sums, ('zl', 'y'), 0, 0, tiled=True)  19.4 us
    all_to_all x1, blocking collectives, local(): far = lax.all_to_all(wave, 'zh', 0, 0, tiled=True)  17.6 us
    ppermute x5, starting transfers between devices, trade(): return lax.ppermute(value, axis, [(i, i ^ bit) for i in range(size)])  17 us
    all_to_all x1, starting transfers between devices, local(): value = lax.all_to_all(value, 'zh', 0, 0, tiled=True)  15.6 us
    all_to_all x1, starting transfers between devices, local(): lines = lax.all_to_all(line, ('x', 'zh', 'c'), 0, 0, tiled=True)  11.8 us
    all_to_all x1, waiting for transfers between devices, local(): lines = lax.all_to_all(line, ('x', 'zh', 'c'), 0, 0, tiled=True)  9.95 us
    all_to_all x1, waiting for transfers between devices, local(): value = lax.all_to_all(value, 'zh', 0, 0, tiled=True)  9.37 us
    all_to_all x1, starting transfers between devices, local(): tokens = lax.all_to_all(value, ('x', 'y'), 0, 0, tiled=True)  6.87 us
  transfers between devices with their start and end apart: 9, of which 7 were waited for; matrix products, arithmetic and copies ran while one was open for 1% of the time, Pallas kernels for 9%

profile of v7, /device:TPU:1, one launch (start us, length us, event | category | flops | bytes accessed | tf_op | source)
XLA Modules:
  0.0 143.2 jit_solution(3116987687066777393)
XLA Ops:
  0.6 1.8 %shard_map.77 = bf16[4,20,512]{2,1,0:T(8,128)(2,1)} custom-call(bf16[20,1664]{1,0:T(8,128)(2,1)} %act.1, bf16[128,128]{1,0:T(8,128)(2,1)} %constant.29.clone.signs), custom_call_target="tpu_custom_call" | custom-call | flops 20971520 | bytes 262144 | tf_op jit(solution)/shard_map/pallas_call | solution.py:263
  2.5 15.6 %all-to-all-start = ((bf16[4,20,512]{2,1,0:T(8,128)(2,1)}), bf16[4,20,512]{2,1,0:T(8,128)(2,1)S(1)}, u32[]{:S(2)}, u32[]{:S(2)}) async-start(bf16[4,20,512]{2,1,0:T(8,128)(2,1)} %shard_map.77), calls=%async_computation | async-start | bytes 196608 | tf_op jit(solution)/shard_map/all_to_all | solution.py:267
  18.1 3.2 %shard_map.80 = bf16[16,56,512]{2,1,0:T(8,128)(2,1)} custom-call(s32[52,8192]{1,0:T(8,128)} %codes_hbm.1, s32[52,64]{1,0:T(8,128)} %index.1, s32[52,1,64]{2,1,0:T(1,128)} %bitcast.9), custom_call_target="tpu_custom_call" | custom-call | bytes 2555904 | tf_op jit(solution)/shard_map/pallas_call | solution.py:253
  21.3 9.4 %all-to-all-done.parts = bf16[4,20,512]{2,1,0:T(8,128)(2,1)S(1)} async-done(((bf16[4,20,512]{2,1,0:T(8,128)(2,1)}), bf16[4,20,512]{2,1,0:T(8,128)(2,1)S(1)}, u32[]{:S(2)}, u32[]{:S(2)}) %all-to-all-start) | async-done | bytes 81952 | tf_op jit(solution)/shard_map/all_to_all | solution.py:267
  30.7 6.8 %all-to-all-start.2 = ((bf16[16,56,512]{2,1,0:T(8,128)(2,1)}), bf16[16,56,512]{2,1,0:T(8,128)(2,1)S(1)}, u32[]{:S(2)}, u32[]{:S(2)}) async-start(bf16[16,56,512]{2,1,0:T(8,128)(2,1)} %shard_map.80), calls=%async_computation.2 | async-start | bytes 1835008 | tf_op jit(solution)/shard_map/all_to_all | solution.py:260
  37.5 3.6 %collective-permute-start.2 = (bf16[80,512]{1,0:T(8,128)(2,1)S(1)}, bf16[80,512]{1,0:T(8,128)(2,1)S(1)}, u32[]{:S(2)}, u32[]{:S(2)}) collective-permute-start(bf16[80,512]{1,0:T(8,128)(2,1)S(1)} %shard_map.78.own), channel_id=1, source_target_pairs={{0,12},{4,8},{8,4},{12,0},{1,13},{5,9},{9,5},{13,1},{2,14},{6,10},... | collective-permute-start | bytes 245768 | tf_op jit(solution)/shard_map/ppermute | solution.py:244
  41.1 1.9 %collective-permute-start.1 = (bf16[80,512]{1,0:T(8,128)(2,1)S(1)}, bf16[80,512]{1,0:T(8,128)(2,1)S(1)}, u32[]{:S(2)}, u32[]{:S(2)}) collective-permute-start(bf16[80,512]{1,0:T(8,128)(2,1)S(1)} %shard_map.78.own), channel_id=1, source_target_pairs={{0,8},{4,12},{8,0},{12,4},{1,9},{5,13},{9,1},{13,5},{2,10},{6,14},... | collective-permute-start | bytes 245768 | tf_op jit(solution)/shard_map/ppermute | solution.py:244
  43.0 3.8 %collective-permute-start = (bf16[80,512]{1,0:T(8,128)(2,1)S(1)}, bf16[80,512]{1,0:T(8,128)(2,1)S(1)}, u32[]{:S(2)}, u32[]{:S(2)}) collective-permute-start(bf16[80,512]{1,0:T(8,128)(2,1)S(1)} %shard_map.78.own), channel_id=1, source_target_pairs={{0,4},{4,0},{8,12},{12,8},{1,5},{5,1},{9,13},{13,9},{2,6},{6,2},{1... | collective-permute-start | bytes 245768 | tf_op jit(solution)/shard_map/ppermute | solution.py:244
  46.9 1.9 %collective-permute-done.1.g2 = bf16[80,512]{1,0:T(8,128)(2,1)S(1)} collective-permute-done((bf16[80,512]{1,0:T(8,128)(2,1)S(1)}, bf16[80,512]{1,0:T(8,128)(2,1)S(1)}, u32[]{:S(2)}, u32[]{:S(2)}) %collective-permute-start.1) | collective-permute-done | bytes 81952 | tf_op jit(solution)/shard_map/ppermute | solution.py:244
  49.7 1.8 %shard_map.79 = bf16[16,80,512]{2,1,0:T(8,128)(2,1)} custom-call(bf16[80,512]{1,0:T(8,128)(2,1)S(1)} %shard_map.78.own, bf16[80,512]{1,0:T(8,128)(2,1)S(1)} %collective-permute-done.g1, bf16[80,512]{1,0:T(8,128)(2,1)S(1)} %collective-permute-done.1.g2, bf16[80,512]{1,0:T(8,128)(2,1)S(1)} %collective-permute-done.2.g3, f32[4]{0:T(128)S(1)} %add_convert_fusion.signs), custom_call_target="tpu_custom_call" | custom-call | bytes 2097152 | tf_op jit(solution)/shard_map/pallas_call | solution.py:278
  51.5 6.9 %all-to-all-start.1 = ((bf16[16,80,512]{2,1,0:T(8,128)(2,1)}), bf16[16,80,512]{2,1,0:T(8,128)(2,1)S(1)}, u32[]{:S(2)}, u32[]{:S(2)}) async-start(bf16[16,80,512]{2,1,0:T(8,128)(2,1)} %shard_map.79), calls=%async_computation.1 | async-start | bytes 2621440 | tf_op jit(solution)/shard_map/all_to_all | solution.py:281
  58.4 5.6 %collective-permute-start.3 = (bf16[16,56,512]{2,1,0:T(8,128)(2,1)S(1)}, bf16[16,56,512]{2,1,0:T(8,128)(2,1)}, u32[]{:S(2)}, u32[]{:S(2)}) collective-permute-start(bf16[16,56,512]{2,1,0:T(8,128)(2,1)S(1)} %all-to-all-done.2.refs_0_), channel_id=1, source_target_pairs={{0,16},{16,0},{1,17},{17,1},{2,18},{18,2},{3,19},{19,3},{4,20},{20... | collective-permute-start | bytes 2752520 | tf_op jit(solution)/shard_map/ppermute | solution.py:244
  64.6 1.6 %collective-permute-done.3.refs_1_ = bf16[16,56,512]{2,1,0:T(8,128)(2,1)} collective-permute-done((bf16[16,56,512]{2,1,0:T(8,128)(2,1)S(1)}, bf16[16,56,512]{2,1,0:T(8,128)(2,1)}, u32[]{:S(2)}, u32[]{:S(2)}) %collective-permute-start.3) | collective-permute-done | bytes 917536 | tf_op jit(solution)/shard_map/ppermute | solution.py:244
  66.2 6.1 %weights.1 = (bf16[2048,512]{1,0:T(8,128)(2,1)}, bf16[2048,512]{1,0:T(8,128)(2,1)}) custom-call(bf16[16,56,512]{2,1,0:T(8,128)(2,1)} %copy-done.1, bf16[16,56,512]{2,1,0:T(8,128)(2,1)} %collective-permute-done.3.refs_1_, f32[16]{0:T(128)} %refs_2_.1, s32[4]{0:T(128)} %pad_add_fusion.refs_3_.place), custom_call_target="tpu_custom_call" | custom-call | flops 17039360 | bytes 5111808 | tf_op jit(solution)/shard_map/weights/pallas_call | solution.py:283
  72.3 2.6 %all-to-all-done.1.tokens = bf16[16,80,512]{2,1,0:T(8,128)(2,1)S(1)} async-done(((bf16[16,80,512]{2,1,0:T(8,128)(2,1)}), bf16[16,80,512]{2,1,0:T(8,128)(2,1)S(1)}, u32[]{:S(2)}, u32[]{:S(2)}) %all-to-all-start.1) | async-done | bytes 1310752 | tf_op jit(solution)/shard_map/all_to_all | solution.py:281
  74.9 3.2 %shard_map.81 = bf16[16,40,512]{2,1,0:T(8,128)(2,1)S(1)} custom-call(bf16[16,80,512]{2,1,0:T(8,128)(2,1)S(1)} %all-to-all-done.1.tokens, bf16[2048,512]{1,0:T(8,128)(2,1)} %get-tuple-element.7.base_hbm, bf16[2048,512]{1,0:T(8,128)(2,1)} %get-tuple-element.8.diff_hbm), custom_call_target="tpu_custom_call" | custom-call | flops 1090519040 | bytes 4472832 | tf_op jit(solution)/shard_map/pallas_call | solution.py:292
  78.1 19.4 %all_to_all.30.parts = bf16[16,40,512]{2,1,0:T(8,128)(2,1)S(1)} all-to-all(bf16[16,40,512]{2,1,0:T(8,128)(2,1)S(1)} %shard_map.81), channel_id=1, replica_groups=mesh['x'=4,'zh'=4,'c'=2,'zl'=4,'y'=4] {'zl','y'}, dimensions={0} | all-to-all | bytes 1310720 | tf_op jit(solution)/shard_map/all_to_all | solution.py:299
  97.6 17.6 %all_to_all.31.parts = bf16[4,160,128]{2,1,0:T(8,128)(2,1)S(1)} all-to-all(bf16[4,160,128]{2,1,0:T(8,128)(2,1)S(1)} %shard_map.82), channel_id=1, replica_groups=mesh['x'=4,'zh'=4,'c'=2,'zl'=4,'y'=4] {'zh'}, dimensions={0} | all-to-all | bytes 327680 | tf_op jit(solution)/shard_map/all_to_all | solution.py:304
  115.3 1.3 shard_map.83
  116.6 11.8 %all-to-all-start.5 = ((f32[32,1,128]{2,1,0:T(1,128)}), f32[32,1,128]{2,1,0:T(1,128)S(1)}, u32[]{:S(2)}, u32[]{:S(2)}) async-start(f32[32,1,128]{2,1,0:T(1,128)} %get-tuple-element.11), calls=%async_computation.5 | async-start | bytes 32768 | tf_op jit(solution)/shard_map/all_to_all | solution.py:312
  128.4 2.1 %collective-permute-start.4 = (bf16[20,256]{1,0:T(8,128)(2,1)S(1)}, bf16[20,256]{1,0:T(8,128)(2,1)S(1)}, u32[]{:S(2)}, u32[]{:S(2)}) collective-permute-start(bf16[20,256]{1,0:T(8,128)(2,1)S(1)} %get-tuple-element.10), channel_id=1, source_target_pairs={{0,16},{16,0},{1,17},{17,1},{2,18},{18,2},{3,19},{19,3},{4,20},{20... | collective-permute-start | bytes 30728 | tf_op jit(solution)/shard_map/ppermute | solution.py:244
  130.6 0.9 collective-permute-done.4.got
  131.5 1.2 shard_map.84
  132.7 10.0 %all-to-all-done.5.lines = f32[32,1,128]{2,1,0:T(1,128)S(1)} async-done(((f32[32,1,128]{2,1,0:T(1,128)}), f32[32,1,128]{2,1,0:T(1,128)S(1)}, u32[]{:S(2)}, u32[]{:S(2)}) %all-to-all-start.5) | async-done | bytes 16416 | tf_op jit(solution)/shard_map/all_to_all | solution.py:312
  (12 shorter events, 2.3 us)
Async XLA Ops:
  2.5 28.2 %all-to-all-start = ((bf16[4,20,512]{2,1,0:T(8,128)(2,1)}), bf16[4,20,512]{2,1,0:T(8,128)(2,1)S(1)}, u32[]{:S(2)}, u32[]{:S(2)}) async-start(bf16[4,20,512]{2,1,0:T(8,128)(2,1)} %shard_map.77), calls=%async_computation | async-start | bytes 196608 | tf_op jit(solution)/shard_map/all_to_all | solution.py:267
  30.7 20.8 %all-to-all-start.2 = ((bf16[16,56,512]{2,1,0:T(8,128)(2,1)}), bf16[16,56,512]{2,1,0:T(8,128)(2,1)S(1)}, u32[]{:S(2)}, u32[]{:S(2)}) async-start(bf16[16,56,512]{2,1,0:T(8,128)(2,1)} %shard_map.80), calls=%async_computation.2 | async-start | bytes 1835008 | tf_op jit(solution)/shard_map/all_to_all | solution.py:260
  37.5 9.4 %collective-permute-start.2 = (bf16[80,512]{1,0:T(8,128)(2,1)S(1)}, bf16[80,512]{1,0:T(8,128)(2,1)S(1)}, u32[]{:S(2)}, u32[]{:S(2)}) collective-permute-start(bf16[80,512]{1,0:T(8,128)(2,1)S(1)} %shard_map.78.own), channel_id=1, source_target_pairs={{0,12},{4,8},{8,4},{12,0},{1,13},{5,9},{9,5},{13,1},{2,14},{6,10},... | collective-permute-start | bytes 245768 | tf_op jit(solution)/shard_map/ppermute | solution.py:244
  41.1 7.8 %collective-permute-start.1 = (bf16[80,512]{1,0:T(8,128)(2,1)S(1)}, bf16[80,512]{1,0:T(8,128)(2,1)S(1)}, u32[]{:S(2)}, u32[]{:S(2)}) collective-permute-start(bf16[80,512]{1,0:T(8,128)(2,1)S(1)} %shard_map.78.own), channel_id=1, source_target_pairs={{0,8},{4,12},{8,0},{12,4},{1,9},{5,13},{9,1},{13,5},{2,10},{6,14},... | collective-permute-start | bytes 245768 | tf_op jit(solution)/shard_map/ppermute | solution.py:244
  43.0 6.7 %collective-permute-start = (bf16[80,512]{1,0:T(8,128)(2,1)S(1)}, bf16[80,512]{1,0:T(8,128)(2,1)S(1)}, u32[]{:S(2)}, u32[]{:S(2)}) collective-permute-start(bf16[80,512]{1,0:T(8,128)(2,1)S(1)} %shard_map.78.own), channel_id=1, source_target_pairs={{0,4},{4,0},{8,12},{12,8},{1,5},{5,1},{9,13},{13,9},{2,6},{6,2},{1... | collective-permute-start | bytes 245768 | tf_op jit(solution)/shard_map/ppermute | solution.py:244
  51.5 6.9 %copy-start.1 = (bf16[16,56,512]{2,1,0:T(8,128)(2,1)}, bf16[16,56,512]{2,1,0:T(8,128)(2,1)S(1)}, u32[]{:S(2)}) copy-start(bf16[16,56,512]{2,1,0:T(8,128)(2,1)S(1)} %all-to-all-done.2.refs_0_) | copy-start | bytes 2752516
  51.5 23.4 %all-to-all-start.1 = ((bf16[16,80,512]{2,1,0:T(8,128)(2,1)}), bf16[16,80,512]{2,1,0:T(8,128)(2,1)S(1)}, u32[]{:S(2)}, u32[]{:S(2)}) async-start(bf16[16,80,512]{2,1,0:T(8,128)(2,1)} %shard_map.79), calls=%async_computation.1 | async-start | bytes 2621440 | tf_op jit(solution)/shard_map/all_to_all | solution.py:281
  58.4 7.8 %collective-permute-start.3 = (bf16[16,56,512]{2,1,0:T(8,128)(2,1)S(1)}, bf16[16,56,512]{2,1,0:T(8,128)(2,1)}, u32[]{:S(2)}, u32[]{:S(2)}) collective-permute-start(bf16[16,56,512]{2,1,0:T(8,128)(2,1)S(1)} %all-to-all-done.2.refs_0_), channel_id=1, source_target_pairs={{0,16},{16,0},{1,17},{17,1},{2,18},{18,2},{3,19},{19,3},{4,20},{20... | collective-permute-start | bytes 2752520 | tf_op jit(solution)/shard_map/ppermute | solution.py:244
  78.1 37.2 %copy-start = (s32[4]{0:T(128)S(1)}, s32[4]{0:T(128)}, u32[]{:S(2)}) copy-start(s32[4]{0:T(128)} %pad_add_fusion.refs_3_.place) | copy-start | bytes 52
  116.6 26.0 %all-to-all-start.5 = ((f32[32,1,128]{2,1,0:T(1,128)}), f32[32,1,128]{2,1,0:T(1,128)S(1)}, u32[]{:S(2)}, u32[]{:S(2)}) async-start(f32[32,1,128]{2,1,0:T(1,128)} %get-tuple-element.11), calls=%async_computation.5 | async-start | bytes 32768 | tf_op jit(solution)/shard_map/all_to_all | solution.py:312
  128.4 3.1 %collective-permute-start.4 = (bf16[20,256]{1,0:T(8,128)(2,1)S(1)}, bf16[20,256]{1,0:T(8,128)(2,1)S(1)}, u32[]{:S(2)}, u32[]{:S(2)}) collective-permute-start(bf16[20,256]{1,0:T(8,128)(2,1)S(1)} %get-tuple-element.10), channel_id=1, source_target_pairs={{0,16},{16,0},{1,17},{17,1},{2,18},{18,2},{3,19},{19,3},{4,20},{20... | collective-permute-start | bytes 30728 | tf_op jit(solution)/shard_map/ppermute | solution.py:244

commit v8 on v7

--- a/solution.py
+++ b/solution.py
@@ -177,13 +177,16 @@
     out[...] = work[...].astype(BF16)
 
 
-def spread_kernel(own, g1, g2, g3, signs, out):
+def spread_kernel(own, g1, g2, g3, signs, out, block, sems):
     mixed = signs[0] * own[...].astype(F32)
     for k, got in enumerate((g1, g2, g3)):
         mixed = mixed + signs[k + 1] * got[...].astype(F32)
-    mixed = mixed.astype(BF16)
-    for k in range(out.shape[0]):
-        out[k] = mixed
+    block[...] = mixed.astype(BF16)
+    copies = [pltpu.make_async_copy(block, out.at[k], sems.at[k]) for k in range(out.shape[0])]
+    for copy in copies:
+        copy.start()
+    for copy in copies:
+        copy.wait()
 
 
 def near_kernel(parts, out):
@@ -275,8 +278,11 @@
   zl = lax.axis_index("zl")
   common = [zl & (zl ^ k) for k in range(4)]
   signs = jnp.stack([1 - 2 * ((v ^ (v >> 1)) & 1) for v in common]).astype(F32)
-  value = call(
-      spread_kernel, jax.ShapeDtypeStruct((16,) + value.shape, BF16), [VMEM] * 4 + [SMEM], (), 0, 1 << 21, 8,
+  value = pl.pallas_call(
+      spread_kernel, out_shape=jax.ShapeDtypeStruct((16,) + value.shape, BF16), in_specs=[VMEM] * 4 + [SMEM],
+      out_specs=HBM, scratch_shapes=[pltpu.VMEM(value.shape, BF16), pltpu.SemaphoreType.DMA((16,))],
+      name="spread", compiler_params=pltpu.CompilerParams(vmem_limit_bytes=8 << 20),
+      cost_estimate=pl.CostEstimate(flops=0, bytes_accessed=1 << 21, transcendentals=0),
   )(value, *got, signs)
   tokens = lax.all_to_all(value, ("x", "y"), 0, 0, tiled=True)
 
@@ -286,7 +292,7 @@
       in_specs=[VMEM, VMEM, SMEM, SMEM], out_specs=[HBM, HBM],
       scratch_shapes=[pltpu.VMEM((128, 128), F32)] + [pltpu.VMEM((16 * LANES, part), F32)] * 2
       + [pltpu.VMEM((16 * LANES, part), BF16)] * 2 + [pltpu.SemaphoreType.DMA((8,))],
-      name="weights", compiler_params=pltpu.CompilerParams(vmem_limit_bytes=int(62.05 * (1 << 20))),
+      name="weights", compiler_params=pltpu.CompilerParams(vmem_limit_bytes=52 << 20),
       cost_estimate=pl.CostEstimate(flops=feat * part * 20, bytes_accessed=feat * part * 6, transcendentals=0),
   )(home, other, scale_table, place)
   sums = call(

time: 144 us -> 144 us (level)
  transfers between devices with their start and end apart: 9 -> 9, of which waited for: 7 -> 7; matrix products, arithmetic and copies ran while one was open for 1% -> 0% of each run, Pallas kernels for 9% -> 8%
where the time goes in v8:
time: 144 us; the launch traced here: 143 us
  starting transfers between devices  58.1 us (40%)
  blocking collectives  37.1 us (26%)
  waiting for transfers between devices  28.6 us (20%)
  Pallas kernels  18.5 us (13%)
    all_to_all x1, blocking collectives, local(): near = lax.all_to_all(sums, ('zl', 'y'), 0, 0, tiled=True)  18.8 us
    all_to_all x1, blocking collectives, local(): far = lax.all_to_all(wave, 'zh', 0, 0, tiled=True)  18.3 us
    ppermute x5, starting transfers between devices, trade(): return lax.ppermute(value, axis, [(i, i ^ bit) for i in range(size)])  17 us
    all_to_all x1, starting transfers between devices, local(): value = lax.all_to_all(value, 'zh', 0, 0, tiled=True)  15.6 us
    all_to_all x1, starting transfers between devices, local(): lines = lax.all_to_all(line, ('x', 'zh', 'c'), 0, 0, tiled=True)  11.8 us
    all_to_all x1, waiting for transfers between devices, local(): lines = lax.all_to_all(line, ('x', 'zh', 'c'), 0, 0, tiled=True)  9.95 us
    all_to_all x1, waiting for transfers between devices, local(): value = lax.all_to_all(value, 'zh', 0, 0, tiled=True)  9.37 us
    all_to_all x1, starting transfers between devices, local(): tokens = lax.all_to_all(value, ('x', 'y'), 0, 0, tiled=True)  6.88 us
  transfers between devices with their start and end apart: 9, of which 7 were waited for; matrix products, arithmetic and copies ran while one was open for 0% of the time, Pallas kernels for 8%

profile of v8, /device:TPU:1, one launch (start us, length us, event | category | flops | bytes accessed | tf_op | source)
XLA Modules:
  0.0 143.3 jit_solution(14535800772627916772)
XLA Ops:
  0.6 1.8 %shard_map.77 = bf16[4,20,512]{2,1,0:T(8,128)(2,1)} custom-call(bf16[20,1664]{1,0:T(8,128)(2,1)} %act.1, bf16[128,128]{1,0:T(8,128)(2,1)} %constant.29.clone.signs), custom_call_target="tpu_custom_call" | custom-call | flops 20971520 | bytes 262144 | tf_op jit(solution)/shard_map/pallas_call | solution.py:266
  2.5 15.6 %all-to-all-start = ((bf16[4,20,512]{2,1,0:T(8,128)(2,1)}), bf16[4,20,512]{2,1,0:T(8,128)(2,1)S(1)}, u32[]{:S(2)}, u32[]{:S(2)}) async-start(bf16[4,20,512]{2,1,0:T(8,128)(2,1)} %shard_map.77), calls=%async_computation | async-start | bytes 196608 | tf_op jit(solution)/shard_map/all_to_all | solution.py:270
  18.1 3.2 %shard_map.79 = bf16[16,56,512]{2,1,0:T(8,128)(2,1)} custom-call(s32[52,8192]{1,0:T(8,128)} %codes_hbm.1, s32[52,64]{1,0:T(8,128)} %index.1, s32[52,1,64]{2,1,0:T(1,128)} %bitcast.9), custom_call_target="tpu_custom_call" | custom-call | bytes 2555904 | tf_op jit(solution)/shard_map/pallas_call | solution.py:256
  21.3 9.4 %all-to-all-done.parts = bf16[4,20,512]{2,1,0:T(8,128)(2,1)S(1)} async-done(((bf16[4,20,512]{2,1,0:T(8,128)(2,1)}), bf16[4,20,512]{2,1,0:T(8,128)(2,1)S(1)}, u32[]{:S(2)}, u32[]{:S(2)}) %all-to-all-start) | async-done | bytes 81952 | tf_op jit(solution)/shard_map/all_to_all | solution.py:270
  30.7 6.8 %all-to-all-start.2 = ((bf16[16,56,512]{2,1,0:T(8,128)(2,1)}), bf16[16,56,512]{2,1,0:T(8,128)(2,1)S(1)}, u32[]{:S(2)}, u32[]{:S(2)}) async-start(bf16[16,56,512]{2,1,0:T(8,128)(2,1)} %shard_map.79), calls=%async_computation.2 | async-start | bytes 1835008 | tf_op jit(solution)/shard_map/all_to_all | solution.py:263
  37.5 3.6 %collective-permute-start.2 = (bf16[80,512]{1,0:T(8,128)(2,1)S(1)}, bf16[80,512]{1,0:T(8,128)(2,1)S(1)}, u32[]{:S(2)}, u32[]{:S(2)}) collective-permute-start(bf16[80,512]{1,0:T(8,128)(2,1)S(1)} %shard_map.78.own), channel_id=1, source_target_pairs={{0,12},{4,8},{8,4},{12,0},{1,13},{5,9},{9,5},{13,1},{2,14},{6,10},... | collective-permute-start | bytes 245768 | tf_op jit(solution)/shard_map/ppermute | solution.py:247
  41.0 1.9 %collective-permute-start.1 = (bf16[80,512]{1,0:T(8,128)(2,1)S(1)}, bf16[80,512]{1,0:T(8,128)(2,1)S(1)}, u32[]{:S(2)}, u32[]{:S(2)}) collective-permute-start(bf16[80,512]{1,0:T(8,128)(2,1)S(1)} %shard_map.78.own), channel_id=1, source_target_pairs={{0,8},{4,12},{8,0},{12,4},{1,9},{5,13},{9,1},{13,5},{2,10},{6,14},... | collective-permute-start | bytes 245768 | tf_op jit(solution)/shard_map/ppermute | solution.py:247
  43.0 3.8 %collective-permute-start = (bf16[80,512]{1,0:T(8,128)(2,1)S(1)}, bf16[80,512]{1,0:T(8,128)(2,1)S(1)}, u32[]{:S(2)}, u32[]{:S(2)}) collective-permute-start(bf16[80,512]{1,0:T(8,128)(2,1)S(1)} %shard_map.78.own), channel_id=1, source_target_pairs={{0,4},{4,0},{8,12},{12,8},{1,5},{5,1},{9,13},{13,9},{2,6},{6,2},{1... | collective-permute-start | bytes 245768 | tf_op jit(solution)/shard_map/ppermute | solution.py:247
  46.9 1.9 %collective-permute-done.1.g2 = bf16[80,512]{1,0:T(8,128)(2,1)S(1)} collective-permute-done((bf16[80,512]{1,0:T(8,128)(2,1)S(1)}, bf16[80,512]{1,0:T(8,128)(2,1)S(1)}, u32[]{:S(2)}, u32[]{:S(2)}) %collective-permute-start.1) | collective-permute-done | bytes 81952 | tf_op jit(solution)/shard_map/ppermute | solution.py:247
  49.7 1.8 %spread.1 = bf16[16,80,512]{2,1,0:T(8,128)(2,1)} custom-call(bf16[80,512]{1,0:T(8,128)(2,1)S(1)} %shard_map.78.own, bf16[80,512]{1,0:T(8,128)(2,1)S(1)} %collective-permute-done.g1, bf16[80,512]{1,0:T(8,128)(2,1)S(1)} %collective-permute-done.1.g2, bf16[80,512]{1,0:T(8,128)(2,1)S(1)} %collective-permute-done.2.g3, f32[4]{0:T(128)S(1)} %add_convert_fusion.signs), custom_call_target="tpu_custom_call" | custom-call | bytes 2097152 | tf_op jit(solution)/shard_map/spread/pallas_call | solution.py:281
  51.5 6.9 %all-to-all-start.1 = ((bf16[16,80,512]{2,1,0:T(8,128)(2,1)}), bf16[16,80,512]{2,1,0:T(8,128)(2,1)S(1)}, u32[]{:S(2)}, u32[]{:S(2)}) async-start(bf16[16,80,512]{2,1,0:T(8,128)(2,1)} %spread.1), calls=%async_computation.1 | async-start | bytes 2621440 | tf_op jit(solution)/shard_map/all_to_all | solution.py:287
  58.4 5.6 %collective-permute-start.3 = (bf16[16,56,512]{2,1,0:T(8,128)(2,1)S(1)}, bf16[16,56,512]{2,1,0:T(8,128)(2,1)S(1)}, u32[]{:S(2)}, u32[]{:S(2)}) collective-permute-start(bf16[16,56,512]{2,1,0:T(8,128)(2,1)S(1)} %all-to-all-done.2.refs_0_), channel_id=1, source_target_pairs={{0,16},{16,0},{1,17},{17,1},{2,18},{18,2},{3,19},{19,3},{4,20},{20... | collective-permute-start | bytes 2752520 | tf_op jit(solution)/shard_map/ppermute | solution.py:247
  64.2 2.0 %collective-permute-done.3.refs_1_ = bf16[16,56,512]{2,1,0:T(8,128)(2,1)S(1)} collective-permute-done((bf16[16,56,512]{2,1,0:T(8,128)(2,1)S(1)}, bf16[16,56,512]{2,1,0:T(8,128)(2,1)S(1)}, u32[]{:S(2)}, u32[]{:S(2)}) %collective-permute-start.3) | collective-permute-done | bytes 917536 | tf_op jit(solution)/shard_map/ppermute | solution.py:247
  66.2 5.3 %weights.1 = (bf16[2048,512]{1,0:T(8,128)(2,1)}, bf16[2048,512]{1,0:T(8,128)(2,1)}) custom-call(bf16[16,56,512]{2,1,0:T(8,128)(2,1)S(1)} %all-to-all-done.2.refs_0_, bf16[16,56,512]{2,1,0:T(8,128)(2,1)S(1)} %collective-permute-done.3.refs_1_, f32[16]{0:T(128)S(1)} %copy-done, s32[4]{0:T(128)S(1)} %pad_add_fusion.refs_3_.place), custom_call_target="tpu_custom_call" | custom-call | flops 17039360 | bytes 5111808 | tf_op jit(solution)/shard_map/weights/pallas_call | solution.py:289
  71.4 3.6 %all-to-all-done.1.tokens = bf16[16,80,512]{2,1,0:T(8,128)(2,1)S(1)} async-done(((bf16[16,80,512]{2,1,0:T(8,128)(2,1)}), bf16[16,80,512]{2,1,0:T(8,128)(2,1)S(1)}, u32[]{:S(2)}, u32[]{:S(2)}) %all-to-all-start.1) | async-done | bytes 1310752 | tf_op jit(solution)/shard_map/all_to_all | solution.py:287
  75.0 3.2 %shard_map.80 = bf16[16,40,512]{2,1,0:T(8,128)(2,1)S(1)} custom-call(bf16[16,80,512]{2,1,0:T(8,128)(2,1)S(1)} %all-to-all-done.1.tokens, bf16[2048,512]{1,0:T(8,128)(2,1)} %get-tuple-element.7.base_hbm, bf16[2048,512]{1,0:T(8,128)(2,1)} %get-tuple-element.8.diff_hbm), custom_call_target="tpu_custom_call" | custom-call | flops 1090519040 | bytes 4472832 | tf_op jit(solution)/shard_map/pallas_call | solution.py:298
  78.2 18.8 %all_to_all.30.parts = bf16[16,40,512]{2,1,0:T(8,128)(2,1)S(1)} all-to-all(bf16[16,40,512]{2,1,0:T(8,128)(2,1)S(1)} %shard_map.80), channel_id=1, replica_groups=mesh['x'=4,'zh'=4,'c'=2,'zl'=4,'y'=4] {'zl','y'}, dimensions={0} | all-to-all | bytes 1310720 | tf_op jit(solution)/shard_map/all_to_all | solution.py:305
  97.1 18.3 %all_to_all.31.parts = bf16[4,160,128]{2,1,0:T(8,128)(2,1)S(1)} all-to-all(bf16[4,160,128]{2,1,0:T(8,128)(2,1)S(1)} %shard_map.81), channel_id=1, replica_groups=mesh['x'=4,'zh'=4,'c'=2,'zl'=4,'y'=4] {'zh'}, dimensions={0} | all-to-all | bytes 327680 | tf_op jit(solution)/shard_map/all_to_all | solution.py:310
  115.3 1.3 shard_map.82
  116.7 11.8 %all-to-all-start.5 = ((f32[32,1,128]{2,1,0:T(1,128)}), f32[32,1,128]{2,1,0:T(1,128)S(1)}, u32[]{:S(2)}, u32[]{:S(2)}) async-start(f32[32,1,128]{2,1,0:T(1,128)} %get-tuple-element.11), calls=%async_computation.5 | async-start | bytes 32768 | tf_op jit(solution)/shard_map/all_to_all | solution.py:318
  128.5 2.1 %collective-permute-start.4 = (bf16[20,256]{1,0:T(8,128)(2,1)S(1)}, bf16[20,256]{1,0:T(8,128)(2,1)S(1)}, u32[]{:S(2)}, u32[]{:S(2)}) collective-permute-start(bf16[20,256]{1,0:T(8,128)(2,1)S(1)} %get-tuple-element.10), channel_id=1, source_target_pairs={{0,16},{16,0},{1,17},{17,1},{2,18},{18,2},{3,19},{19,3},{4,20},{20... | collective-permute-start | bytes 30728 | tf_op jit(solution)/shard_map/ppermute | solution.py:247
  130.7 0.9 collective-permute-done.4.got
  131.6 1.2 shard_map.83
  132.7 9.9 %all-to-all-done.5.lines = f32[32,1,128]{2,1,0:T(1,128)S(1)} async-done(((f32[32,1,128]{2,1,0:T(1,128)}), f32[32,1,128]{2,1,0:T(1,128)S(1)}, u32[]{:S(2)}, u32[]{:S(2)}) %all-to-all-start.5) | async-done | bytes 16416 | tf_op jit(solution)/shard_map/all_to_all | solution.py:318
  (10 shorter events, 1.7 us)
Async XLA Ops:
  2.5 28.2 %all-to-all-start = ((bf16[4,20,512]{2,1,0:T(8,128)(2,1)}), bf16[4,20,512]{2,1,0:T(8,128)(2,1)S(1)}, u32[]{:S(2)}, u32[]{:S(2)}) async-start(bf16[4,20,512]{2,1,0:T(8,128)(2,1)} %shard_map.77), calls=%async_computation | async-start | bytes 196608 | tf_op jit(solution)/shard_map/all_to_all | solution.py:270
  30.7 20.9 %all-to-all-start.2 = ((bf16[16,56,512]{2,1,0:T(8,128)(2,1)}), bf16[16,56,512]{2,1,0:T(8,128)(2,1)S(1)}, u32[]{:S(2)}, u32[]{:S(2)}) async-start(bf16[16,56,512]{2,1,0:T(8,128)(2,1)} %shard_map.79), calls=%async_computation.2 | async-start | bytes 1835008 | tf_op jit(solution)/shard_map/all_to_all | solution.py:263
  37.5 9.4 %collective-permute-start.2 = (bf16[80,512]{1,0:T(8,128)(2,1)S(1)}, bf16[80,512]{1,0:T(8,128)(2,1)S(1)}, u32[]{:S(2)}, u32[]{:S(2)}) collective-permute-start(bf16[80,512]{1,0:T(8,128)(2,1)S(1)} %shard_map.78.own), channel_id=1, source_target_pairs={{0,12},{4,8},{8,4},{12,0},{1,13},{5,9},{9,5},{13,1},{2,14},{6,10},... | collective-permute-start | bytes 245768 | tf_op jit(solution)/shard_map/ppermute | solution.py:247
  41.0 7.8 %collective-permute-start.1 = (bf16[80,512]{1,0:T(8,128)(2,1)S(1)}, bf16[80,512]{1,0:T(8,128)(2,1)S(1)}, u32[]{:S(2)}, u32[]{:S(2)}) collective-permute-start(bf16[80,512]{1,0:T(8,128)(2,1)S(1)} %shard_map.78.own), channel_id=1, source_target_pairs={{0,8},{4,12},{8,0},{12,4},{1,9},{5,13},{9,1},{13,5},{2,10},{6,14},... | collective-permute-start | bytes 245768 | tf_op jit(solution)/shard_map/ppermute | solution.py:247
  43.0 6.7 %collective-permute-start = (bf16[80,512]{1,0:T(8,128)(2,1)S(1)}, bf16[80,512]{1,0:T(8,128)(2,1)S(1)}, u32[]{:S(2)}, u32[]{:S(2)}) collective-permute-start(bf16[80,512]{1,0:T(8,128)(2,1)S(1)} %shard_map.78.own), channel_id=1, source_target_pairs={{0,4},{4,0},{8,12},{12,8},{1,5},{5,1},{9,13},{13,9},{2,6},{6,2},{1... | collective-permute-start | bytes 245768 | tf_op jit(solution)/shard_map/ppermute | solution.py:247
  46.9 19.3 %copy-start = (f32[16]{0:T(128)S(1)}, f32[16]{0:T(128)}, u32[]{:S(2)}) copy-start(f32[16]{0:T(128)} %refs_2_.1) | copy-start | bytes 196
  51.5 23.5 %all-to-all-start.1 = ((bf16[16,80,512]{2,1,0:T(8,128)(2,1)}), bf16[16,80,512]{2,1,0:T(8,128)(2,1)S(1)}, u32[]{:S(2)}, u32[]{:S(2)}) async-start(bf16[16,80,512]{2,1,0:T(8,128)(2,1)} %spread.1), calls=%async_computation.1 | async-start | bytes 2621440 | tf_op jit(solution)/shard_map/all_to_all | solution.py:287
  58.4 7.7 %collective-permute-start.3 = (bf16[16,56,512]{2,1,0:T(8,128)(2,1)S(1)}, bf16[16,56,512]{2,1,0:T(8,128)(2,1)S(1)}, u32[]{:S(2)}, u32[]{:S(2)}) collective-permute-start(bf16[16,56,512]{2,1,0:T(8,128)(2,1)S(1)} %all-to-all-done.2.refs_0_), channel_id=1, source_target_pairs={{0,16},{16,0},{1,17},{17,1},{2,18},{18,2},{3,19},{19,3},{4,20},{20... | collective-permute-start | bytes 2752520 | tf_op jit(solution)/shard_map/ppermute | solution.py:247
  116.7 26.0 %all-to-all-start.5 = ((f32[32,1,128]{2,1,0:T(1,128)}), f32[32,1,128]{2,1,0:T(1,128)S(1)}, u32[]{:S(2)}, u32[]{:S(2)}) async-start(f32[32,1,128]{2,1,0:T(1,128)} %get-tuple-element.11), calls=%async_computation.5 | async-start | bytes 32768 | tf_op jit(solution)/shard_map/all_to_all | solution.py:318
  128.5 3.1 %collective-permute-start.4 = (bf16[20,256]{1,0:T(8,128)(2,1)S(1)}, bf16[20,256]{1,0:T(8,128)(2,1)S(1)}, u32[]{:S(2)}, u32[]{:S(2)}) collective-permute-start(bf16[20,256]{1,0:T(8,128)(2,1)S(1)} %get-tuple-element.10), channel_id=1, source_target_pairs={{0,16},{16,0},{1,17},{17,1},{2,18},{18,2},{3,19},{19,3},{4,20},{20... | collective-permute-start | bytes 30728 | tf_op jit(solution)/shard_map/ppermute | solution.py:247
